TPU v7x, 32 devices: a whole 2x2x4 slice. The times are simulated.
32 devices in a mesh: gx: 8 (over z, core), gy: 4 (over y, x).
Axes of the slice: x: 2, y: 2, z: 4, core: 2. Of those that a mesh axis runs over, the one named last changes fastest.
Arguments:
- coarse: bfloat16 [32, 8, 64, 128], P(None, None, 'gy'), may hold values from -6 to 6
- w_three: bfloat16 [27, 16, 32], replicated, may hold values from -0.5 to 0.5
- w_four: bfloat16 [27, 16], replicated, may hold values from -0.75 to 0.75
- elec_field: bfloat16 [3, 32, 256, 512], P(None, 'gx', 'gy'), may hold values from -6 to 6
- temp_grad: bfloat16 [3, 32, 256, 512], P(None, 'gx', 'gy'), may hold values from -6 to 6
- adjoint: bfloat16 [32, 256, 512], P('gx', 'gy'), may hold values from -6 to 6
- adjoint_grad: bfloat16 [3, 32, 256, 512], P(None, 'gx', 'gy'), may hold values from -6 to 6
Outputs:
- density: float32 [32, 256, 512], P('gx', 'gy')
- grad_three: float32 [27, 16, 32], replicated
- grad_four: float32 [27, 16], replicated
All inputs are finite; a program needn't handle non-finite values.
Results may differ from a plain program's by a relative error of at most 0.0053.
Values may be sent and summed in bfloat16 or wider, within the bound.
No kernel may reach another device: no remote copies, remote signals or barrier semaphores. Data moves between devices by JAX's collectives and lax.ppermute only.
A program may use at most 128 MiB of HBM per device.

v0:
```python
import math

import jax
import jax.numpy as jnp
import numpy as np
from jax import lax
from jax.sharding import PartitionSpec as P

HIGH = lax.Precision.HIGHEST


def passed_along(value, axis, by):
    size = lax.axis_size(axis)
    pairs = [(i, i + by) for i in range(size) if 0 <= i + by < size]
    return lax.ppermute(value, axis, pairs)


def tap_tables():
    onehot = np.zeros((8, 8, 27), np.float32)
    strides = (9, 3, 1)
    for offset in range(8):
        for parity in range(8):
            kernel = 0
            usable = True
            for axis_pos in range(3):
                bit_off = offset >> 2 - axis_pos & 1
                bit_par = parity >> 2 - axis_pos & 1
                if bit_off > bit_par:
                    usable = False
                if bit_par == 0:
                    along = 1
                elif bit_off == 0:
                    along = 2
                else:
                    along = 0
                kernel = kernel + along * strides[axis_pos]
            if usable:
                onehot[offset, parity, kernel] = 1.0
    return onehot


def residue_table():
    per_axis = ({0: 1}, {0: 2, 1: 0}, {1: 1}, {1: 2, 2: 0})
    lookup = np.zeros((64, 27, 27), np.float32)
    for residue in range(64):
        res_x, res_y, res_z = (residue // 16, residue // 4 % 4, residue % 4)
        for src_x, tap_x in per_axis[res_x].items():
            for src_y, tap_y in per_axis[res_y].items():
                for src_z, tap_z in per_axis[res_z].items():
                    lookup[
                        residue, 9 * src_x + 3 * src_y + src_z, 9 * tap_x + 3 * tap_y + tap_z
                    ] = 1.0
    return lookup


def bits_of(offset):
    return (offset >> 2 & 1, offset >> 1 & 1, offset & 1)


def shift_last(block):
    return jnp.concatenate([block[..., 1:], jnp.zeros_like(block[..., :1])], -1)


def delay_last(block):
    return jnp.concatenate([jnp.zeros_like(block[..., :1]), block[..., :-1]], -1)


def beside_y(block, steps_by):
    return passed_along(block, "gy", steps_by)


def silu_slope(values):
    sigma_pre = jax.nn.sigmoid(values)
    return sigma_pre * (1.0 + values * (1.0 - sigma_pre))


def coarse_windows(ext_three, count_a, count_b):
    stacked = []
    for offset in range(8):
        bit_a, bit_b, bit_c = bits_of(offset)
        window = ext_three[:, bit_a : bit_a + count_a, bit_b : bit_b + count_b, :]
        if bit_c == 1:
            window = shift_last(window)
        stacked.append(window)
    merged = jnp.stack(stacked)
    return merged.reshape((merged.shape[0] * merged.shape[1],) + merged.shape[2:])


def layer_three_matrix(weight):
    lookup = jnp.asarray(tap_tables(), jnp.bfloat16)
    spread = jnp.einsum("spk,koc->posc", lookup, weight, preferred_element_type=jnp.float32).astype(
        jnp.bfloat16
    )
    return spread.reshape(8 * weight.shape[1], 8 * weight.shape[2])


def layer_four_matrix(w_four):
    lookup = jnp.asarray(residue_table(), jnp.bfloat16)
    spread = jnp.einsum("usk,ki->usi", lookup, w_four, preferred_element_type=jnp.float32).astype(
        jnp.bfloat16
    )
    return spread.reshape(64, 27 * w_four.shape[1])


def hidden_windows(hidden):
    even_x = hidden[0]
    rim_plane = passed_along(even_x, "gx", -1)
    next_x = jnp.concatenate([even_x[:, :, :, 1:], rim_plane], 3)
    along_x = jnp.stack([even_x, hidden[1], next_x])
    even_y = along_x[:, 0]
    rim_side = beside_y(even_y[:, :, :, :, :1], -1)
    next_y = jnp.concatenate([even_y[:, :, :, :, 1:], rim_side], 4)
    along_y = jnp.stack([even_y, along_x[:, 1], next_y], 1)
    even_z = along_y[:, :, 0]
    along_z = jnp.stack([even_z, along_y[:, :, 1], shift_last(even_z)], 2)
    shape = along_z.shape
    return along_z.reshape((27 * shape[3],) + shape[4:])


def gather_back(spread):
    fold_z = jnp.stack([spread[:, :, 0] + delay_last(spread[:, :, 2]), spread[:, :, 1]], 2)
    later_y = fold_z[:, 2]
    rim_side = passed_along(later_y[:, :, :, :, -1:], "gy", 1)
    moved_y = jnp.concatenate([rim_side, later_y[:, :, :, :, :-1]], 4)
    fold_y = jnp.stack([fold_z[:, 0] + moved_y, fold_z[:, 1]], 1)
    later_x = fold_y[2]
    rim_plane = passed_along(later_x, "gx", 1)
    moved_x = jnp.concatenate([rim_plane, later_x[:, :, :, :-1]], 3)
    fold_x = jnp.stack([fold_y[0] + moved_x, fold_y[1]])
    return fold_x.reshape((8,) + fold_x.shape[3:])


def to_storage(classes, count_a, count_b):
    depth = classes.shape[-1]
    split = classes.reshape(4, 4, 4, count_a, count_b, depth).transpose(3, 0, 4, 1, 2, 5)
    return split.reshape(4 * count_a, 4 * count_b, 4 * depth)


def to_classes(fine, count_a, count_b):
    depth = fine.shape[-1] // 4
    split = fine.reshape(count_a, 4, count_b, 4, 4, depth).transpose(1, 3, 4, 0, 2, 5)
    return split.reshape(64, count_a, count_b, depth)


def first_layer(windows_three, weight):
    matrix_three = layer_three_matrix(weight)
    pre_three = jnp.einsum(
        "qk,kabd->qabd", matrix_three, windows_three, preferred_element_type=jnp.float32
    )
    return pre_three.reshape((8, weight.shape[1]) + pre_three.shape[1:])


def three_gradient(g_pre, windows_three):
    chan_out = g_pre.shape[1]
    flat = g_pre.reshape((8 * chan_out,) + g_pre.shape[2:])
    terms = jnp.einsum("qabd,kabd->qk", flat, windows_three, preferred_element_type=jnp.float32)
    chan_in = windows_three.shape[0] // 8
    terms = terms.reshape(8, chan_out, 8, chan_in)
    lookup = jnp.asarray(tap_tables(), jnp.float32)
    return jnp.einsum("spk,posc->koc", lookup, terms, precision=HIGH)


def shards(coarse, w_three, w_four, elec_field, temp_grad, adjoint, adjoint_grad):
    groups_x = lax.axis_size("gx")
    chan_total, chan_in = (w_three.shape[1], w_three.shape[2])
    fine_x, fine_y, fine_z = adjoint.shape
    count_a, count_b = (fine_x // 4, fine_y // 4)
    cells = fine_x * groups_x * fine_y * lax.axis_size("gy") * fine_z
    rim_row = beside_y(coarse[:, :, :1], -1)
    ext_full = jnp.pad(jnp.concatenate([coarse, rim_row], 2), ((0, 0), (0, 1), (0, 0), (0, 0)))
    ext_brick = lax.dynamic_slice_in_dim(ext_full, lax.axis_index("gx") * count_a, count_a + 1, 1)
    windows_three = coarse_windows(ext_brick, count_a, count_b)
    pre_three = first_layer(windows_three, w_three)
    hidden = jax.nn.silu(pre_three).astype(jnp.bfloat16)
    hidden = hidden.reshape((2, 2, 2) + hidden.shape[1:])
    windows_four = hidden_windows(hidden)
    matrix_four = layer_four_matrix(w_four)
    out_four = jnp.einsum(
        "qk,kabd->qabd", matrix_four, windows_four, preferred_element_type=jnp.float32
    )
    density = to_storage(jax.nn.sigmoid(out_four), count_a, count_b)
    field_e = elec_field.astype(jnp.float32)
    energy = jnp.sum(field_e * field_e, axis=0)
    thermal = jnp.sum(temp_grad.astype(jnp.float32) * adjoint_grad.astype(jnp.float32), axis=0)
    adjoint_f = adjoint.astype(jnp.float32)
    sensitivity = (
        3.0 * (1.0 - 0.001) * density * density * energy * adjoint_f
        - 2.0 * (1.0 - 0.01) * density * thermal
    )
    scale = 8.0 / math.sqrt(cells)
    g_fine = (scale * sensitivity * density * (1.0 - density)).astype(jnp.bfloat16)
    g_classes = to_classes(g_fine, count_a, count_b)
    terms_four = jnp.einsum(
        "qabd,kabd->qk", g_classes, windows_four, preferred_element_type=jnp.float32
    )
    grad_four = jnp.einsum(
        "usk,usi->ki",
        jnp.asarray(residue_table(), jnp.float32),
        terms_four.reshape(64, 27, chan_total),
        precision=HIGH,
    )
    spread_back = jnp.einsum(
        "qk,qabd->kabd", matrix_four, g_classes, preferred_element_type=jnp.float32
    )
    spread_back = spread_back.reshape((3, 3, 3, chan_total) + spread_back.shape[1:])
    hidden_gradient = gather_back(spread_back).astype(jnp.bfloat16)
    g_pre = (hidden_gradient.astype(jnp.float32) * silu_slope(pre_three)).astype(jnp.bfloat16)
    grad_three = three_gradient(g_pre, windows_three)
    grad_three, grad_four = lax.psum((grad_three, grad_four), ("gx", "gy"))
    return (density, grad_three, grad_four)


def solution(mesh):
    return jax.shard_map(
        shards,
        mesh=mesh,
        in_specs=(
            P(None, None, "gy", None),
            P(),
            P(),
            P(None, "gx", "gy", None),
            P(None, "gx", "gy", None),
            P("gx", "gy", None),
            P(None, "gx", "gy", None),
        ),
        out_specs=(P("gx", "gy", None), P(), P()),
        check_vma=False,
    )
```

profile of v0, /device:TPU:0, one launch (start us, length us, event | category | flops | bytes accessed | tf_op | source)
XLA Modules:
  0.0 97.6 jit_solution(15323634922617167889)
XLA Ops:
  0.7 1.2 %slice.103 = bf16[32,8,1,128]{3,2,1,0:T(2,128)(2,1)S(1)} slice(bf16[32,8,16,128]{3,2,1,0:T(8,128)(2,1)} %param.11), slice={[0:32], [0:8], [0:1], [0:128]} | slice | bytes 131072 | tf_op jit(solution)/shard_map/slice | solution.py:169
  1.9 1.3 %collective-permute-start = (bf16[32,8,1,128]{3,2,1,0:T(2,128)(2,1)S(1)}, bf16[32,8,1,128]{3,2,1,0:T(2,128)(2,1)S(1)}, u32[]{:S(2)}, u32[]{:S(2)}) collective-permute-start(bf16[32,8,1,128]{3,2,1,0:T(2,128)(2,1)S(1)} %slice.103), channel_id=1, source_target_pairs={{1,0},{2,1},{3,2},{5,4},{6,5},{7,6},{9,8},{10,9},{11,10},{13,12},{... | collective-permute-start | bytes 196616 | tf_op jit(solution)/shard_map/ppermute | solution.py:15
  3.2 1.1 %fusion.6 = bf16[8,16,8,32]{3,0,1,2:T(8,128)(2,1)S(1)} fusion(bf16[8,8,27,1]{2,1,3,0:T(8,128)(2,1)} %constant.59, bf16[27,16,32]{2,1,0:T(8,128)(2,1)} %param.12), kind=kOutput, calls=%fused_computation.26 | convolution fusion | flops 1802240 | bytes 96640 | tf_op jit(solution)/shard_map/spk,koc->posc/dot_general | solution.py:91
  4.7 5.6 %collective-permute-done = bf16[32,8,1,128]{3,2,1,0:T(2,128)(2,1)S(1)} collective-permute-done((bf16[32,8,1,128]{3,2,1,0:T(2,128)(2,1)S(1)}, bf16[32,8,1,128]{3,2,1,0:T(2,128)(2,1)S(1)}, u32[]{:S(2)}, u32[]{:S(2)}) %collective-permute-start) | collective-permute-done | bytes 65568 | tf_op jit(solution)/shard_map/ppermute | solution.py:15
  12.3 1.4 %collective-permute-start.1 = (bf16[2,2,16,1,16,128]{5,2,4,1,0,3:T(8,128)(2,1)S(1)}, bf16[2,2,16,1,16,128]{5,2,4,1,0,3:T(8,128)(2,1)S(1)}, u32[]{:S(2)}, u32[]{:S(2)}) collective-permute-start(bf16[2,2,16,1,16,128]{5,2,4,1,0,3:T(8,128)(2,1)S(1)} %copy.49), channel_id=1, source_target_pairs={{4,0},{8,4},{12,8},{16,12},{20,16},{24,20},{28,24},{5,1},{9,5},{13... | collective-permute-start | bytes 786440 | tf_op jit(solution)/shard_map/ppermute | solution.py:15
  13.8 1.4 %multiply_reduce_fusion = (f32[4,64,512]{2,1,0:T(8,128)}, f32[4,64,512]{2,1,0:T(8,128)}) fusion(bf16[3,4,64,512]{3,2,1,0:T(8,128)(2,1)S(1)} %copy-done.4, bf16[3,4,64,512]{3,2,1,0:T(8,128)(2,1)S(1)} %copy-done.5, bf16[3,4,64,512]{3,2,1,0:T(8,128)(2,1)S(1)} %copy-done.6), kind=kLoop, calls=%fused_computation.11 | loop fusion | flops 2490368 | bytes 3407872 | tf_op jit(solution)/shard_map/reduce_sum | solution.py:184
  15.1 0.7 collective-permute-done.1
  16.0 1.3 %collective-permute-start.2 = (bf16[3,2,16,1,1,128]{5,2,0,4,1,3:T(8,128)(2,1)S(1)}, bf16[3,2,16,1,1,128]{5,2,0,4,1,3:T(8,128)(2,1)S(1)}, u32[]{:S(2)}, u32[]{:S(2)}) collective-permute-start(bf16[3,2,16,1,1,128]{5,2,0,4,1,3:T(8,128)(2,1)S(1)} %slice.145), channel_id=1, source_target_pairs={{1,0},{2,1},{3,2},{5,4},{6,5},{7,6},{9,8},{10,9},{11,10},{13,12},{... | collective-permute-start | bytes 73736 | tf_op jit(solution)/shard_map/ppermute | solution.py:15
  17.6 4.8 %collective-permute-done.2 = bf16[3,2,16,1,1,128]{5,2,0,4,1,3:T(8,128)(2,1)S(1)} collective-permute-done((bf16[3,2,16,1,1,128]{5,2,0,4,1,3:T(8,128)(2,1)S(1)}, bf16[3,2,16,1,1,128]{5,2,0,4,1,3:T(8,128)(2,1)S(1)}, u32[]{:S(2)}, u32[]{:S(2)}) %collective-permute-start.2) | collective-permute-done | bytes 24608 | tf_op jit(solution)/shard_map/ppermute | solution.py:15
  23.2 0.5 fusion.3
  23.8 1.0 %reshape.154 = f32[4,64,512]{2,1,0:T(8,128)} reshape(f32[1,4,16,4,4,128]{5,4,3,2,1,0:T(4,128)S(1)} %copy.55) | data formatting | bytes 1048576 | tf_op jit(solution)/shard_map/reshape | solution.py:136
  24.8 1.7 %fusion.23 = bf16[4,64,512]{2,1,0:T(8,128)(2,1)S(1)} fusion(f32[4,64,512]{2,1,0:T(8,128)} %reshape.154, f32[4,64,512]{2,1,0:T(8,128)} %get-tuple-element.20, f32[4,64,512]{2,1,0:T(8,128)} %get-tuple-element.19, bf16[4,64,512]{2,1,0:T(8,128)(2,1)} %param.16), kind=kLoop, calls=%fused_computation.52 | loop fusion | flops 1703936 | bytes 2097152 | tf_op jit(solution)/shard_map/convert_element_type | solution.py:191
  26.6 0.6 convolution_bitcast_fusion
  27.9 4.8 %collective-permute-start.3 = (f32[3,2,16,1,1,128]{5,2,4,1,0,3:T(8,128)S(1)}, f32[3,2,16,1,1,128]{5,2,4,1,0,3:T(8,128)S(1)}, u32[]{:S(2)}, u32[]{:S(2)}) collective-permute-start(f32[3,2,16,1,1,128]{5,2,4,1,0,3:T(8,128)S(1)} %slice.157), channel_id=1, source_target_pairs={{0,1},{1,2},{2,3},{4,5},{5,6},{6,7},{8,9},{9,10},{10,11},{12,13},{... | collective-permute-start | bytes 147464 | tf_op jit(solution)/shard_map/ppermute | solution.py:15
  32.8 1.7 %collective-permute-done.3 = f32[3,2,16,1,1,128]{5,2,4,1,0,3:T(8,128)S(1)} collective-permute-done((f32[3,2,16,1,1,128]{5,2,4,1,0,3:T(8,128)S(1)}, f32[3,2,16,1,1,128]{5,2,4,1,0,3:T(8,128)S(1)}, u32[]{:S(2)}, u32[]{:S(2)}) %collective-permute-start.3) | collective-permute-done | bytes 49184 | tf_op jit(solution)/shard_map/ppermute | solution.py:15
  34.7 4.3 %collective-permute-start.4 = (f32[2,2,16,1,16,128]{5,2,4,1,0,3:T(8,128)S(1)}, f32[2,2,16,1,16,128]{5,2,4,1,0,3:T(8,128)S(1)}, u32[]{:S(2)}, u32[]{:S(2)}) collective-permute-start(f32[2,2,16,1,16,128]{5,2,4,1,0,3:T(8,128)S(1)} %slice_bitcast_fusion.3), channel_id=1, source_target_pairs={{0,4},{4,8},{8,12},{12,16},{16,20},{20,24},{24,28},{1,5},{5,9},{9,... | collective-permute-start | bytes 1572872 | tf_op jit(solution)/shard_map/ppermute | solution.py:15
  39.0 0.6 fusion.41
  39.7 0.5 convolution_bitcast_fusion.2
  40.8 0.4 multiply_convert_fusion
  41.2 0.8 copy-done.3
  42.1 1.0 fusion.7
  43.0 0.6 convolution_bitcast_fusion.1
  43.6 53.2 %all-reduce.7 = (f32[27,16,32]{2,0,1:T(8,128)S(1)}, f32[27,16]{0,1:T(8,128)}) all-reduce(f32[27,16,32]{2,0,1:T(8,128)S(1)} %convolution_bitcast_fusion.1, f32[27,16]{0,1:T(8,128)S(1)} %convolution_bitcast_fusion.2), channel_id=1, replica_groups=mesh['gx'=8,'gy'=4] {'gx','gy'}, use_global_device_ids=true, to_apply=%region_2.3 | all-reduce | flops 14256 | bytes 114048 | tf_op jit(solution)/shard_map/psum | solution.py:209
  96.8 0.8 copy.64
  (64 shorter events, 5.3 us)
Async XLA Ops:
  0.6 16.7 %copy-start = (bf16[27,16]{0,1:T(8,128)(2,1)S(1)}, bf16[27,16]{0,1:T(8,128)(2,1)}, u32[]{:S(2)}) copy-start(bf16[27,16]{0,1:T(8,128)(2,1)} %param.13) | copy-start | bytes 2596
  0.6 9.6 %copy-start.1 = (bf16[32,8,16,128]{3,2,1,0:T(8,128)(2,1)S(1)}, bf16[32,8,16,128]{3,2,1,0:T(8,128)(2,1)}, u32[]{:S(2)}) copy-start(bf16[32,8,16,128]{3,2,1,0:T(8,128)(2,1)} %param.11) | copy-start | bytes 3145732
  1.9 8.4 %collective-permute-start = (bf16[32,8,1,128]{3,2,1,0:T(2,128)(2,1)S(1)}, bf16[32,8,1,128]{3,2,1,0:T(2,128)(2,1)S(1)}, u32[]{:S(2)}, u32[]{:S(2)}) collective-permute-start(bf16[32,8,1,128]{3,2,1,0:T(2,128)(2,1)S(1)} %slice.103), channel_id=1, source_target_pairs={{1,0},{2,1},{3,2},{5,4},{6,5},{7,6},{9,8},{10,9},{11,10},{13,12},{... | collective-permute-start | bytes 196616 | tf_op jit(solution)/shard_map/ppermute | solution.py:15
  11.0 1.0 copy-start.2
  11.9 1.8 %copy-start.4 = (bf16[3,4,64,512]{3,2,1,0:T(8,128)(2,1)S(1)}, bf16[3,4,64,512]{3,2,1,0:T(8,128)(2,1)}, u32[]{:S(2)}) copy-start(bf16[3,4,64,512]{3,2,1,0:T(8,128)(2,1)} %param.17) | copy-start | bytes 2359300
  11.9 1.8 %copy-start.5 = (bf16[3,4,64,512]{3,2,1,0:T(8,128)(2,1)S(1)}, bf16[3,4,64,512]{3,2,1,0:T(8,128)(2,1)}, u32[]{:S(2)}) copy-start(bf16[3,4,64,512]{3,2,1,0:T(8,128)(2,1)} %param.15) | copy-start | bytes 2359300
  11.9 1.8 %copy-start.6 = (bf16[3,4,64,512]{3,2,1,0:T(8,128)(2,1)S(1)}, bf16[3,4,64,512]{3,2,1,0:T(8,128)(2,1)}, u32[]{:S(2)}) copy-start(bf16[3,4,64,512]{3,2,1,0:T(8,128)(2,1)} %param.14) | copy-start | bytes 2359300
  12.3 3.6 %collective-permute-start.1 = (bf16[2,2,16,1,16,128]{5,2,4,1,0,3:T(8,128)(2,1)S(1)}, bf16[2,2,16,1,16,128]{5,2,4,1,0,3:T(8,128)(2,1)S(1)}, u32[]{:S(2)}, u32[]{:S(2)}) collective-permute-start(bf16[2,2,16,1,16,128]{5,2,4,1,0,3:T(8,128)(2,1)S(1)} %copy.49), channel_id=1, source_target_pairs={{4,0},{8,4},{12,8},{16,12},{20,16},{24,20},{28,24},{5,1},{9,5},{13... | collective-permute-start | bytes 786440 | tf_op jit(solution)/shard_map/ppermute | solution.py:15
  15.1 2.2 %copy-start.8 = (bf16[64,27,27]{0,2,1:T(8,128)(2,1)S(1)}, bf16[64,27,27]{0,2,1:T(8,128)(2,1)}, u32[]{:S(2)}) copy-start(bf16[64,27,27]{0,2,1:T(8,128)(2,1)} %constant.38.clone) | copy-start | bytes 279940
  16.0 6.3 %collective-permute-start.2 = (bf16[3,2,16,1,1,128]{5,2,0,4,1,3:T(8,128)(2,1)S(1)}, bf16[3,2,16,1,1,128]{5,2,0,4,1,3:T(8,128)(2,1)S(1)}, u32[]{:S(2)}, u32[]{:S(2)}) collective-permute-start(bf16[3,2,16,1,1,128]{5,2,0,4,1,3:T(8,128)(2,1)S(1)} %slice.145), channel_id=1, source_target_pairs={{1,0},{2,1},{3,2},{5,4},{6,5},{7,6},{9,8},{10,9},{11,10},{13,12},{... | collective-permute-start | bytes 73736 | tf_op jit(solution)/shard_map/ppermute | solution.py:15
  27.9 6.6 %collective-permute-start.3 = (f32[3,2,16,1,1,128]{5,2,4,1,0,3:T(8,128)S(1)}, f32[3,2,16,1,1,128]{5,2,4,1,0,3:T(8,128)S(1)}, u32[]{:S(2)}, u32[]{:S(2)}) collective-permute-start(f32[3,2,16,1,1,128]{5,2,4,1,0,3:T(8,128)S(1)} %slice.157), channel_id=1, source_target_pairs={{0,1},{1,2},{2,3},{4,5},{5,6},{6,7},{8,9},{9,10},{10,11},{12,13},{... | collective-permute-start | bytes 147464 | tf_op jit(solution)/shard_map/ppermute | solution.py:15
  34.7 5.0 %copy-start.7 = (f32[64,27,27]{0,2,1:T(8,128)S(1)}, f32[64,27,27]{0,2,1:T(8,128)}, u32[]{:S(2)}) copy-start(f32[64,27,27]{0,2,1:T(8,128)} %constant.39.clone) | copy-start | bytes 559876
  34.7 5.8 %collective-permute-start.4 = (f32[2,2,16,1,16,128]{5,2,4,1,0,3:T(8,128)S(1)}, f32[2,2,16,1,16,128]{5,2,4,1,0,3:T(8,128)S(1)}, u32[]{:S(2)}, u32[]{:S(2)}) collective-permute-start(f32[2,2,16,1,16,128]{5,2,4,1,0,3:T(8,128)S(1)} %slice_bitcast_fusion.3), channel_id=1, source_target_pairs={{0,4},{4,8},{8,12},{12,16},{16,20},{20,24},{24,28},{1,5},{5,9},{9,... | collective-permute-start | bytes 1572872 | tf_op jit(solution)/shard_map/ppermute | solution.py:15
  40.8 1.2 %copy-start.3 = (bf16[8,32,1,16,128]{4,3,1,2,0:T(8,128)(2,1)S(1)}, bf16[8,32,1,16,128]{4,3,1,2,0:T(8,128)(2,1)}, u32[]{:S(2)}) copy-start(bf16[8,32,1,16,128]{4,3,1,2,0:T(8,128)(2,1)} %copy-done.2) | copy-start | bytes 3145732
  42.1 1.0 copy-start.9
where the time goes:
time: 98 us; the launch traced here: 97.6 us
  blocking collectives  53.2 us (54%)
  starting transfers between devices  13.1 us (13%)
  waiting for transfers between devices  12.9 us (13%)
  local copies, waits for them, and re-layouts  6.6 us (7%)
  other arithmetic  5.36 us (5%)
  matrix products  5.33 us (5%)
  between operations  1.08 us (1%)
    psum x1, blocking collectives, shards(): grad_three, grad_four = lax.psum((grad_three, grad_four), ('gx', 'gy'))  53.2 us
    ppermute x5, starting transfers between devices, passed_along(): return lax.ppermute(value, axis, pairs)  13.1 us
    ppermute x5, waiting for transfers between devices, passed_along(): return lax.ppermute(value, axis, pairs)  12.9 us
    unnamed x28, local copies, waits for them, and re-layouts  2.32 us
  transfers between devices with their start and end apart: 5, of which 5 were waited for; matrix products, arithmetic and copies ran while one was open for 5% of the time, Pallas kernels for 0%

commit v1 on v0

--- a/solution.py
+++ b/solution.py
@@ -160,6 +160,51 @@
     return jnp.einsum("spk,posc->koc", lookup, terms, precision=HIGH)
 
 
+def exchanged(value, axis, bit):
+    size = lax.axis_size(axis)
+    return lax.ppermute(value, axis, [(i, i ^ bit) for i in range(size)])
+
+
+def doubling_bits(size, first):
+    bits = []
+    bit = first
+    while bit < size:
+        bits.append(bit)
+        bit = bit * 2
+    return bits
+
+
+def sum_halves(half):
+    for bit in doubling_bits(lax.axis_size("gx"), 2):
+        half = half + exchanged(half, "gx", bit)
+    for bit in doubling_bits(lax.axis_size("gy"), 1):
+        half = half + exchanged(half, "gy", bit)
+    return half
+
+
+def sum_everywhere(grad_three, grad_four):
+    for axis in ("gx", "gy"):
+        size = lax.axis_size(axis)
+        assert size & (size - 1) == 0
+    flat = jnp.concatenate([grad_three.reshape(-1), grad_four.reshape(-1)])
+    held = flat.shape[0]
+    rows = -(-held // 2048) * 16
+    packed = jnp.pad(flat, (0, rows * 128 - held)).reshape(2, rows // 2, 128)
+    core = lax.axis_index("gx") % 2
+    mine = jnp.where(core == 0, packed[0], packed[1])
+    other = jnp.where(core == 0, packed[1], packed[0])
+    mine = sum_halves(mine + exchanged(other, "gx", 1))
+    other = exchanged(mine, "gx", 1)
+    first = jnp.where(core == 0, mine, other)
+    second = jnp.where(core == 0, other, mine)
+    summed = jnp.concatenate([first, second]).reshape(-1)
+    count_three = grad_three.size
+    return (
+        summed[:count_three].reshape(grad_three.shape),
+        summed[count_three:held].reshape(grad_four.shape),
+    )
+
+
 def shards(coarse, w_three, w_four, elec_field, temp_grad, adjoint, adjoint_grad):
     groups_x = lax.axis_size("gx")
     chan_total, chan_in = (w_three.shape[1], w_three.shape[2])
@@ -206,7 +251,7 @@
     hidden_gradient = gather_back(spread_back).astype(jnp.bfloat16)
     g_pre = (hidden_gradient.astype(jnp.float32) * silu_slope(pre_three)).astype(jnp.bfloat16)
     grad_three = three_gradient(g_pre, windows_three)
-    grad_three, grad_four = lax.psum((grad_three, grad_four), ("gx", "gy"))
+    grad_three, grad_four = sum_everywhere(grad_three, grad_four)
     return (density, grad_three, grad_four)
 
 

time: 98 us -> 77.8 us (0.79)
  blocking collectives: 53.2 us -> 0 us
  starting transfers between devices: 13.1 us -> 28.8 us
  waiting for transfers between devices: 12.9 us -> 22.5 us
  local copies, waits for them, and re-layouts: 6.6 us -> 11.7 us
  other arithmetic: 5.36 us -> 7.84 us
    psum x1 -> x0, blocking collectives: 53.2 us -> none  [shards(): grad_three, grad_four = lax.psum((grad_three, grad_four), ('gx', 'gy'))]
    ppermute x0 -> x6, starting transfers between devices: none -> 15.1 us  [exchanged(): return lax.ppermute(value, axis, [(i, i ^ bit) for i in range(size)])]
    ppermute x0 -> x6, waiting for transfers between devices: none -> 9.75 us  [exchanged(): return lax.ppermute(value, axis, [(i, i ^ bit) for i in range(size)])]
    unnamed x28 -> x40, local copies, waits for them, and re-layouts: 2.32 us -> 5.28 us
    another operation x2, other arithmetic: 0.26 us -> 1.48 us  [gather_back(): fold_y = jnp.stack([fold_z[:, 0] + moved_y, fold_z[:, 1]], 1)]
    another operation x1, other arithmetic: 0.07 us -> 1.27 us  [gather_back(): fold_x = jnp.stack([fold_y[0] + moved_x, fold_y[1]])]
    reshape x0 -> x3, local copies, waits for them, and re-layouts: none -> 0.98 us  [the longest x1 0.8 us: sum_everywhere(): summed[:count_three].reshape(grad_three.shape)]
  transfers between devices with their start and end apart: 5 -> 11, of which waited for: 5 -> 10; matrix products, arithmetic and copies ran while one was open for 5% -> 7% of each run, Pallas kernels for 0% -> 0%
where the time goes in v1:
time: 77.8 us; the launch traced here: 77.4 us
  starting transfers between devices  28.8 us (37%)
  waiting for transfers between devices  22.5 us (29%)
  local copies, waits for them, and re-layouts  11.7 us (15%)
  other arithmetic  7.84 us (10%)
  matrix products  5.31 us (7%)
  between operations  1.19 us (2%)
    ppermute x6, starting transfers between devices, exchanged(): return lax.ppermute(value, axis, [(i, i ^ bit) for i in range(size)])  15.1 us
    ppermute x5, starting transfers between devices, passed_along(): return lax.ppermute(value, axis, pairs)  13.7 us
    ppermute x5, waiting for transfers between devices, passed_along(): return lax.ppermute(value, axis, pairs)  12.8 us
    ppermute x6, waiting for transfers between devices, exchanged(): return lax.ppermute(value, axis, [(i, i ^ bit) for i in range(size)])  9.75 us
    unnamed x40, local copies, waits for them, and re-layouts  5.28 us
    convert_element_type x1, other arithmetic, shards(): (scale * sensitivity * density * (1.0 - density)).astype(jnp.bfloat16)  1.65 us
  transfers between devices with their start and end apart: 11, of which 10 were waited for; matrix products, arithmetic and copies ran while one was open for 7% of the time, Pallas kernels for 0%

profile of v1, /device:TPU:0, one launch (start us, length us, event | category | flops | bytes accessed | tf_op | source)
XLA Modules:
  0.0 77.4 jit_solution(13581667235302163316)
XLA Ops:
  0.7 1.2 %slice.136 = bf16[32,8,1,128]{3,2,1,0:T(2,128)(2,1)S(1)} slice(bf16[32,8,16,128]{3,2,1,0:T(8,128)(2,1)} %param.11), slice={[0:32], [0:8], [0:1], [0:128]} | slice | bytes 131072 | tf_op jit(solution)/shard_map/slice | solution.py:214
  1.9 1.3 %collective-permute-start = (bf16[32,8,1,128]{3,2,1,0:T(2,128)(2,1)S(1)}, bf16[32,8,1,128]{3,2,1,0:T(2,128)(2,1)S(1)}, u32[]{:S(2)}, u32[]{:S(2)}) collective-permute-start(bf16[32,8,1,128]{3,2,1,0:T(2,128)(2,1)S(1)} %slice.136), channel_id=1, source_target_pairs={{1,0},{2,1},{3,2},{5,4},{6,5},{7,6},{9,8},{10,9},{11,10},{13,12},{... | collective-permute-start | bytes 196616 | tf_op jit(solution)/shard_map/ppermute | solution.py:15
  3.2 1.1 %fusion.6 = bf16[8,16,8,32]{3,0,1,2:T(8,128)(2,1)S(1)} fusion(bf16[8,8,27,1]{2,1,3,0:T(8,128)(2,1)} %constant.74, bf16[27,16,32]{2,1,0:T(8,128)(2,1)} %param.12), kind=kOutput, calls=%fused_computation.26 | convolution fusion | flops 1802240 | bytes 96640 | tf_op jit(solution)/shard_map/spk,koc->posc/dot_general | solution.py:91
  4.7 5.6 %collective-permute-done = bf16[32,8,1,128]{3,2,1,0:T(2,128)(2,1)S(1)} collective-permute-done((bf16[32,8,1,128]{3,2,1,0:T(2,128)(2,1)S(1)}, bf16[32,8,1,128]{3,2,1,0:T(2,128)(2,1)S(1)}, u32[]{:S(2)}, u32[]{:S(2)}) %collective-permute-start) | collective-permute-done | bytes 65568 | tf_op jit(solution)/shard_map/ppermute | solution.py:15
  12.3 1.4 %collective-permute-start.1 = (bf16[2,2,16,1,16,128]{5,2,4,1,0,3:T(8,128)(2,1)S(1)}, bf16[2,2,16,1,16,128]{5,2,4,1,0,3:T(8,128)(2,1)S(1)}, u32[]{:S(2)}, u32[]{:S(2)}) collective-permute-start(bf16[2,2,16,1,16,128]{5,2,4,1,0,3:T(8,128)(2,1)S(1)} %copy.48), channel_id=1, source_target_pairs={{4,0},{8,4},{12,8},{16,12},{20,16},{24,20},{28,24},{5,1},{9,5},{13... | collective-permute-start | bytes 786440 | tf_op jit(solution)/shard_map/ppermute | solution.py:15
  13.8 1.4 %multiply_reduce_fusion = (f32[4,64,512]{2,1,0:T(8,128)}, f32[4,64,512]{2,1,0:T(8,128)}) fusion(bf16[3,4,64,512]{3,2,1,0:T(8,128)(2,1)S(1)} %copy-done.10, bf16[3,4,64,512]{3,2,1,0:T(8,128)(2,1)S(1)} %copy-done.11, bf16[3,4,64,512]{3,2,1,0:T(8,128)(2,1)S(1)} %copy-done.12), kind=kLoop, calls=%fused_computation.11 | loop fusion | flops 2490368 | bytes 3407872 | tf_op jit(solution)/shard_map/reduce_sum | solution.py:229
  16.9 1.3 %collective-permute-start.2 = (bf16[3,2,16,1,1,128]{5,2,0,4,1,3:T(8,128)(2,1)S(1)}, bf16[3,2,16,1,1,128]{5,2,0,4,1,3:T(8,128)(2,1)S(1)}, u32[]{:S(2)}, u32[]{:S(2)}) collective-permute-start(bf16[3,2,16,1,1,128]{5,2,0,4,1,3:T(8,128)(2,1)S(1)} %slice.184), channel_id=1, source_target_pairs={{1,0},{2,1},{3,2},{5,4},{6,5},{7,6},{9,8},{10,9},{11,10},{13,12},{... | collective-permute-start | bytes 73736 | tf_op jit(solution)/shard_map/ppermute | solution.py:15
  18.5 4.8 %collective-permute-done.2 = bf16[3,2,16,1,1,128]{5,2,0,4,1,3:T(8,128)(2,1)S(1)} collective-permute-done((bf16[3,2,16,1,1,128]{5,2,0,4,1,3:T(8,128)(2,1)S(1)}, bf16[3,2,16,1,1,128]{5,2,0,4,1,3:T(8,128)(2,1)S(1)}, u32[]{:S(2)}, u32[]{:S(2)}) %collective-permute-start.2) | collective-permute-done | bytes 24608 | tf_op jit(solution)/shard_map/ppermute | solution.py:15
  27.1 1.7 %fusion.23 = bf16[4,64,512]{2,1,0:T(8,128)(2,1)S(1)} fusion(f32[4,64,512]{2,1,0:T(8,128)} %reshape.184, f32[4,64,512]{2,1,0:T(8,128)} %get-tuple-element.17, f32[4,64,512]{2,1,0:T(8,128)} %get-tuple-element.16, bf16[4,64,512]{2,1,0:T(8,128)(2,1)} %param.16), kind=kLoop, calls=%fused_computation.52 | loop fusion | flops 1703936 | bytes 2097152 | tf_op jit(solution)/shard_map/convert_element_type | solution.py:236
  30.2 4.8 %collective-permute-start.3 = (f32[3,2,16,1,1,128]{5,2,4,1,0,3:T(8,128)S(1)}, f32[3,2,16,1,1,128]{5,2,4,1,0,3:T(8,128)S(1)}, u32[]{:S(2)}, u32[]{:S(2)}) collective-permute-start(f32[3,2,16,1,1,128]{5,2,4,1,0,3:T(8,128)S(1)} %slice.196), channel_id=1, source_target_pairs={{0,1},{1,2},{2,3},{4,5},{5,6},{6,7},{8,9},{9,10},{10,11},{12,13},{... | collective-permute-start | bytes 147464 | tf_op jit(solution)/shard_map/ppermute | solution.py:15
  35.1 1.7 %collective-permute-done.3 = f32[3,2,16,1,1,128]{5,2,4,1,0,3:T(8,128)S(1)} collective-permute-done((f32[3,2,16,1,1,128]{5,2,4,1,0,3:T(8,128)S(1)}, f32[3,2,16,1,1,128]{5,2,4,1,0,3:T(8,128)S(1)}, u32[]{:S(2)}, u32[]{:S(2)}) %collective-permute-start.3) | collective-permute-done | bytes 49184 | tf_op jit(solution)/shard_map/ppermute | solution.py:15
  38.6 4.9 %collective-permute-start.4 = (f32[2,2,16,1,16,128]{5,2,4,1,0,3:T(8,128)}, f32[2,2,16,1,16,128]{5,2,4,1,0,3:T(8,128)}, u32[]{:S(2)}, u32[]{:S(2)}) collective-permute-start(f32[2,2,16,1,16,128]{5,2,4,1,0,3:T(8,128)} %slice_bitcast_fusion.3), channel_id=1, source_target_pairs={{0,4},{4,8},{8,12},{12,16},{16,20},{20,24},{24,28},{1,5},{5,9},{9,... | collective-permute-start | bytes 1572872 | tf_op jit(solution)/shard_map/ppermute | solution.py:15
  44.7 1.3 %fusion = f32[3,2,2,16,1,16,128]{6,3,5,2,1,0,4:T(8,128)S(1)} fusion(f32[3,3,1,16,1,16,128]{6,3,5,2,1,0,4:T(8,128)S(1)} %get-tuple-element.7, f32[3,3,1,16,1,16,128]{6,3,5,2,1,0,4:T(8,128)S(1)} %fusion.5, f32[3,1,2,16,1,16,128]{6,3,5,2,1,0,4:T(8,128)} %copy-done.3), kind=kLoop, calls=%fused_computation.9 | loop fusion | flops 1966080 | bytes 4718592 | tf_op jit(solution)/shard_map/stack | solution.py:125
  46.1 1.3 %fusion.30 = bf16[1,2,2,16,1,16,128]{6,3,5,2,1,0,4:T(8,128)(2,1)S(1)} fusion(f32[2,2,16,1,16,128]{5,2,4,1,0,3:T(8,128)} %collective-permute-done.4, f32[3,2,2,16,1,16,128]{6,3,5,2,1,4,0:T(8,128)} %copy-done.6), kind=kLoop, calls=%fused_computation.65 | loop fusion | flops 262144 | bytes 1310720 | tf_op jit(solution)/shard_map/stack | solution.py:129
  50.8 5.0 %collective-permute-start.5 = (f32[56,128]{1,0:T(8,128)S(1)}, f32[56,128]{1,0:T(8,128)S(1)}, u32[]{:S(2)}, u32[]{:S(2)}) collective-permute-start(f32[56,128]{1,0:T(8,128)S(1)} %broadcast_select_fusion.2), channel_id=1, source_target_pairs={{0,4},{4,0},{8,12},{12,8},{16,20},{20,16},{24,28},{28,24},{1,5},{5... | collective-permute-start | bytes 86024 | tf_op jit(solution)/shard_map/ppermute | solution.py:165
  56.7 2.8 %collective-permute-start.6 = (f32[56,128]{1,0:T(8,128)S(1)}, f32[56,128]{1,0:T(8,128)S(1)}, u32[]{:S(2)}, u32[]{:S(2)}) collective-permute-start(f32[56,128]{1,0:T(8,128)S(1)} %select_add_fusion), channel_id=1, source_target_pairs={{0,8},{4,12},{8,0},{12,4},{16,24},{20,28},{24,16},{28,20},{1,9},{5... | collective-permute-start | bytes 86024 | tf_op jit(solution)/shard_map/ppermute | solution.py:165
  59.5 1.9 %collective-permute-done.6 = f32[56,128]{1,0:T(8,128)S(1)} collective-permute-done((f32[56,128]{1,0:T(8,128)S(1)}, f32[56,128]{1,0:T(8,128)S(1)}, u32[]{:S(2)}, u32[]{:S(2)}) %collective-permute-start.6) | collective-permute-done | bytes 28704 | tf_op jit(solution)/shard_map/ppermute | solution.py:165
  61.4 3.0 %collective-permute-start.7 = (f32[56,128]{1,0:T(8,128)S(1)}, f32[56,128]{1,0:T(8,128)S(1)}, u32[]{:S(2)}, u32[]{:S(2)}) collective-permute-start(f32[56,128]{1,0:T(8,128)S(1)} %add.89), channel_id=1, source_target_pairs={{0,16},{4,20},{8,24},{12,28},{16,0},{20,4},{24,8},{28,12},{1,17},{... | collective-permute-start | bytes 86024 | tf_op jit(solution)/shard_map/ppermute | solution.py:165
  64.4 1.8 %collective-permute-done.7 = f32[56,128]{1,0:T(8,128)S(1)} collective-permute-done((f32[56,128]{1,0:T(8,128)S(1)}, f32[56,128]{1,0:T(8,128)S(1)}, u32[]{:S(2)}, u32[]{:S(2)}) %collective-permute-start.7) | collective-permute-done | bytes 28704 | tf_op jit(solution)/shard_map/ppermute | solution.py:165
  66.3 2.5 %collective-permute-start.8 = (f32[56,128]{1,0:T(8,128)S(1)}, f32[56,128]{1,0:T(8,128)S(1)}, u32[]{:S(2)}, u32[]{:S(2)}) collective-permute-start(f32[56,128]{1,0:T(8,128)S(1)} %add.90), channel_id=1, source_target_pairs={{0,1},{1,0},{2,3},{3,2},{4,5},{5,4},{6,7},{7,6},{8,9},{9,8},{10,11... | collective-permute-start | bytes 86024 | tf_op jit(solution)/shard_map/ppermute | solution.py:165
  68.7 1.8 %collective-permute-done.8 = f32[56,128]{1,0:T(8,128)S(1)} collective-permute-done((f32[56,128]{1,0:T(8,128)S(1)}, f32[56,128]{1,0:T(8,128)S(1)}, u32[]{:S(2)}, u32[]{:S(2)}) %collective-permute-start.8) | collective-permute-done | bytes 28704 | tf_op jit(solution)/shard_map/ppermute | solution.py:165
  70.6 1.7 %collective-permute-start.9 = (f32[56,128]{1,0:T(8,128)S(1)}, f32[56,128]{1,0:T(8,128)S(1)}, u32[]{:S(2)}, u32[]{:S(2)}) collective-permute-start(f32[56,128]{1,0:T(8,128)S(1)} %add.91), channel_id=1, source_target_pairs={{0,2},{1,3},{2,0},{3,1},{4,6},{5,7},{6,4},{7,5},{8,10},{9,11},{10,... | collective-permute-start | bytes 86024 | tf_op jit(solution)/shard_map/ppermute | solution.py:165
  72.3 2.2 %collective-permute-done.9 = f32[56,128]{1,0:T(8,128)S(1)} collective-permute-done((f32[56,128]{1,0:T(8,128)S(1)}, f32[56,128]{1,0:T(8,128)S(1)}, u32[]{:S(2)}, u32[]{:S(2)}) %collective-permute-start.9) | collective-permute-done | bytes 28704 | tf_op jit(solution)/shard_map/ppermute | solution.py:165
  74.5 1.2 %collective-permute-done.10 = f32[56,128]{1,0:T(8,128)S(1)} collective-permute-done((f32[56,128]{1,0:T(8,128)S(1)}, f32[56,128]{1,0:T(8,128)S(1)}, u32[]{:S(2)}, u32[]{:S(2)}) %collective-permute-start.10) | collective-permute-done | bytes 28704 | tf_op jit(solution)/shard_map/ppermute | solution.py:165
  (105 shorter events, 18.5 us)
Async XLA Ops:
  0.6 17.6 %copy-start = (bf16[27,16]{0,1:T(8,128)(2,1)S(1)}, bf16[27,16]{0,1:T(8,128)(2,1)}, u32[]{:S(2)}) copy-start(bf16[27,16]{0,1:T(8,128)(2,1)} %param.13) | copy-start | bytes 2596
  0.6 9.6 %copy-start.7 = (bf16[32,8,16,128]{3,2,1,0:T(8,128)(2,1)S(1)}, bf16[32,8,16,128]{3,2,1,0:T(8,128)(2,1)}, u32[]{:S(2)}) copy-start(bf16[32,8,16,128]{3,2,1,0:T(8,128)(2,1)} %param.11) | copy-start | bytes 3145732
  1.9 8.4 %collective-permute-start = (bf16[32,8,1,128]{3,2,1,0:T(2,128)(2,1)S(1)}, bf16[32,8,1,128]{3,2,1,0:T(2,128)(2,1)S(1)}, u32[]{:S(2)}, u32[]{:S(2)}) collective-permute-start(bf16[32,8,1,128]{3,2,1,0:T(2,128)(2,1)S(1)} %slice.136), channel_id=1, source_target_pairs={{1,0},{2,1},{3,2},{5,4},{6,5},{7,6},{9,8},{10,9},{11,10},{13,12},{... | collective-permute-start | bytes 196616 | tf_op jit(solution)/shard_map/ppermute | solution.py:15
  11.0 1.0 %copy-start.8 = (bf16[8,32,1,16,128]{4,3,1,2,0:T(8,128)(2,1)}, bf16[8,32,1,16,128]{4,3,1,2,0:T(8,128)(2,1)S(1)}, u32[]{:S(2)}) copy-start(bf16[8,32,1,16,128]{4,3,1,2,0:T(8,128)(2,1)S(1)} %bitcast_dynamic-update-slice_fusion) | copy-start | bytes 3145732
  11.9 1.8 %copy-start.10 = (bf16[3,4,64,512]{3,2,1,0:T(8,128)(2,1)S(1)}, bf16[3,4,64,512]{3,2,1,0:T(8,128)(2,1)}, u32[]{:S(2)}) copy-start(bf16[3,4,64,512]{3,2,1,0:T(8,128)(2,1)} %param.17) | copy-start | bytes 2359300
  11.9 1.8 %copy-start.11 = (bf16[3,4,64,512]{3,2,1,0:T(8,128)(2,1)S(1)}, bf16[3,4,64,512]{3,2,1,0:T(8,128)(2,1)}, u32[]{:S(2)}) copy-start(bf16[3,4,64,512]{3,2,1,0:T(8,128)(2,1)} %param.15) | copy-start | bytes 2359300
  11.9 1.8 %copy-start.12 = (bf16[3,4,64,512]{3,2,1,0:T(8,128)(2,1)S(1)}, bf16[3,4,64,512]{3,2,1,0:T(8,128)(2,1)}, u32[]{:S(2)}) copy-start(bf16[3,4,64,512]{3,2,1,0:T(8,128)(2,1)} %param.14) | copy-start | bytes 2359300
  12.3 3.6 %collective-permute-start.1 = (bf16[2,2,16,1,16,128]{5,2,4,1,0,3:T(8,128)(2,1)S(1)}, bf16[2,2,16,1,16,128]{5,2,4,1,0,3:T(8,128)(2,1)S(1)}, u32[]{:S(2)}, u32[]{:S(2)}) collective-permute-start(bf16[2,2,16,1,16,128]{5,2,4,1,0,3:T(8,128)(2,1)S(1)} %copy.48), channel_id=1, source_target_pairs={{4,0},{8,4},{12,8},{16,12},{20,16},{24,20},{28,24},{5,1},{9,5},{13... | collective-permute-start | bytes 786440 | tf_op jit(solution)/shard_map/ppermute | solution.py:15
  15.1 3.1 %copy-start.14 = (bf16[64,27,27]{0,2,1:T(8,128)(2,1)S(1)}, bf16[64,27,27]{0,2,1:T(8,128)(2,1)}, u32[]{:S(2)}) copy-start(bf16[64,27,27]{0,2,1:T(8,128)(2,1)} %constant.51.clone) | copy-start | bytes 279940
  16.9 6.3 %collective-permute-start.2 = (bf16[3,2,16,1,1,128]{5,2,0,4,1,3:T(8,128)(2,1)S(1)}, bf16[3,2,16,1,1,128]{5,2,0,4,1,3:T(8,128)(2,1)S(1)}, u32[]{:S(2)}, u32[]{:S(2)}) collective-permute-start(bf16[3,2,16,1,1,128]{5,2,0,4,1,3:T(8,128)(2,1)S(1)} %slice.184), channel_id=1, source_target_pairs={{1,0},{2,1},{3,2},{5,4},{6,5},{7,6},{9,8},{10,9},{11,10},{13,12},{... | collective-permute-start | bytes 73736 | tf_op jit(solution)/shard_map/ppermute | solution.py:15
  23.4 1.1 %copy-start.5 = (bf16[3,2,2,16,1,16,128]{6,3,0,5,2,4,1:T(8,128)(2,1)S(1)}, bf16[3,2,2,16,1,16,128]{6,3,0,5,2,4,1:T(8,128)(2,1)}, u32[]{:S(2)}) copy-start(bf16[3,2,2,16,1,16,128]{6,3,0,5,2,4,1:T(8,128)(2,1)} %copy-done.4) | copy-start | bytes 2359300
  24.9 1.3 %copy-start.1 = (bf16[3,3,3,16,1,16,128]{6,3,2,1,0,5,4:T(8,128)(2,1)}, bf16[3,3,3,16,1,16,128]{6,3,2,1,0,5,4:T(8,128)(2,1)S(1)}, u32[]{:S(2)}) copy-start(bf16[3,3,3,16,1,16,128]{6,3,2,1,0,5,4:T(8,128)(2,1)S(1)} %pad_maximum_fusion) | copy-start | bytes 5308420
  30.2 6.6 %collective-permute-start.3 = (f32[3,2,16,1,1,128]{5,2,4,1,0,3:T(8,128)S(1)}, f32[3,2,16,1,1,128]{5,2,4,1,0,3:T(8,128)S(1)}, u32[]{:S(2)}, u32[]{:S(2)}) collective-permute-start(f32[3,2,16,1,1,128]{5,2,4,1,0,3:T(8,128)S(1)} %slice.196), channel_id=1, source_target_pairs={{0,1},{1,2},{2,3},{4,5},{5,6},{6,7},{8,9},{9,10},{10,11},{12,13},{... | collective-permute-start | bytes 147464 | tf_op jit(solution)/shard_map/ppermute | solution.py:15
  36.9 6.7 %copy-start.2 = (bf16[3,3,3,16,1,16,128]{6,3,2,1,0,5,4:T(8,128)(2,1)S(1)}, bf16[3,3,3,16,1,16,128]{6,3,2,1,0,5,4:T(8,128)(2,1)}, u32[]{:S(2)}) copy-start(bf16[3,3,3,16,1,16,128]{6,3,2,1,0,5,4:T(8,128)(2,1)} %copy-done.1) | copy-start | bytes 5308420
  37.8 6.4 %copy-start.6 = (f32[3,2,2,16,1,16,128]{6,3,5,2,1,4,0:T(8,128)}, f32[3,2,2,16,1,16,128]{6,3,5,2,1,4,0:T(8,128)S(1)}, u32[]{:S(2)}) copy-start(f32[3,2,2,16,1,16,128]{6,3,5,2,1,4,0:T(8,128)S(1)} %fusion.58) | copy-start | bytes 4718596
  37.8 6.4 %copy-start.13 = (f32[64,27,27]{0,2,1:T(8,128)S(1)}, f32[64,27,27]{0,2,1:T(8,128)}, u32[]{:S(2)}) copy-start(f32[64,27,27]{0,2,1:T(8,128)} %constant.52.clone) | copy-start | bytes 559876
  38.6 7.5 %collective-permute-start.4 = (f32[2,2,16,1,16,128]{5,2,4,1,0,3:T(8,128)}, f32[2,2,16,1,16,128]{5,2,4,1,0,3:T(8,128)}, u32[]{:S(2)}, u32[]{:S(2)}) collective-permute-start(f32[2,2,16,1,16,128]{5,2,4,1,0,3:T(8,128)} %slice_bitcast_fusion.3), channel_id=1, source_target_pairs={{0,4},{4,8},{8,12},{12,16},{16,20},{20,24},{24,28},{1,5},{5,9},{9,... | collective-permute-start | bytes 1572872 | tf_op jit(solution)/shard_map/ppermute | solution.py:15
  47.6 1.2 %copy-start.9 = (bf16[8,32,1,16,128]{4,3,1,2,0:T(8,128)(2,1)S(1)}, bf16[8,32,1,16,128]{4,3,1,2,0:T(8,128)(2,1)}, u32[]{:S(2)}) copy-start(bf16[8,32,1,16,128]{4,3,1,2,0:T(8,128)(2,1)} %copy-done.8) | copy-start | bytes 3145732
  50.8 5.9 %collective-permute-start.5 = (f32[56,128]{1,0:T(8,128)S(1)}, f32[56,128]{1,0:T(8,128)S(1)}, u32[]{:S(2)}, u32[]{:S(2)}) collective-permute-start(f32[56,128]{1,0:T(8,128)S(1)} %broadcast_select_fusion.2), channel_id=1, source_target_pairs={{0,4},{4,0},{8,12},{12,8},{16,20},{20,16},{24,28},{28,24},{1,5},{5... | collective-permute-start | bytes 86024 | tf_op jit(solution)/shard_map/ppermute | solution.py:165
  56.7 4.6 %collective-permute-start.6 = (f32[56,128]{1,0:T(8,128)S(1)}, f32[56,128]{1,0:T(8,128)S(1)}, u32[]{:S(2)}, u32[]{:S(2)}) collective-permute-start(f32[56,128]{1,0:T(8,128)S(1)} %select_add_fusion), channel_id=1, source_target_pairs={{0,8},{4,12},{8,0},{12,4},{16,24},{20,28},{24,16},{28,20},{1,9},{5... | collective-permute-start | bytes 86024 | tf_op jit(solution)/shard_map/ppermute | solution.py:165
  61.4 4.9 %collective-permute-start.7 = (f32[56,128]{1,0:T(8,128)S(1)}, f32[56,128]{1,0:T(8,128)S(1)}, u32[]{:S(2)}, u32[]{:S(2)}) collective-permute-start(f32[56,128]{1,0:T(8,128)S(1)} %add.89), channel_id=1, source_target_pairs={{0,16},{4,20},{8,24},{12,28},{16,0},{20,4},{24,8},{28,12},{1,17},{... | collective-permute-start | bytes 86024 | tf_op jit(solution)/shard_map/ppermute | solution.py:165
  66.3 4.3 %collective-permute-start.8 = (f32[56,128]{1,0:T(8,128)S(1)}, f32[56,128]{1,0:T(8,128)S(1)}, u32[]{:S(2)}, u32[]{:S(2)}) collective-permute-start(f32[56,128]{1,0:T(8,128)S(1)} %add.90), channel_id=1, source_target_pairs={{0,1},{1,0},{2,3},{3,2},{4,5},{5,4},{6,7},{7,6},{8,9},{9,8},{10,11... | collective-permute-start | bytes 86024 | tf_op jit(solution)/shard_map/ppermute | solution.py:165
  70.6 3.9 %collective-permute-start.9 = (f32[56,128]{1,0:T(8,128)S(1)}, f32[56,128]{1,0:T(8,128)S(1)}, u32[]{:S(2)}, u32[]{:S(2)}) collective-permute-start(f32[56,128]{1,0:T(8,128)S(1)} %add.91), channel_id=1, source_target_pairs={{0,2},{1,3},{2,0},{3,1},{4,6},{5,7},{6,4},{7,5},{8,10},{9,11},{10,... | collective-permute-start | bytes 86024 | tf_op jit(solution)/shard_map/ppermute | solution.py:165
  74.5 1.2 %collective-permute-start.10 = (f32[56,128]{1,0:T(8,128)S(1)}, f32[56,128]{1,0:T(8,128)S(1)}, u32[]{:S(2)}, u32[]{:S(2)}) collective-permute-start(f32[56,128]{1,0:T(8,128)S(1)} %add.92), channel_id=1, source_target_pairs={{0,4},{4,0},{8,12},{12,8},{16,20},{20,16},{24,28},{28,24},{1,5},{5... | collective-permute-start | bytes 86024 | tf_op jit(solution)/shard_map/ppermute | solution.py:165
  (3 other events, 2.8 us)

commit v2 on v0

v2 whole, which is shorter than its diff:
```python
import math

import jax
import jax.numpy as jnp
import numpy as np
from jax import lax
from jax.experimental import pallas as pl
from jax.experimental.pallas import tpu as pltpu
from jax.sharding import PartitionSpec as P

ROWS = 4
HIDDEN_ROWS = 2 * ROWS + 1
PAIR_ROWS = 5
BLOCKS = 3 * PAIR_ROWS * 3
LANES = 128
MIB = 1024 * 1024


def axis_tap(parity, offset):
    if parity == 0:
        return 1
    return 2 if offset == 0 else 0


def block_taps():
    per_axis = ({0: 1}, {0: 2, 1: 0}, {1: 1}, {1: 2, 2: 0})
    table = np.full((48, LANES), -1, np.int32)
    for src_x in range(3):
        for src_y in range(PAIR_ROWS):
            for src_z in range(3):
                block = (src_x * PAIR_ROWS + src_y) * 3 + src_z
                for res_x in range(4):
                    for res_z in range(4):
                        for row in range(8):
                            along_y = src_y - 2 * (row // 4)
                            tap_x = per_axis[res_x].get(src_x)
                            tap_y = per_axis[row % 4].get(along_y)
                            tap_z = per_axis[res_z].get(src_z)
                            if tap_x is None or tap_y is None or tap_z is None:
                                continue
                            at = (res_x * 4 + res_z) * 8 + row
                            table[block, at] = 9 * tap_x + 3 * tap_y + tap_z
    return table


def slot_of(tap):
    tap_x, tap_y, tap_z = (tap // 9, tap // 3 % 3, tap % 3)
    off_y, off_z = (int(tap_y == 0), int(tap_z == 0))
    if tap_y == 1 and tap_z == 1:
        return (96, 32 * tap_x)
    if tap_y == 1:
        return (32 * tap_x + 16, 32 * off_z)
    if tap_z == 1:
        return (32 * tap_x + 16, 64 if off_y == 1 else 96)
    return (32 * tap_x, 64 * off_y + 32 * off_z)


def lane_index(shape):
    return lax.broadcasted_iota(jnp.int32, shape, 1)


def next_lane(tile):
    moved = pltpu.roll(tile, LANES - 1, 1)
    return jnp.where(lane_index(tile.shape) == LANES - 1, 0.0, moved)


def previous_lane(tile):
    moved = pltpu.roll(tile, 1, 1)
    return jnp.where(lane_index(tile.shape) == 0, 0.0, moved)


def logistic(values):
    return 1.0 / (1.0 + jnp.exp(-values))


def matmul(left, right):
    return jnp.dot(left, right, preferred_element_type=jnp.float32)


def matmul_nt(left, right):
    return lax.dot_general(
        left, right, (((1,), (1,)), ((), ())), preferred_element_type=jnp.float32
    )


def fill_onehot(taps, onehot):
    row = lax.broadcasted_iota(jnp.int32, (32, LANES), 0)
    for block in range(BLOCKS):
        hit = row == jnp.broadcast_to(taps[block : block + 1, :], (32, LANES))
        onehot[:, block * LANES : (block + 1) * LANES] = jnp.where(hit, 1.0, 0.0).astype(
            jnp.bfloat16
        )


def fill_matrices(w_three, w_four, onehot, m_three, m_four, m_back, build):
    build[...] = jnp.zeros_like(build)
    for tap in range(27):
        tap_x, tap_y, tap_z = (tap // 9, tap // 3 % 3, tap % 3)
        par_y, off_y = (int(tap_y != 1), int(tap_y == 0))
        par_z, off_z = (int(tap_z != 1), int(tap_z == 0))
        row = par_y * 32 + par_z * 16
        lane = off_y * 64 + off_z * 32
        places = (((1, 1),), ((0, 0), (2, 1)), ((1, 0),))[tap_x]
        values = w_three[tap].astype(jnp.float32)
        for plane, off_x in places:
            build[
                plane * 64 + row : plane * 64 + row + 16,
                off_x * 128 + lane : off_x * 128 + lane + 32,
            ] = values
    m_three[...] = build[...].astype(jnp.bfloat16)
    spread = matmul(w_four[...], onehot[:27, :])
    columns = jnp.concatenate(
        [spread[:, block * LANES : (block + 1) * LANES] for block in range(BLOCKS)], 0
    )
    m_back[...] = columns.astype(jnp.bfloat16)
    m_four[...] = columns.T.astype(jnp.bfloat16)


def coarse_tile(rows):
    return jnp.concatenate([rows, next_lane(rows)], 0).astype(jnp.bfloat16)


def field_pair(elec, temp, adj, adj_grad, scale, res_x, lanes):
    energy = 0.0
    thermal = 0.0
    for comp in range(3):
        field = elec[comp, res_x, :, lanes].astype(jnp.float32)
        energy = energy + field * field
        thermal = thermal + temp[comp, res_x, :, lanes].astype(jnp.float32) * adj_grad[
            comp, res_x, :, lanes
        ].astype(jnp.float32)
    gain = (scale * 3.0 * (1.0 - 0.001)) * (energy * adj[res_x, :, lanes].astype(jnp.float32))
    return (gain, (scale * 2.0 * (1.0 - 0.01)) * thermal)


def quad(refs, tiles, field_terms):
    (m_three, m_four, m_back, density) = refs[:4]
    (sum_three, sum_four, wide, slope, windows, g_fine, g_pre) = refs[4:]
    blank = jnp.zeros((64, LANES), jnp.bfloat16)
    for b in range(ROWS + 1):
        for plane in range(2):
            after = tiles[plane][b + 1] if b < ROWS else blank
            wide[plane * 128 : plane * 128 + 64, b * LANES : (b + 1) * LANES] = tiles[plane][b]
            wide[plane * 128 + 64 : plane * 128 + 128, b * LANES : (b + 1) * LANES] = after
    pre = matmul(m_three[...], wide[...])
    sigma = logistic(pre)
    hidden = pre * sigma
    slope[...] = sigma * (1.0 + pre * (1.0 - sigma))
    for plane in range(3):
        for row in range(HIDDEN_ROWS):
            b, par = (row // 2, row % 2)
            at = plane * 64 + par * 32
            both = hidden[at : at + 32, b * LANES : (b + 1) * LANES]
            tall = jnp.concatenate([both, next_lane(both[:16])], 0).astype(jnp.bfloat16)
            for half in range(2):
                within = row - 4 * half
                if 0 <= within < PAIR_ROWS:
                    start = (plane * PAIR_ROWS + within) * 48
                    windows[start : start + 48, half * LANES : (half + 1) * LANES] = tall
    dens = logistic(matmul(m_four[...], windows[...]))
    for res_x in range(4):
        for res_z in range(4):
            at = (res_x * 4 + res_z) * 8
            lanes = slice(res_z * LANES, (res_z + 1) * LANES)
            d = jnp.concatenate([dens[at : at + 8, :LANES], dens[at : at + 8, LANES:]], 0)
            density[res_x, :, lanes] = d
            gain, loss = field_terms(res_x, lanes)
            g = d * d * (1.0 - d) * (gain * d - loss)
            g_fine[at : at + 8, :LANES] = g[:8]
            g_fine[at : at + 8, LANES:] = g[8:]
    g_out = g_fine[...].astype(jnp.bfloat16)
    sum_four[...] += matmul_nt(windows[...], g_out)
    spread = matmul(m_back[...], g_out)
    for plane in range(3):
        for row in range(HIDDEN_ROWS):
            b, par = (row // 2, row % 2)
            tall = 0.0
            for half in range(2):
                within = row - 4 * half
                if 0 <= within < PAIR_ROWS:
                    start = (plane * PAIR_ROWS + within) * 48
                    tall = tall + spread[start : start + 48, half * LANES : (half + 1) * LANES]
            both = jnp.concatenate([tall[:16] + previous_lane(tall[32:]), tall[16:32]], 0)
            at = plane * 64 + par * 32
            lanes = slice(b * LANES, (b + 1) * LANES)
            if plane == 1 and 0 < row < HIDDEN_ROWS - 1:
                both = both.astype(jnp.bfloat16).astype(jnp.float32)
            g_pre[at : at + 32, lanes] = (both * slope[at : at + 32, lanes]).astype(jnp.bfloat16)
        g_pre[plane * 64 + 32 : plane * 64 + 64, ROWS * LANES :] = jnp.zeros(
            (32, LANES), jnp.bfloat16
        )
    sum_three[...] += matmul_nt(g_pre[...], wide[...])


def interior_kernel(scale, count_a, place, *refs):
    (near, far, w_three, w_four, taps, elec, temp, adj, adj_grad) = refs[:9]
    (density, sum_three, sum_four, m_three, m_four, m_back) = refs[9:15]
    (last_gain, last_loss, last_cells) = refs[15:18]
    (build, onehot, flat, cells, wide, slope, windows, g_fine, g_pre) = refs[18:]
    step = pl.program_id(0)
    held = near.shape[2]

    @pl.when(step == 0)
    def _():
        sum_three[...] = jnp.zeros_like(sum_three)
        sum_four[...] = jnp.zeros_like(sum_four)
        fill_onehot(taps, onehot)
        fill_matrices(w_three, w_four, onehot, m_three, m_four, m_back, build)
        inside = (place[0] + 1 < count_a).astype(jnp.float32)
        for plane, block in enumerate((near, far)):
            values = block[:, 0].astype(jnp.float32)
            if plane == 1:
                values = values * inside
            flat[plane] = values.reshape(flat.shape[1:])
        for plane in range(2):
            for b in range(held):
                tile = coarse_tile(flat[plane, pl.ds(b, 32, held), :])
                cells[plane, b] = tile
                if b >= held - ROWS:
                    last_cells[plane, b - held + ROWS] = tile

    def field_terms(res_x, lanes):
        return field_pair(elec, temp, adj, adj_grad, scale, res_x, lanes)

    @pl.when(step < pl.num_programs(0) - 1)
    def _():
        tiles = [[cells[plane, step * ROWS + b] for b in range(ROWS + 1)] for plane in range(2)]
        quad(
            (m_three, m_four, m_back, density)
            + (sum_three, sum_four, wide, slope, windows, g_fine, g_pre),
            tiles,
            field_terms,
        )

    @pl.when(step == pl.num_programs(0) - 1)
    def _():
        for res_x in range(4):
            for res_z in range(4):
                lanes = slice(res_z * LANES, (res_z + 1) * LANES)
                gain, loss = field_terms(res_x, lanes)
                last_gain[res_x, :, lanes] = gain
                last_loss[res_x, :, lanes] = loss


def rim_kernel(count_a, place, *refs):
    (rim, taps, m_three, m_four, m_back, sum_three_in, sum_four_in) = refs[:7]
    (last_gain, last_loss, last_cells, _) = refs[7:11]
    (density, mine, other) = refs[11:14]
    (packed, sum_three, sum_four, onehot, wide, slope, windows, g_fine, g_pre) = refs[14:]
    sum_three[...] = sum_three_in[...]
    sum_four[...] = sum_four_in[...]
    inside = (place[0] + 1 < count_a).astype(jnp.float32)
    tiles = []
    for plane in range(2):
        edge = rim[plane].astype(jnp.float32)
        if plane == 1:
            edge = edge * inside
        tiles.append([last_cells[plane, b] for b in range(ROWS)] + [coarse_tile(edge)])
    fill_onehot(taps, onehot)
    quad(
        (m_three, m_four, m_back, density)
        + (sum_three, sum_four, wide, slope, windows, g_fine, g_pre),
        tiles,
        lambda res_x, lanes: (last_gain[res_x, :, lanes], last_loss[res_x, :, lanes]),
    )
    by_tap = (
        sum_three[64:128, 128:],
        sum_three[:64, :128] + sum_three[128:, 128:],
        sum_three[64:128, :128],
    )
    for tap_x in range(3):
        part = by_tap[tap_x]
        packed[32 * tap_x : 32 * tap_x + 16, :] = part[48:64]
        lanes = lane_index((16, LANES))
        mixed = jnp.where(
            lanes < 64,
            part[16:32],
            jnp.where(lanes < 96, part[32:48], pltpu.roll(part[32:48], 96, 1)),
        )
        packed[32 * tap_x + 16 : 32 * tap_x + 32, :] = mixed
        packed[96:112, 32 * tap_x : 32 * tap_x + 32] = part[:16, :32]
    rest = jnp.concatenate(
        [sum_four[16 * block : 16 * block + 16, :] for block in range(BLOCKS)], 1
    )
    pieces = []
    for _ in range(3):
        piece = rest.astype(jnp.bfloat16)
        pieces.append(piece)
        rest = rest - piece.astype(jnp.float32)
    folded = matmul_nt(jnp.concatenate(pieces, 0), onehot[...])
    packed[96:112, 96:128] = folded[:16] + folded[16:32] + folded[32:48]
    part = place[1]
    half = mine.shape[0]
    mine[...] = packed[pl.ds(pl.multiple_of(part * half, 8), half), :]
    other[...] = packed[pl.ds(pl.multiple_of((1 - part) * half, 8), half), :]


def unpack_kernel(part, mine, other, grad_three, grad_four):
    low = part[0] == 0
    whole = jnp.concatenate(
        [
            jnp.where(low, mine[...], other[...]),
            jnp.where(low, other[...], mine[...]),
        ],
        0,
    )
    for tap in range(27):
        row, lane = slot_of(tap)
        grad_three[tap] = whole[row : row + 16, lane : lane + 32]
    grad_four[...] = whole[96:112, 96:123]


def exchanged(value, bit_x, bit_y):
    size_x, size_y = (lax.axis_size("gx"), lax.axis_size("gy"))
    pairs = [
        (i * size_y + j, (i ^ bit_x) * size_y + (j ^ bit_y))
        for i in range(size_x)
        for j in range(size_y)
    ]
    return lax.ppermute(value, ("gx", "gy"), pairs)


def parity_of(index):
    total = index
    for shift in (1, 2, 3, 4, 5, 6, 7):
        total = total ^ (index >> shift)
    return total & 1


def sum_everywhere(mine, other, part):
    size_x, size_y = (lax.axis_size("gx"), lax.axis_size("gy"))
    assert size_x & (size_x - 1) == 0 and size_y & (size_y - 1) == 0
    assert 2 <= size_x <= 256 and size_y <= 256
    mine = mine + exchanged(other, 1, 0)
    bit = 2
    while bit < size_x:
        mine = mine + exchanged(mine, bit + 1, 0)
        bit = bit * 2
    bit = 1
    while bit < size_y:
        mine = mine + exchanged(mine, 1, bit)
        bit = bit * 2
    other = exchanged(mine, 1, 0)
    spec = pl.BlockSpec(memory_space=pltpu.VMEM)
    grad_three, grad_four = pl.pallas_call(
        unpack_kernel,
        out_shape=(
            jax.ShapeDtypeStruct((27, 16, 32), jnp.float32),
            jax.ShapeDtypeStruct((16, 27), jnp.float32),
        ),
        in_specs=[pl.BlockSpec(memory_space=pltpu.SMEM), spec, spec],
        out_specs=(spec, spec),
        compiler_params=pltpu.CompilerParams(vmem_limit_bytes=2 * MIB),
        name="unpack",
    )(part, mine, other)
    return (grad_three, grad_four.T)


def shards(coarse, w_three, w_four, elec_field, temp_grad, adjoint, adjoint_grad):
    groups_x, groups_y = (lax.axis_size("gx"), lax.axis_size("gy"))
    chan_in, count_a, held, depth = coarse.shape
    fine_x, fine_y, fine_z = adjoint.shape
    assert (fine_x, fine_y, fine_z) == (4, 4 * held, 4 * LANES)
    assert depth == LANES and chan_in == 32 and held % ROWS == 0 and count_a == groups_x
    cells = fine_x * groups_x * fine_y * groups_y * fine_z
    scale = 8.0 / math.sqrt(cells)
    at_x = lax.axis_index("gx").astype(jnp.int32)
    far_x = jnp.minimum(at_x + 1, count_a - 1)
    first_row = jnp.concatenate(
        [
            lax.dynamic_slice(coarse, (0, at, 0, 0), (chan_in, 1, 1, depth)).reshape(
                1, chan_in, depth
            )
            for at in (at_x, far_x)
        ],
        0,
    )
    rim = lax.ppermute(first_row, "gy", [(i + 1, i) for i in range(groups_y - 1)])
    part = parity_of(lax.axis_index("gx")) ^ parity_of(lax.axis_index("gy"))
    place = jnp.stack([at_x, part.astype(jnp.int32)])
    taps = jnp.asarray(block_taps())
    steps = held // ROWS
    window_rows = 48 * 3 * PAIR_ROWS
    inner = (
        pltpu.VMEM((256, (ROWS + 1) * LANES), jnp.bfloat16),
        pltpu.VMEM((192, (ROWS + 1) * LANES), jnp.float32),
        pltpu.VMEM((window_rows, 2 * LANES), jnp.bfloat16),
        pltpu.VMEM((LANES, 2 * LANES), jnp.float32),
        pltpu.VMEM((192, (ROWS + 1) * LANES), jnp.bfloat16),
    )
    onehot = pltpu.VMEM((32, BLOCKS * LANES), jnp.bfloat16)

    def whole(entry):
        return pl.BlockSpec(entry.shape, lambda step, place: (0,) * len(entry.shape))

    def shape(dims, dtype):
        return jax.ShapeDtypeStruct(dims, dtype)

    def in_hbm(value):
        return pltpu.with_memory_space_constraint(value, pltpu.HBM)

    triple = pl.BlockSpec((3, 4, 16, fine_z), lambda step, place: (0, 0, step, 0))
    single = pl.BlockSpec((4, 16, fine_z), lambda step, place: (0, step, 0))
    dense = shape(adjoint.shape, jnp.float32)
    sums = (shape((192, 256), jnp.float32), shape((window_rows, LANES), jnp.float32))
    matrices = (
        shape((192, 256), jnp.bfloat16),
        shape((LANES, window_rows), jnp.bfloat16),
        shape((window_rows, LANES), jnp.bfloat16),
    )
    handed = (
        shape((4, 16, fine_z), jnp.float32),
        shape((4, 16, fine_z), jnp.float32),
        shape((2, ROWS, 64, LANES), jnp.bfloat16),
    )
    half = shape((56, LANES), jnp.float32)
    w_four_t = w_four.T
    coarse_hbm = in_hbm(coarse)
    density, sum_three, sum_four, m_three, m_four, m_back, *rest = pl.pallas_call(
        lambda *refs: interior_kernel(scale, count_a, *refs),
        out_shape=(dense,) + sums + matrices + handed,
        grid_spec=pltpu.PrefetchScalarGridSpec(
            num_scalar_prefetch=1,
            grid=(steps,),
            in_specs=[
                pl.BlockSpec((chan_in, 1, held, depth), lambda step, place: (0, place[0], 0, 0)),
                pl.BlockSpec(
                    (chan_in, 1, held, depth),
                    lambda step, place: (0, jnp.minimum(place[0] + 1, count_a - 1), 0, 0),
                ),
                whole(w_three),
                whole(w_four_t),
                whole(taps),
                triple,
                triple,
                single,
                triple,
            ],
            out_specs=[
                pl.BlockSpec(
                    (4, 16, fine_z), lambda step, place: (0, jnp.minimum(step, steps - 2), 0)
                )
            ]
            + [whole(entry) for entry in sums + matrices + handed],
            scratch_shapes=(
                pltpu.VMEM((192, 256), jnp.float32),
                onehot,
                pltpu.VMEM((2, chan_in * held, LANES), jnp.float32),
                pltpu.VMEM((2, held, 64, LANES), jnp.bfloat16),
            )
            + inner,
        ),
        compiler_params=pltpu.CompilerParams(vmem_limit_bytes=24 * MIB),
        cost_estimate=pl.CostEstimate(
            flops=2000000000, bytes_accessed=4000000, transcendentals=2000000
        ),
        name="interior",
    )(
        place,
        coarse_hbm,
        coarse_hbm,
        w_three,
        w_four_t,
        taps,
        in_hbm(elec_field),
        in_hbm(temp_grad),
        in_hbm(adjoint),
        in_hbm(adjoint_grad),
    )
    density, mine, other = pl.pallas_call(
        lambda *refs: rim_kernel(count_a, *refs),
        out_shape=(dense, half, half),
        grid_spec=pltpu.PrefetchScalarGridSpec(
            num_scalar_prefetch=1,
            grid=(1,),
            in_specs=[whole(rim), whole(taps)]
            + [whole(entry) for entry in matrices + sums + handed]
            + [pl.BlockSpec(memory_space=pl.ANY)],
            out_specs=[
                pl.BlockSpec((4, 16, fine_z), lambda step, place: (0, steps - 1, 0)),
                whole(half),
                whole(half),
            ],
            scratch_shapes=(pltpu.VMEM((112, LANES), jnp.float32),)
            + tuple(pltpu.VMEM(entry.shape, entry.dtype) for entry in sums)
            + (onehot,)
            + inner,
        ),
        input_output_aliases={11: 0},
        compiler_params=pltpu.CompilerParams(vmem_limit_bytes=16 * MIB),
        cost_estimate=pl.CostEstimate(
            flops=700000000, bytes_accessed=2000000, transcendentals=700000
        ),
        name="rim",
    )(place, rim, taps, m_three, m_four, m_back, sum_three, sum_four, *rest, density)
    grad_three, grad_four = sum_everywhere(mine, other, place[1:])
    return (density, grad_three, grad_four)


def solution(mesh):
    return jax.shard_map(
        shards,
        mesh=mesh,
        in_specs=(
            P(None, None, "gy", None),
            P(),
            P(),
            P(None, "gx", "gy", None),
            P(None, "gx", "gy", None),
            P("gx", "gy", None),
            P(None, "gx", "gy", None),
        ),
        out_specs=(P("gx", "gy", None), P(), P()),
        check_vma=False,
    )
```

time: 98 us -> 34.4 us (0.35)
  blocking collectives: 53.2 us -> 0 us
  Pallas kernels: 0 us -> 10.8 us
  matrix products: 5.33 us -> 0 us
  other arithmetic: 5.36 us -> 0.11 us
  local copies, waits for them, and re-layouts: 6.6 us -> 1.58 us
  waiting for transfers between devices: 12.9 us -> 7.96 us
    psum x1 -> x0, blocking collectives: 53.2 us -> none  [shards(): grad_three, grad_four = lax.psum((grad_three, grad_four), ('gx', 'gy'))]
    pallas_call x0 -> x3, Pallas kernels: none -> 10.8 us  [the longest x1 7.36 us: shards(): pl.pallas_call(lambda *refs: interior_kernel(scale, count_a, *refs), out_...]
    ppermute x5 -> x7, waiting for transfers between devices: 12.9 us -> 7.96 us  [the longest x6 7.95 us: exchanged(): return lax.ppermute(value, ('gx', 'gy'), pairs)]
    dot_general x8 -> x0, matrix products: 4.73 us -> none  [the longest x1 1.13 us: layer_three_matrix(): jnp.einsum('spk,koc->posc', lookup, weight, preferred_element_type=jnp.fl...]
    convert_element_type x4 -> x0, other arithmetic: 2.4 us -> none  [the longest x1 1.65 us: shards(): (scale * sensitivity * density * (1.0 - density)).astype(jnp.bfloat16)]
    slice x9 -> x0, local copies, waits for them, and re-layouts: 1.79 us -> none  [the longest x1 1.21 us: shards(): rim_row = beside_y(coarse[:, :, :1], -1)]
    unnamed x28 -> x6, local copies, waits for them, and re-layouts: 2.32 us -> 0.64 us
    reduce_sum x1 -> x0, other arithmetic: 1.36 us -> none  [shards(): jnp.sum(temp_grad.astype(jnp.float32) * adjoint_grad.astype(jnp.float32),...]
  transfers between devices with their start and end apart: 5 -> 7, of which waited for: 5 -> 6; matrix products, arithmetic and copies ran while one was open for 5% -> 0% of each run, Pallas kernels for 0% -> 22%
where the time goes in v2:
time: 34.4 us; the launch traced here: 34.1 us
  starting transfers between devices  12.9 us (38%)
  Pallas kernels  10.8 us (31%)
  waiting for transfers between devices  7.96 us (23%)
  local copies, waits for them, and re-layouts  1.58 us (5%)
  between operations  0.72 us (2%)
    ppermute x6, starting transfers between devices, exchanged(): return lax.ppermute(value, ('gx', 'gy'), pairs)  11.6 us
    ppermute x6, waiting for transfers between devices, exchanged(): return lax.ppermute(value, ('gx', 'gy'), pairs)  7.95 us
    pallas_call x1, Pallas kernels, shards(): pl.pallas_call(lambda *refs: interior_kernel(scale, count_a, *refs), out_...  7.36 us
    pallas_call x1, Pallas kernels, shards(): pl.pallas_call(lambda *refs: rim_kernel(count_a, *refs), out_shape=(dense...  2.64 us
    ppermute x1, starting transfers between devices, shards(): lax.ppermute(first_row, 'gy', [(i + 1, i) for i in range(groups_y - 1)])  1.29 us
    dynamic_slice x1, local copies, waits for them, and re-layouts, shards(): lax.dynamic_slice(coarse, (0, at, 0, 0), (chan_in, 1, 1, depth))  0.93 us
    pallas_call x1, Pallas kernels, sum_everywhere(): pl.pallas_call(unpack_kernel, out_shape=(jax.ShapeDtypeStruct((27, 16, 32...  0.8 us
  transfers between devices with their start and end apart: 7, of which 6 were waited for; matrix products, arithmetic and copies ran while one was open for 0% of the time, Pallas kernels for 22%

profile of v2, /device:TPU:0, one launch (start us, length us, event | category | flops | bytes accessed | tf_op | source)
XLA Modules:
  0.0 34.1 jit_solution(3572961826267100638)
XLA Ops:
  0.6 0.0 copy-start
  0.6 0.9 %constant_dynamic-slice_fusion.1 = (bf16[32,1,1,128]{3,2,1,0:T(2,128)(2,1)S(1)}, bf16[32,1,1,128]{3,2,1,0:T(2,128)(2,1)S(1)}) fusion(bf16[32,8,16,128]{3,2,1,0:T(8,128)(2,1)} %refs_2_.2, s32[]{:T(128)S(6)} %select_n.6, s32[]{:T(128)S(6)} %select_n.7), kind=kLoop, calls=%fused_computation.5 | loop fusion | bytes 32776 | tf_op jit(solution)/shard_map/dynamic_slice | solution.py:371
  1.6 1.3 %collective-permute-start = (bf16[2,32,128]{2,1,0:T(8,128)(2,1)S(1)}, bf16[2,32,128]{2,1,0:T(8,128)(2,1)S(1)}, u32[]{:S(2)}, u32[]{:S(2)}) collective-permute-start(bf16[2,32,128]{2,1,0:T(8,128)(2,1)S(1)} %pad_maximum_fusion), channel_id=1, source_target_pairs={{1,0},{2,1},{3,2},{5,4},{6,5},{7,6},{9,8},{10,9},{11,10},{13,12},{... | collective-permute-start | bytes 49160 | tf_op jit(solution)/shard_map/ppermute | solution.py:378
  2.9 0.0 copy-start.2
  2.9 0.0 copy-start.1
  3.0 0.1 pad_add_fusion.refs_0_
  3.0 0.0 copy-done
  3.0 0.6 %copy-done.2 = s32[48,128]{1,0:T(8,128)S(1)} copy-done((s32[48,128]{1,0:T(8,128)S(1)}, s32[48,128]{1,0:T(8,128)}, u32[]{:S(2)}) %copy-start.2) | copy-done | bytes 24600
  3.7 7.4 %interior.1 = (f32[4,64,512]{2,1,0:T(8,128)}, f32[192,256]{1,0:T(8,128)S(1)}, f32[720,128]{1,0:T(8,128)S(1)}, bf16[192,256]{1,0:T(8,128)(2,1)S(1)}, bf16[128,720...) custom-call(s32[2]{0:T(128)S(1)} %pad_add_fusion.refs_0_, ...), custom_call_target="tpu_custom_call" | custom-call | flops 2000000000 | bytes 4000000 | tf_op jit(solution)/shard_map/interior/pallas_call | solution.py:419
  11.0 0.0 collective-permute-done.refs_1_
  11.0 2.6 %rim.1 = (f32[4,64,512]{2,1,0:T(8,128)}, f32[56,128]{1,0:T(8,128)S(1)}, f32[56,128]{1,0:T(8,128)S(1)}) custom-call(s32[2]{0:T(128)S(1)} %pad_add_fusion.refs_0_, bf16[2,32,128]{2,1,0:T(8,128)(2,1)S(1)} %collective-permute-done.refs_1_, s32[48,128]{1,0:T(8,128)S(1)} %copy-done.2, ...), custom_call_target="tpu_custom_call", output_to_operand_aliasing={{0}: (11, {})} | custom-call | flops 700000000 | bytes 2000000 | tf_op jit(solution)/shard_map/rim/pallas_call | solution.py:470
  13.7 0.5 %collective-permute-start.1 = (f32[56,128]{1,0:T(8,128)S(1)}, f32[56,128]{1,0:T(8,128)S(1)}, u32[]{:S(2)}, u32[]{:S(2)}) collective-permute-start(f32[56,128]{1,0:T(8,128)S(1)} %get-tuple-element.28), channel_id=1, source_target_pairs={{0,4},{1,5},{2,6},{3,7},{4,0},{5,1},{6,2},{7,3},{8,12},{9,13},{10,... | collective-permute-start | bytes 86024 | tf_op jit(solution)/shard_map/ppermute | solution.py:320
  14.2 0.9 %collective-permute-done.1 = f32[56,128]{1,0:T(8,128)S(1)} collective-permute-done((f32[56,128]{1,0:T(8,128)S(1)}, f32[56,128]{1,0:T(8,128)S(1)}, u32[]{:S(2)}, u32[]{:S(2)}) %collective-permute-start.1) | collective-permute-done | bytes 28704 | tf_op jit(solution)/shard_map/ppermute | solution.py:320
  15.0 2.7 %collective-permute-start.2 = (f32[56,128]{1,0:T(8,128)S(1)}, f32[56,128]{1,0:T(8,128)S(1)}, u32[]{:S(2)}, u32[]{:S(2)}) collective-permute-start(f32[56,128]{1,0:T(8,128)S(1)} %add.27), channel_id=1, source_target_pairs={{0,12},{1,13},{2,14},{3,15},{4,8},{5,9},{6,10},{7,11},{8,4},{9,5},... | collective-permute-start | bytes 86024 | tf_op jit(solution)/shard_map/ppermute | solution.py:320
  17.7 1.6 %collective-permute-done.2 = f32[56,128]{1,0:T(8,128)S(1)} collective-permute-done((f32[56,128]{1,0:T(8,128)S(1)}, f32[56,128]{1,0:T(8,128)S(1)}, u32[]{:S(2)}, u32[]{:S(2)}) %collective-permute-start.2) | collective-permute-done | bytes 28704 | tf_op jit(solution)/shard_map/ppermute | solution.py:320
  19.3 2.7 %collective-permute-start.3 = (f32[56,128]{1,0:T(8,128)S(1)}, f32[56,128]{1,0:T(8,128)S(1)}, u32[]{:S(2)}, u32[]{:S(2)}) collective-permute-start(f32[56,128]{1,0:T(8,128)S(1)} %add.28), channel_id=1, source_target_pairs={{0,20},{1,21},{2,22},{3,23},{4,16},{5,17},{6,18},{7,19},{8,28},{9,... | collective-permute-start | bytes 86024 | tf_op jit(solution)/shard_map/ppermute | solution.py:320
  22.0 1.6 %collective-permute-done.3 = f32[56,128]{1,0:T(8,128)S(1)} collective-permute-done((f32[56,128]{1,0:T(8,128)S(1)}, f32[56,128]{1,0:T(8,128)S(1)}, u32[]{:S(2)}, u32[]{:S(2)}) %collective-permute-start.3) | collective-permute-done | bytes 28704 | tf_op jit(solution)/shard_map/ppermute | solution.py:320
  23.6 2.6 %collective-permute-start.4 = (f32[56,128]{1,0:T(8,128)S(1)}, f32[56,128]{1,0:T(8,128)S(1)}, u32[]{:S(2)}, u32[]{:S(2)}) collective-permute-start(f32[56,128]{1,0:T(8,128)S(1)} %add.29), channel_id=1, source_target_pairs={{0,5},{1,4},{2,7},{3,6},{4,1},{5,0},{6,3},{7,2},{8,13},{9,12},{10,... | collective-permute-start | bytes 86024 | tf_op jit(solution)/shard_map/ppermute | solution.py:320
  26.2 1.6 %collective-permute-done.4 = f32[56,128]{1,0:T(8,128)S(1)} collective-permute-done((f32[56,128]{1,0:T(8,128)S(1)}, f32[56,128]{1,0:T(8,128)S(1)}, u32[]{:S(2)}, u32[]{:S(2)}) %collective-permute-start.4) | collective-permute-done | bytes 28704 | tf_op jit(solution)/shard_map/ppermute | solution.py:320
  27.7 2.8 %collective-permute-start.5 = (f32[56,128]{1,0:T(8,128)S(1)}, f32[56,128]{1,0:T(8,128)S(1)}, u32[]{:S(2)}, u32[]{:S(2)}) collective-permute-start(f32[56,128]{1,0:T(8,128)S(1)} %add.30), channel_id=1, source_target_pairs={{0,6},{1,7},{2,4},{3,5},{4,2},{5,3},{6,0},{7,1},{8,14},{9,15},{10,... | collective-permute-start | bytes 86024 | tf_op jit(solution)/shard_map/ppermute | solution.py:320
  30.5 1.6 %collective-permute-done.5 = f32[56,128]{1,0:T(8,128)S(1)} collective-permute-done((f32[56,128]{1,0:T(8,128)S(1)}, f32[56,128]{1,0:T(8,128)S(1)}, u32[]{:S(2)}, u32[]{:S(2)}) %collective-permute-start.5) | collective-permute-done | bytes 28704 | tf_op jit(solution)/shard_map/ppermute | solution.py:320
  32.1 0.3 collective-permute-start.6
  32.4 0.9 %collective-permute-done.6.other = f32[56,128]{1,0:T(8,128)S(1)} collective-permute-done((f32[56,128]{1,0:T(8,128)S(1)}, f32[56,128]{1,0:T(8,128)S(1)}, u32[]{:S(2)}, u32[]{:S(2)}) %collective-permute-start.6) | collective-permute-done | bytes 28704 | tf_op jit(solution)/shard_map/ppermute | solution.py:320
  33.3 0.8 %unpack.1 = (f32[27,16,32]{2,1,0:T(8,128)}, f32[16,27]{1,0:T(8,128)}) custom-call(s32[1]{0:T(128)} %bitcast.1.part, f32[56,128]{1,0:T(8,128)S(1)} %add.31.mine, f32[56,128]{1,0:T(8,128)S(1)} %collective-permute-done.6.other), custom_call_target="tpu_custom_call" | custom-call | tf_op jit(solution)/shard_map/unpack/pallas_call | solution.py:345
  (8 shorter events, 0.0 us)
Async XLA Ops:
  0.6 2.4 %copy-start = (bf16[27,16,32]{2,1,0:T(8,128)(2,1)S(1)}, bf16[27,16,32]{2,1,0:T(8,128)(2,1)}, u32[]{:S(2)}) copy-start(bf16[27,16,32]{2,1,0:T(8,128)(2,1)} %refs_3_.1) | copy-start | bytes 82948
  1.6 9.4 %collective-permute-start = (bf16[2,32,128]{2,1,0:T(8,128)(2,1)S(1)}, bf16[2,32,128]{2,1,0:T(8,128)(2,1)S(1)}, u32[]{:S(2)}, u32[]{:S(2)}) collective-permute-start(bf16[2,32,128]{2,1,0:T(8,128)(2,1)S(1)} %pad_maximum_fusion), channel_id=1, source_target_pairs={{1,0},{2,1},{3,2},{5,4},{6,5},{7,6},{9,8},{10,9},{11,10},{13,12},{... | collective-permute-start | bytes 49160 | tf_op jit(solution)/shard_map/ppermute | solution.py:378
  2.9 0.7 %copy-start.2 = (s32[48,128]{1,0:T(8,128)S(1)}, s32[48,128]{1,0:T(8,128)}, u32[]{:S(2)}) copy-start(s32[48,128]{1,0:T(8,128)} %constant.29.clone.refs_5_.refs_2_) | copy-start | bytes 73732
  2.9 0.7 %copy-start.1 = (bf16[27,16]{0,1:T(8,128)(2,1)S(1)}, bf16[27,16]{0,1:T(8,128)(2,1)}, u32[]{:S(2)}) copy-start(bf16[27,16]{0,1:T(8,128)(2,1)} %param.10) | copy-start | bytes 2596
  13.7 1.4 %collective-permute-start.1 = (f32[56,128]{1,0:T(8,128)S(1)}, f32[56,128]{1,0:T(8,128)S(1)}, u32[]{:S(2)}, u32[]{:S(2)}) collective-permute-start(f32[56,128]{1,0:T(8,128)S(1)} %get-tuple-element.28), channel_id=1, source_target_pairs={{0,4},{1,5},{2,6},{3,7},{4,0},{5,1},{6,2},{7,3},{8,12},{9,13},{10,... | collective-permute-start | bytes 86024 | tf_op jit(solution)/shard_map/ppermute | solution.py:320
  15.0 4.2 %collective-permute-start.2 = (f32[56,128]{1,0:T(8,128)S(1)}, f32[56,128]{1,0:T(8,128)S(1)}, u32[]{:S(2)}, u32[]{:S(2)}) collective-permute-start(f32[56,128]{1,0:T(8,128)S(1)} %add.27), channel_id=1, source_target_pairs={{0,12},{1,13},{2,14},{3,15},{4,8},{5,9},{6,10},{7,11},{8,4},{9,5},... | collective-permute-start | bytes 86024 | tf_op jit(solution)/shard_map/ppermute | solution.py:320
  19.3 4.3 %collective-permute-start.3 = (f32[56,128]{1,0:T(8,128)S(1)}, f32[56,128]{1,0:T(8,128)S(1)}, u32[]{:S(2)}, u32[]{:S(2)}) collective-permute-start(f32[56,128]{1,0:T(8,128)S(1)} %add.28), channel_id=1, source_target_pairs={{0,20},{1,21},{2,22},{3,23},{4,16},{5,17},{6,18},{7,19},{8,28},{9,... | collective-permute-start | bytes 86024 | tf_op jit(solution)/shard_map/ppermute | solution.py:320
  23.6 4.1 %collective-permute-start.4 = (f32[56,128]{1,0:T(8,128)S(1)}, f32[56,128]{1,0:T(8,128)S(1)}, u32[]{:S(2)}, u32[]{:S(2)}) collective-permute-start(f32[56,128]{1,0:T(8,128)S(1)} %add.29), channel_id=1, source_target_pairs={{0,5},{1,4},{2,7},{3,6},{4,1},{5,0},{6,3},{7,2},{8,13},{9,12},{10,... | collective-permute-start | bytes 86024 | tf_op jit(solution)/shard_map/ppermute | solution.py:320
  27.7 4.3 %collective-permute-start.5 = (f32[56,128]{1,0:T(8,128)S(1)}, f32[56,128]{1,0:T(8,128)S(1)}, u32[]{:S(2)}, u32[]{:S(2)}) collective-permute-start(f32[56,128]{1,0:T(8,128)S(1)} %add.30), channel_id=1, source_target_pairs={{0,6},{1,7},{2,4},{3,5},{4,2},{5,3},{6,0},{7,1},{8,14},{9,15},{10,... | collective-permute-start | bytes 86024 | tf_op jit(solution)/shard_map/ppermute | solution.py:320
  32.1 1.2 %collective-permute-start.6 = (f32[56,128]{1,0:T(8,128)S(1)}, f32[56,128]{1,0:T(8,128)S(1)}, u32[]{:S(2)}, u32[]{:S(2)}) collective-permute-start(f32[56,128]{1,0:T(8,128)S(1)} %add.31.mine), channel_id=1, source_target_pairs={{0,4},{1,5},{2,6},{3,7},{4,0},{5,1},{6,2},{7,3},{8,12},{9,13},{10,... | collective-permute-start | bytes 86024 | tf_op jit(solution)/shard_map/ppermute | solution.py:320

commit v3 on v2

v3 whole, which is shorter than its diff:
```python
import math

import jax
import jax.numpy as jnp
from jax import lax
from jax.experimental import pallas as pl
from jax.experimental.pallas import tpu as pltpu
from jax.sharding import PartitionSpec as P

PAIR_ROWS = 5
BLOCKS = 3 * PAIR_ROWS * 3
WINDOW = BLOCKS * 16
LANES = 128
MIB = 1024 * 1024


def slot_of(tap):
    tap_x, tap_y, tap_z = (tap // 9, tap // 3 % 3, tap % 3)
    off_y, off_z = (int(tap_y == 0), int(tap_z == 0))
    if tap_y == 1 and tap_z == 1:
        return (96, 32 * tap_x)
    if tap_y == 1:
        return (32 * tap_x + 16, 32 * off_z)
    if tap_z == 1:
        return (32 * tap_x + 16, 64 if off_y == 1 else 96)
    return (32 * tap_x, 64 * off_y + 32 * off_z)


def lane_index(shape):
    return lax.broadcasted_iota(jnp.int32, shape, 1)


def next_lane(tile):
    moved = pltpu.roll(tile, LANES - 1, 1)
    return jnp.where(lane_index(tile.shape) == LANES - 1, 0.0, moved)


def previous_lane(tile):
    moved = pltpu.roll(tile, 1, 1)
    return jnp.where(lane_index(tile.shape) == 0, 0.0, moved)


def logistic(values):
    return 1.0 / (1.0 + jnp.exp(-values))


def matmul(left, right):
    return jnp.dot(left, right, preferred_element_type=jnp.float32)


def matmul_nt(left, right):
    return lax.dot_general(
        left, right, (((1,), (1,)), ((), ())), preferred_element_type=jnp.float32
    )


def block_lanes(block):
    return slice(block * LANES, (block + 1) * LANES)


def fill_onehot(onehot):
    tap = lax.broadcasted_iota(jnp.int32, (32, LANES), 0)
    at = lane_index((32, LANES))
    tap_x = jnp.where(tap >= 9, 1, 0) + jnp.where(tap >= 18, 1, 0)
    within = tap - 9 * tap_x
    tap_y = jnp.where(within >= 3, 1, 0) + jnp.where(within >= 6, 1, 0)
    tap_z = within - 3 * tap_y
    twice_x = (at >> 5) + 1 - tap_x
    twice_z = ((at >> 3) & 3) + 1 - tap_z
    twice_y = (at & 7) + 1 - tap_y
    code = (twice_x + 2) * 256 + (twice_y + 2) * 16 + (twice_z + 2)
    code = jnp.where(tap < 27, code, -1)
    for block in range(BLOCKS):
        src_x, src_y, src_z = (block // 15, block // 3 % 5, block % 3)
        wanted = (2 * src_x + 2) * 256 + (2 * src_y + 2) * 16 + (2 * src_z + 2)
        onehot[:, block_lanes(block)] = jnp.where(code == wanted, 1.0, 0.0).astype(jnp.bfloat16)
        if block % 5 == 4:
            yield


def fill_three(w_three, m_three, build):
    build[...] = jnp.zeros_like(build)
    for tap in range(27):
        tap_x, tap_y, tap_z = (tap // 9, tap // 3 % 3, tap % 3)
        par_y, off_y = (int(tap_y != 1), int(tap_y == 0))
        par_z, off_z = (int(tap_z != 1), int(tap_z == 0))
        row = par_y * 32 + par_z * 16
        lane = off_y * 64 + off_z * 32
        places = (((1, 1),), ((0, 0), (2, 1)), ((1, 0),))[tap_x]
        values = w_three[tap].astype(jnp.float32)
        for plane, off_x in places:
            build[
                plane * 64 + row : plane * 64 + row + 16,
                off_x * 128 + lane : off_x * 128 + lane + 32,
            ] = values
    m_three[...] = build[...].astype(jnp.bfloat16)


def fill_four(w_four, onehot, m_four, m_back):
    spread = matmul(w_four[...], onehot[:27, :])
    columns = jnp.concatenate([spread[:, block_lanes(block)] for block in range(BLOCKS)], 0)
    m_back[...] = columns.astype(jnp.bfloat16)
    m_four[...] = columns.T.astype(jnp.bfloat16)


def coarse_tile(rows):
    return jnp.concatenate([rows, next_lane(rows)], 0).astype(jnp.bfloat16)


def window_of(cells, b, last):
    after = b if last else b + 1
    return jnp.concatenate([cells[0, b], cells[0, after], cells[1, b], cells[1, after]], 0)


def field_pair(elec, temp, adj, adj_grad, scale, res_x, rows, lanes):
    energy = 0.0
    thermal = 0.0
    for comp in range(3):
        field = elec[comp, res_x, rows, lanes].astype(jnp.float32)
        energy = energy + field * field
        thermal = thermal + temp[comp, res_x, rows, lanes].astype(jnp.float32) * adj_grad[
            comp, res_x, rows, lanes
        ].astype(jnp.float32)
    gain = (scale * 3.0 * (1.0 - 0.001)) * (energy * adj[res_x, rows, lanes].astype(jnp.float32))
    return (gain, (scale * 2.0 * (1.0 - 0.01)) * thermal)


class Group:
    def __init__(self, pairs, first, matrices, scratch, top):
        self.pairs, self.first, self.top = (pairs, first, top)
        self.m_three, self.m_four, self.m_back = matrices
        self.cells, self.windows, self.slope, self.g_fine, self.g_pre = scratch
        self.hidden_rows = 4 * pairs + 1

    def window(self, b):
        return window_of(self.cells, self.first + b, self.top and b == 2 * self.pairs)

    def forward(self):
        coarse_rows = 2 * self.pairs + 1
        self.g_pre_blank()
        for b in range(coarse_rows):
            halo = b == coarse_rows - 1
            if halo:
                matrix = jnp.concatenate(
                    [self.m_three[plane * 64 : plane * 64 + 32, :] for plane in range(3)], 0
                )
                part = matmul(matrix, self.window(b))
            elif b % 2 == 0:
                both = matmul(
                    self.m_three[...],
                    jnp.concatenate([self.window(b), self.window(b + 1)], 1),
                )
                part = both[:, :LANES]
            else:
                part = both[:, LANES:]
            per_plane = 32 if halo else 64
            for plane in range(3):
                pre = part[plane * per_plane : (plane + 1) * per_plane]
                sigma = logistic(pre)
                hidden = pre * sigma
                self.slope[plane * 64 : plane * 64 + per_plane, block_lanes(b)] = sigma * (
                    1.0 + pre * (1.0 - sigma)
                )
                for par in range(per_plane // 32):
                    row = 2 * b + par
                    two = hidden[par * 32 : par * 32 + 32]
                    tall = jnp.concatenate([two, next_lane(two[:16])], 0).astype(jnp.bfloat16)
                    for pair in range(self.pairs):
                        within = row - 4 * pair
                        if 0 <= within < PAIR_ROWS:
                            start = (plane * PAIR_ROWS + within) * 48
                            self.windows[start : start + 48, block_lanes(pair)] = tall
                yield

    def g_pre_blank(self):
        for plane in range(3):
            self.g_pre[plane * 64 + 32 : plane * 64 + 64, block_lanes(2 * self.pairs)] = jnp.zeros(
                (32, LANES), jnp.bfloat16
            )

    def backward(self, field_terms, density, sums_from, sums_to):
        logits = matmul(self.m_four[...], self.windows[...])
        for res_x in range(4):
            for res_z in range(4):
                at = (res_x * 4 + res_z) * 8
                lanes = block_lanes(res_z)
                d = logistic(
                    jnp.concatenate(
                        [logits[at : at + 8, block_lanes(pair)] for pair in range(self.pairs)], 0
                    )
                )
                density[res_x, :, lanes] = d
                gain, loss = field_terms(res_x, lanes)
                g = d * d * (1.0 - d) * (gain * d - loss)
                for pair in range(self.pairs):
                    self.g_fine[at : at + 8, block_lanes(pair)] = g[8 * pair : 8 * pair + 8]
            yield
        g_out = self.g_fine[...].astype(jnp.bfloat16)
        for plane in range(3):
            span = slice(plane * 240, plane * 240 + 240)
            spread = matmul(self.m_back[span, :], g_out)
            for row in range(self.hidden_rows):
                tall = 0.0
                for pair in range(self.pairs):
                    within = row - 4 * pair
                    if 0 <= within < PAIR_ROWS:
                        tall = tall + spread[within * 48 : within * 48 + 48, block_lanes(pair)]
                both = jnp.concatenate([tall[:16] + previous_lane(tall[32:]), tall[16:32]], 0)
                at = plane * 64 + row % 2 * 32
                lanes = block_lanes(row // 2)
                if plane == 1 and 0 < row < self.hidden_rows - 1:
                    both = both.astype(jnp.bfloat16).astype(jnp.float32)
                self.g_pre[at : at + 32, lanes] = (
                    both * self.slope[at : at + 32, lanes]
                ).astype(jnp.bfloat16)
            yield
            sums_to[1][span, :] = sums_from[1][span, :] + matmul_nt(self.windows[span, :], g_out)
            yield
        wide = jnp.concatenate([self.window(b) for b in range(2 * self.pairs + 1)], 1)
        sums_to[0][...] = sums_from[0][...] + matmul_nt(self.g_pre[...], wide)
        yield


def run(*streams):
    live = list(streams)
    while live:
        for stream in list(live):
            if next(stream, live) is live:
                live.remove(stream)


def chain(*streams):
    for stream in streams:
        yield from stream


def interior_kernel(scale, near_far, w_three, w_four, elec, temp, adj, adj_grad, *refs):
    (density, sum_three, sum_four, m_three, m_four, m_back) = refs[:6]
    (onehot, last_gain, last_loss, last_cells) = refs[6:10]
    (build, flat, cells, elec_v, temp_v, adj_v, adj_grad_v, dense) = refs[10:18]
    sems = refs[18]
    held = near_far.shape[2]
    groups = held // 4
    scratch = refs[19:]
    sets = [scratch[4 * i : 4 * i + 4] for i in range(groups)]
    copies = []
    for q in range(groups):
        rows = pl.ds(16 * q, 16)
        copies.append(
            [
                pltpu.make_async_copy(far.at[:, :, rows, :], here.at[:, :, rows, :], sems.at[q, i])
                for i, (far, here) in enumerate(
                    ((elec, elec_v), (temp, temp_v), (adj_grad, adj_grad_v))
                )
            ]
            + [pltpu.make_async_copy(adj.at[:, rows, :], adj_v.at[:, rows, :], sems.at[q, 3])]
        )
        for copy in copies[q]:
            copy.start()
    outs = []

    def field_terms_at(first, count):
        rows = slice(first, first + count)
        return lambda res_x, lanes: field_pair(
            elec_v, temp_v, adj_v, adj_grad_v, scale, res_x, rows, lanes
        )

    def load_cells():
        for plane in range(2):
            flat[plane] = near_far[plane].astype(jnp.float32).reshape(flat.shape[1:])
            yield
        for b in range(held):
            for plane in range(2):
                tile = coarse_tile(flat[plane, pl.ds(b, 32, held), :])
                cells[plane, b] = tile
                if b >= held - 2:
                    last_cells[plane, b - held + 2] = tile
            if b % 2 == 1:
                yield

    def zero_sums():
        sum_three[...] = jnp.zeros_like(sum_three)
        sum_four[...] = jnp.zeros_like(sum_four)
        yield

    matrices = (m_three, m_four, m_back)
    sums = (sum_three, sum_four)
    parts = []
    for q in range(groups):
        pairs = 2 if q < groups - 1 else 1
        parts.append(Group(pairs, 4 * q, matrices, (cells,) + tuple(sets[q]), False))

    def second(q):
        for copy in copies[q]:
            copy.wait()
        count = 8 * parts[q].pairs
        rows = slice(16 * q, 16 * q + count)
        yield from parts[q].backward(
            field_terms_at(16 * q, count), dense.at[:, rows, :], sums, sums
        )
        out = pltpu.make_async_copy(
            dense.at[:, pl.ds(16 * q, count), :],
            density.at[:, pl.ds(16 * q, count), :],
            sems.at[q, 4],
        )
        out.start()
        outs.append(out)

    def last_fields():
        terms = field_terms_at(16 * groups - 8, 8)
        for res_x in range(4):
            for res_z in range(4):
                lanes = block_lanes(res_z)
                gain, loss = terms(res_x, lanes)
                last_gain[res_x, :, lanes] = gain
                last_loss[res_x, :, lanes] = loss
            yield

    fill_three(w_three, m_three, build)
    run(fill_onehot(onehot), load_cells(), zero_sums())
    fill_four(w_four, onehot, m_four, m_back)
    run(parts[0].forward())
    for q in range(groups - 1):
        run(second(q), parts[q + 1].forward())
    run(second(groups - 1), last_fields())
    for out in outs:
        out.wait()


def rim_kernel(place, rim, m_three, m_four, m_back, sum_three_in, sum_four_in, *refs):
    (onehot, last_gain, last_loss, last_cells, _) = refs[:5]
    (density, mine, other) = refs[5:8]
    (packed, sum_three, sum_four, cells, dense, sem) = refs[8:14]
    scratch = refs[14:]
    fine_rows = density.shape[1]
    for plane in range(2):
        for b in range(2):
            cells[plane, b] = last_cells[plane, b]
        cells[plane, 2] = coarse_tile(rim[plane].astype(jnp.float32))
    part = Group(1, 0, (m_three, m_four, m_back), (cells,) + tuple(scratch), True)
    run(part.forward())
    run(
        part.backward(
            lambda res_x, lanes: (last_gain[res_x, :, lanes], last_loss[res_x, :, lanes]),
            dense,
            (sum_three_in, sum_four_in),
            (sum_three, sum_four),
        )
    )
    out = pltpu.make_async_copy(dense, density.at[:, pl.ds(fine_rows - 8, 8), :], sem)
    out.start()
    by_tap = (
        sum_three[64:128, 128:],
        sum_three[:64, :128] + sum_three[128:, 128:],
        sum_three[64:128, :128],
    )
    for tap_x in range(3):
        part = by_tap[tap_x]
        packed[32 * tap_x : 32 * tap_x + 16, :] = part[48:64]
        lanes = lane_index((16, LANES))
        mixed = jnp.where(
            lanes < 64,
            part[16:32],
            jnp.where(lanes < 96, part[32:48], pltpu.roll(part[32:48], 96, 1)),
        )
        packed[32 * tap_x + 16 : 32 * tap_x + 32, :] = mixed
        packed[96:112, 32 * tap_x : 32 * tap_x + 32] = part[:16, :32]
    rest = jnp.concatenate(
        [sum_four[16 * block : 16 * block + 16, :] for block in range(BLOCKS)], 1
    )
    pieces = []
    for _ in range(3):
        piece = rest.astype(jnp.bfloat16)
        pieces.append(piece)
        rest = rest - piece.astype(jnp.float32)
    folded = matmul_nt(jnp.concatenate(pieces, 0), onehot[...])
    packed[96:112, 96:128] = folded[:16] + folded[16:32] + folded[32:48]
    which = place[0]
    half = mine.shape[0]
    mine[...] = packed[pl.ds(pl.multiple_of(which * half, 8), half), :]
    other[...] = packed[pl.ds(pl.multiple_of((1 - which) * half, 8), half), :]
    out.wait()


def unpack_kernel(part, mine, other, grad_three, grad_four):
    low = part[0] == 0
    whole = jnp.concatenate(
        [
            jnp.where(low, mine[...], other[...]),
            jnp.where(low, other[...], mine[...]),
        ],
        0,
    )
    for tap in range(27):
        row, lane = slot_of(tap)
        grad_three[tap] = whole[row : row + 16, lane : lane + 32]
    grad_four[...] = whole[96:112, 96:123]


def exchanged(value, bit_x, bit_y):
    size_x, size_y = (lax.axis_size("gx"), lax.axis_size("gy"))
    pairs = [
        (i * size_y + j, (i ^ bit_x) * size_y + (j ^ bit_y))
        for i in range(size_x)
        for j in range(size_y)
    ]
    return lax.ppermute(value, ("gx", "gy"), pairs)


def parity_of(index):
    total = index
    for shift in (1, 2, 3, 4, 5, 6, 7):
        total = total ^ (index >> shift)
    return total & 1


def sum_everywhere(mine, other, part):
    size_x, size_y = (lax.axis_size("gx"), lax.axis_size("gy"))
    assert size_x & (size_x - 1) == 0 and size_y & (size_y - 1) == 0
    assert 2 <= size_x <= 256 and size_y <= 256
    mine = mine + exchanged(other, 1, 0)
    bit = 2
    while bit < size_x:
        mine = mine + exchanged(mine, bit + 1, 0)
        bit = bit * 2
    bit = 1
    while bit < size_y:
        mine = mine + exchanged(mine, 1, bit)
        bit = bit * 2
    other = exchanged(mine, 1, 0)
    spec = pl.BlockSpec(memory_space=pltpu.VMEM)
    grad_three, grad_four = pl.pallas_call(
        unpack_kernel,
        out_shape=(
            jax.ShapeDtypeStruct((27, 16, 32), jnp.float32),
            jax.ShapeDtypeStruct((16, 27), jnp.float32),
        ),
        in_specs=[pl.BlockSpec(memory_space=pltpu.SMEM), spec, spec],
        out_specs=(spec, spec),
        compiler_params=pltpu.CompilerParams(vmem_limit_bytes=2 * MIB),
        name="unpack",
    )(part, mine, other)
    return (grad_three, grad_four.T)


def shards(coarse, w_three, w_four, elec_field, temp_grad, adjoint, adjoint_grad):
    groups_x, groups_y = (lax.axis_size("gx"), lax.axis_size("gy"))
    chan_in, count_a, held, depth = coarse.shape
    fine_x, fine_y, fine_z = adjoint.shape
    assert (fine_x, fine_y, fine_z) == (4, 4 * held, 4 * LANES)
    assert depth == LANES and chan_in == 32 and held % 4 == 0 and count_a == groups_x
    cells = fine_x * groups_x * fine_y * groups_y * fine_z
    scale = 8.0 / math.sqrt(cells)
    at_x = lax.axis_index("gx").astype(jnp.int32)
    inside = at_x + 1 < count_a
    near = lax.dynamic_index_in_dim(coarse, at_x, 1, keepdims=False)
    far = lax.dynamic_index_in_dim(coarse, jnp.minimum(at_x + 1, count_a - 1), 1, keepdims=False)
    near_far = jnp.stack([near, jnp.where(inside, far, jnp.zeros_like(far))])
    rim = lax.ppermute(near_far[:, :, 0, :], "gy", [(i + 1, i) for i in range(groups_y - 1)])
    part = parity_of(lax.axis_index("gx")) ^ parity_of(lax.axis_index("gy"))
    part = part.astype(jnp.int32).reshape(1)
    groups = held // 4

    def shape(dims, dtype):
        return jax.ShapeDtypeStruct(dims, dtype)

    def in_hbm(value):
        return pltpu.with_memory_space_constraint(value, pltpu.HBM)

    def group_scratch(pairs):
        return (
            pltpu.VMEM((WINDOW, pairs * LANES), jnp.bfloat16),
            pltpu.VMEM((192, (2 * pairs + 1) * LANES), jnp.float32),
            pltpu.VMEM((LANES, pairs * LANES), jnp.float32),
            pltpu.VMEM((192, (2 * pairs + 1) * LANES), jnp.bfloat16),
        )

    in_vmem = pl.BlockSpec(memory_space=pltpu.VMEM)
    anywhere = pl.BlockSpec(memory_space=pl.ANY)
    hbm = pl.BlockSpec(memory_space=pltpu.HBM)
    in_smem = pl.BlockSpec(memory_space=pltpu.SMEM)
    dense = shape(adjoint.shape, jnp.float32)
    handed = (
        shape((192, 256), jnp.float32),
        shape((WINDOW, LANES), jnp.float32),
        shape((192, 256), jnp.bfloat16),
        shape((LANES, WINDOW), jnp.bfloat16),
        shape((WINDOW, LANES), jnp.bfloat16),
        shape((32, BLOCKS * LANES), jnp.bfloat16),
        shape((4, 8, fine_z), jnp.float32),
        shape((4, 8, fine_z), jnp.float32),
        shape((2, 2, 64, LANES), jnp.bfloat16),
    )
    half = shape((56, LANES), jnp.float32)
    per_group = ()
    for q in range(groups):
        per_group = per_group + group_scratch(2 if q < groups - 1 else 1)
    density, sum_three, sum_four, m_three, m_four, m_back, *rest = pl.pallas_call(
        lambda *refs: interior_kernel(scale, *refs),
        out_shape=(dense,) + handed,
        in_specs=[in_vmem] * 3 + [hbm] * 4,
        out_specs=(anywhere,) + (in_vmem,) * len(handed),
        scratch_shapes=(
            pltpu.VMEM((192, 256), jnp.float32),
            pltpu.VMEM((2, chan_in * held, LANES), jnp.float32),
            pltpu.VMEM((2, held, 64, LANES), jnp.bfloat16),
            pltpu.VMEM(elec_field.shape, jnp.bfloat16),
            pltpu.VMEM(temp_grad.shape, jnp.bfloat16),
            pltpu.VMEM(adjoint.shape, jnp.bfloat16),
            pltpu.VMEM(adjoint_grad.shape, jnp.bfloat16),
            pltpu.VMEM(adjoint.shape, jnp.float32),
            pltpu.SemaphoreType.DMA((groups, 5)),
        )
        + per_group,
        compiler_params=pltpu.CompilerParams(vmem_limit_bytes=32 * MIB),
        cost_estimate=pl.CostEstimate(
            flops=2000000000, bytes_accessed=4000000, transcendentals=2000000
        ),
        name="interior",
    )(
        near_far,
        w_three,
        w_four.T,
        in_hbm(elec_field),
        in_hbm(temp_grad),
        in_hbm(adjoint),
        in_hbm(adjoint_grad),
    )
    density, mine, other = pl.pallas_call(
        rim_kernel,
        out_shape=(dense, half, half),
        in_specs=[in_smem] + [in_vmem] * (1 + len(handed)) + [anywhere],
        out_specs=(anywhere, in_vmem, in_vmem),
        scratch_shapes=(
            pltpu.VMEM((112, LANES), jnp.float32),
            pltpu.VMEM((192, 256), jnp.float32),
            pltpu.VMEM((WINDOW, LANES), jnp.float32),
            pltpu.VMEM((2, 3, 64, LANES), jnp.bfloat16),
            pltpu.VMEM((4, 8, fine_z), jnp.float32),
            pltpu.SemaphoreType.DMA(()),
        )
        + group_scratch(1),
        input_output_aliases={2 + len(handed): 0},
        compiler_params=pltpu.CompilerParams(vmem_limit_bytes=16 * MIB),
        cost_estimate=pl.CostEstimate(
            flops=400000000, bytes_accessed=2000000, transcendentals=400000
        ),
        name="rim",
    )(part, rim, m_three, m_four, m_back, sum_three, sum_four, *rest, density)
    grad_three, grad_four = sum_everywhere(mine, other, part)
    return (density, grad_three, grad_four)


def solution(mesh):
    return jax.shard_map(
        shards,
        mesh=mesh,
        in_specs=(
            P(None, None, "gy", None),
            P(),
            P(),
            P(None, "gx", "gy", None),
            P(None, "gx", "gy", None),
            P("gx", "gy", None),
            P(None, "gx", "gy", None),
        ),
        out_specs=(P("gx", "gy", None), P(), P()),
        check_vma=False,
    )
```

time: 34.4 us -> 31.3 us (0.910)
  Pallas kernels: 10.8 us -> 7.31 us
    pallas_call x2, Pallas kernels: 10 us -> 6.51 us  [the longest x1 5.03 us: shards(): pl.pallas_call(lambda *refs: interior_kernel(scale, *refs), out_shape=(de...]
    unnamed x6 -> x4, local copies, waits for them, and re-layouts: 0.64 us -> 0.7 us
  transfers between devices with their start and end apart: 7 -> 7, of which waited for: 6 -> 6; matrix products, arithmetic and copies ran while one was open for 0% -> 1% of each run, Pallas kernels for 22% -> 16%
where the time goes in v3:
time: 31.3 us; the launch traced here: 31 us
  starting transfers between devices  13 us (42%)
  waiting for transfers between devices  7.96 us (25%)
  Pallas kernels  7.31 us (23%)
  local copies, waits for them, and re-layouts  1.88 us (6%)
  between operations  0.75 us (2%)
    ppermute x6, starting transfers between devices, exchanged(): return lax.ppermute(value, ('gx', 'gy'), pairs)  11.7 us
    ppermute x6, waiting for transfers between devices, exchanged(): return lax.ppermute(value, ('gx', 'gy'), pairs)  7.95 us
    pallas_call x1, Pallas kernels, shards(): pl.pallas_call(lambda *refs: interior_kernel(scale, *refs), out_shape=(de...  5.03 us
    pallas_call x1, Pallas kernels, shards(): pl.pallas_call(rim_kernel, out_shape=(dense, half, half), in_specs=[in_sm...  1.49 us
    ppermute x1, starting transfers between devices, shards(): lax.ppermute(near_far[:, :, 0, :], 'gy', [(i + 1, i) for i in range(group...  1.29 us
    dynamic_slice x1, local copies, waits for them, and re-layouts, shards(): near = lax.dynamic_index_in_dim(coarse, at_x, 1, keepdims=False)  1 us
    pallas_call x1, Pallas kernels, sum_everywhere(): pl.pallas_call(unpack_kernel, out_shape=(jax.ShapeDtypeStruct((27, 16, 32...  0.8 us
    unnamed x4, local copies, waits for them, and re-layouts  0.7 us
  transfers between devices with their start and end apart: 7, of which 6 were waited for; matrix products, arithmetic and copies ran while one was open for 1% of the time, Pallas kernels for 16%

profile of v3, /device:TPU:0, one launch (start us, length us, event | category | flops | bytes accessed | tf_op | source)
XLA Modules:
  0.0 31.0 jit_solution(17296074525609600410)
XLA Ops:
  0.6 1.0 %constant_dynamic-slice_fusion.1 = (bf16[32,1,16,128]{3,2,1,0:T(8,128)(2,1)S(1)}, bf16[32,1,16,128]{3,2,1,0:T(8,128)(2,1)S(1)}) fusion(bf16[32,8,16,128]{3,2,1,0:T(8,128)(2,1)} %param.7, s32[]{:T(128)S(6)} %select_n.25, s32[]{:T(128)S(6)} %select_n.27), kind=kLoop, calls=%fused_computation.9 | loop fusion | bytes 524296 | tf_op jit(solution)/shard_map/jit(dynamic_index_in_dim)/dynamic_slice | solution.py:456
  1.6 0.1 fusion
  1.7 1.3 %collective-permute-start = (bf16[2,32,128]{2,1,0:T(8,128)(2,1)S(1)}, bf16[2,32,128]{2,1,0:T(8,128)(2,1)S(1)}, u32[]{:S(2)}, u32[]{:S(2)}) collective-permute-start(bf16[2,32,128]{2,1,0:T(8,128)(2,1)S(1)} %fusion.2), channel_id=1, source_target_pairs={{1,0},{2,1},{3,2},{5,4},{6,5},{7,6},{9,8},{10,9},{11,10},{13,12},{... | collective-permute-start | bytes 49160 | tf_op jit(solution)/shard_map/ppermute | solution.py:459
  3.1 0.0 copy-start
  3.1 0.0 copy-start.1
  3.1 0.2 copy.13.refs_0_
  3.3 0.7 %copy-done = bf16[27,16,32]{2,1,0:T(8,128)(2,1)S(1)} copy-done((bf16[27,16,32]{2,1,0:T(8,128)(2,1)S(1)}, bf16[27,16,32]{2,1,0:T(8,128)(2,1)}, u32[]{:S(2)}) %copy-start) | copy-done | bytes 27672
  4.0 0.0 copy-done.1
  4.0 5.0 %interior.1 = (f32[4,64,512]{2,1,0:T(8,128)}, f32[192,256]{1,0:T(8,128)S(1)}, f32[720,128]{1,0:T(8,128)S(1)}, bf16[192,256]{1,0:T(8,128)(2,1)S(1)}, bf16[128,720...) custom-call(bf16[2,32,16,128]{3,2,1,0:T(8,128)(2,1)S(1)} %copy.13.re, ...), custom_call_target="tpu_custom_call" | custom-call | flops 2000000000 | bytes 4000000 | tf_op jit(solution)/shard_map/interior/pallas_call | solution.py:498
  9.0 0.0 collective-permute-done.rim
  9.0 1.5 %rim.1 = (f32[4,64,512]{2,1,0:T(8,128)}, f32[56,128]{1,0:T(8,128)S(1)}, f32[56,128]{1,0:T(8,128)S(1)}) custom-call(s32[1]{0:T(128)} %bitcast.place.part, bf16[2,32,128]{2,1,0:T(8,128)(2,1)S(1)} %collective-permute-done.rim, bf16[192,256]{1,0:T(8,128)(2,1)S(1)} %get-tuple-element.18.m_three, ...), custom_call_target="tpu_custom_call", output_to_operand_aliasing={{0}: (11, {})} | custom-call | flops 400000000 | bytes 2000000 | tf_op jit(solution)/shard_map/rim/pallas_call | solution.py:529
  10.5 0.6 %collective-permute-start.1 = (f32[56,128]{1,0:T(8,128)S(1)}, f32[56,128]{1,0:T(8,128)S(1)}, u32[]{:S(2)}, u32[]{:S(2)}) collective-permute-start(f32[56,128]{1,0:T(8,128)S(1)} %get-tuple-element.30), channel_id=1, source_target_pairs={{0,4},{1,5},{2,6},{3,7},{4,0},{5,1},{6,2},{7,3},{8,12},{9,13},{10,... | collective-permute-start | bytes 86024 | tf_op jit(solution)/shard_map/ppermute | solution.py:407
  11.1 0.9 %collective-permute-done.1 = f32[56,128]{1,0:T(8,128)S(1)} collective-permute-done((f32[56,128]{1,0:T(8,128)S(1)}, f32[56,128]{1,0:T(8,128)S(1)}, u32[]{:S(2)}, u32[]{:S(2)}) %collective-permute-start.1) | collective-permute-done | bytes 28704 | tf_op jit(solution)/shard_map/ppermute | solution.py:407
  11.9 2.7 %collective-permute-start.2 = (f32[56,128]{1,0:T(8,128)S(1)}, f32[56,128]{1,0:T(8,128)S(1)}, u32[]{:S(2)}, u32[]{:S(2)}) collective-permute-start(f32[56,128]{1,0:T(8,128)S(1)} %add.29), channel_id=1, source_target_pairs={{0,12},{1,13},{2,14},{3,15},{4,8},{5,9},{6,10},{7,11},{8,4},{9,5},... | collective-permute-start | bytes 86024 | tf_op jit(solution)/shard_map/ppermute | solution.py:407
  14.6 1.6 %collective-permute-done.2 = f32[56,128]{1,0:T(8,128)S(1)} collective-permute-done((f32[56,128]{1,0:T(8,128)S(1)}, f32[56,128]{1,0:T(8,128)S(1)}, u32[]{:S(2)}, u32[]{:S(2)}) %collective-permute-start.2) | collective-permute-done | bytes 28704 | tf_op jit(solution)/shard_map/ppermute | solution.py:407
  16.2 2.8 %collective-permute-start.3 = (f32[56,128]{1,0:T(8,128)S(1)}, f32[56,128]{1,0:T(8,128)S(1)}, u32[]{:S(2)}, u32[]{:S(2)}) collective-permute-start(f32[56,128]{1,0:T(8,128)S(1)} %add.30), channel_id=1, source_target_pairs={{0,20},{1,21},{2,22},{3,23},{4,16},{5,17},{6,18},{7,19},{8,28},{9,... | collective-permute-start | bytes 86024 | tf_op jit(solution)/shard_map/ppermute | solution.py:407
  18.9 1.6 %collective-permute-done.3 = f32[56,128]{1,0:T(8,128)S(1)} collective-permute-done((f32[56,128]{1,0:T(8,128)S(1)}, f32[56,128]{1,0:T(8,128)S(1)}, u32[]{:S(2)}, u32[]{:S(2)}) %collective-permute-start.3) | collective-permute-done | bytes 28704 | tf_op jit(solution)/shard_map/ppermute | solution.py:407
  20.5 2.6 %collective-permute-start.4 = (f32[56,128]{1,0:T(8,128)S(1)}, f32[56,128]{1,0:T(8,128)S(1)}, u32[]{:S(2)}, u32[]{:S(2)}) collective-permute-start(f32[56,128]{1,0:T(8,128)S(1)} %add.31), channel_id=1, source_target_pairs={{0,5},{1,4},{2,7},{3,6},{4,1},{5,0},{6,3},{7,2},{8,13},{9,12},{10,... | collective-permute-start | bytes 86024 | tf_op jit(solution)/shard_map/ppermute | solution.py:407
  23.1 1.6 %collective-permute-done.4 = f32[56,128]{1,0:T(8,128)S(1)} collective-permute-done((f32[56,128]{1,0:T(8,128)S(1)}, f32[56,128]{1,0:T(8,128)S(1)}, u32[]{:S(2)}, u32[]{:S(2)}) %collective-permute-start.4) | collective-permute-done | bytes 28704 | tf_op jit(solution)/shard_map/ppermute | solution.py:407
  24.7 2.8 %collective-permute-start.5 = (f32[56,128]{1,0:T(8,128)S(1)}, f32[56,128]{1,0:T(8,128)S(1)}, u32[]{:S(2)}, u32[]{:S(2)}) collective-permute-start(f32[56,128]{1,0:T(8,128)S(1)} %add.32), channel_id=1, source_target_pairs={{0,6},{1,7},{2,4},{3,5},{4,2},{5,3},{6,0},{7,1},{8,14},{9,15},{10,... | collective-permute-start | bytes 86024 | tf_op jit(solution)/shard_map/ppermute | solution.py:407
  27.4 1.6 %collective-permute-done.5 = f32[56,128]{1,0:T(8,128)S(1)} collective-permute-done((f32[56,128]{1,0:T(8,128)S(1)}, f32[56,128]{1,0:T(8,128)S(1)}, u32[]{:S(2)}, u32[]{:S(2)}) %collective-permute-start.5) | collective-permute-done | bytes 28704 | tf_op jit(solution)/shard_map/ppermute | solution.py:407
  29.0 0.3 %collective-permute-start.6 = (f32[56,128]{1,0:T(8,128)S(1)}, f32[56,128]{1,0:T(8,128)S(1)}, u32[]{:S(2)}, u32[]{:S(2)}) collective-permute-start(f32[56,128]{1,0:T(8,128)S(1)} %add.33.mine), channel_id=1, source_target_pairs={{0,4},{1,5},{2,6},{3,7},{4,0},{5,1},{6,2},{7,3},{8,12},{9,13},{10,... | collective-permute-start | bytes 86024 | tf_op jit(solution)/shard_map/ppermute | solution.py:407
  29.3 0.9 %collective-permute-done.6.other = f32[56,128]{1,0:T(8,128)S(1)} collective-permute-done((f32[56,128]{1,0:T(8,128)S(1)}, f32[56,128]{1,0:T(8,128)S(1)}, u32[]{:S(2)}, u32[]{:S(2)}) %collective-permute-start.6) | collective-permute-done | bytes 28704 | tf_op jit(solution)/shard_map/ppermute | solution.py:407
  30.2 0.8 %unpack.1 = (f32[27,16,32]{2,1,0:T(8,128)}, f32[16,27]{1,0:T(8,128)}) custom-call(s32[1]{0:T(128)} %bitcast.place.part, f32[56,128]{1,0:T(8,128)S(1)} %add.33.mine, f32[56,128]{1,0:T(8,128)S(1)} %collective-permute-done.6.other), custom_call_target="tpu_custom_call" | custom-call | tf_op jit(solution)/shard_map/unpack/pallas_call | solution.py:432
  (7 shorter events, 0.1 us)
Async XLA Ops:
  1.7 7.3 %collective-permute-start = (bf16[2,32,128]{2,1,0:T(8,128)(2,1)S(1)}, bf16[2,32,128]{2,1,0:T(8,128)(2,1)S(1)}, u32[]{:S(2)}, u32[]{:S(2)}) collective-permute-start(bf16[2,32,128]{2,1,0:T(8,128)(2,1)S(1)} %fusion.2), channel_id=1, source_target_pairs={{1,0},{2,1},{3,2},{5,4},{6,5},{7,6},{9,8},{10,9},{11,10},{13,12},{... | collective-permute-start | bytes 49160 | tf_op jit(solution)/shard_map/ppermute | solution.py:459
  3.1 0.9 %copy-start = (bf16[27,16,32]{2,1,0:T(8,128)(2,1)S(1)}, bf16[27,16,32]{2,1,0:T(8,128)(2,1)}, u32[]{:S(2)}) copy-start(bf16[27,16,32]{2,1,0:T(8,128)(2,1)} %refs_1_.1) | copy-start | bytes 82948
  3.1 0.9 %copy-start.1 = (bf16[27,16]{0,1:T(8,128)(2,1)S(1)}, bf16[27,16]{0,1:T(8,128)(2,1)}, u32[]{:S(2)}) copy-start(bf16[27,16]{0,1:T(8,128)(2,1)} %param.9) | copy-start | bytes 2596
  10.5 1.4 %collective-permute-start.1 = (f32[56,128]{1,0:T(8,128)S(1)}, f32[56,128]{1,0:T(8,128)S(1)}, u32[]{:S(2)}, u32[]{:S(2)}) collective-permute-start(f32[56,128]{1,0:T(8,128)S(1)} %get-tuple-element.30), channel_id=1, source_target_pairs={{0,4},{1,5},{2,6},{3,7},{4,0},{5,1},{6,2},{7,3},{8,12},{9,13},{10,... | collective-permute-start | bytes 86024 | tf_op jit(solution)/shard_map/ppermute | solution.py:407
  11.9 4.2 %collective-permute-start.2 = (f32[56,128]{1,0:T(8,128)S(1)}, f32[56,128]{1,0:T(8,128)S(1)}, u32[]{:S(2)}, u32[]{:S(2)}) collective-permute-start(f32[56,128]{1,0:T(8,128)S(1)} %add.29), channel_id=1, source_target_pairs={{0,12},{1,13},{2,14},{3,15},{4,8},{5,9},{6,10},{7,11},{8,4},{9,5},... | collective-permute-start | bytes 86024 | tf_op jit(solution)/shard_map/ppermute | solution.py:407
  16.2 4.3 %collective-permute-start.3 = (f32[56,128]{1,0:T(8,128)S(1)}, f32[56,128]{1,0:T(8,128)S(1)}, u32[]{:S(2)}, u32[]{:S(2)}) collective-permute-start(f32[56,128]{1,0:T(8,128)S(1)} %add.30), channel_id=1, source_target_pairs={{0,20},{1,21},{2,22},{3,23},{4,16},{5,17},{6,18},{7,19},{8,28},{9,... | collective-permute-start | bytes 86024 | tf_op jit(solution)/shard_map/ppermute | solution.py:407
  20.5 4.1 %collective-permute-start.4 = (f32[56,128]{1,0:T(8,128)S(1)}, f32[56,128]{1,0:T(8,128)S(1)}, u32[]{:S(2)}, u32[]{:S(2)}) collective-permute-start(f32[56,128]{1,0:T(8,128)S(1)} %add.31), channel_id=1, source_target_pairs={{0,5},{1,4},{2,7},{3,6},{4,1},{5,0},{6,3},{7,2},{8,13},{9,12},{10,... | collective-permute-start | bytes 86024 | tf_op jit(solution)/shard_map/ppermute | solution.py:407
  24.7 4.3 %collective-permute-start.5 = (f32[56,128]{1,0:T(8,128)S(1)}, f32[56,128]{1,0:T(8,128)S(1)}, u32[]{:S(2)}, u32[]{:S(2)}) collective-permute-start(f32[56,128]{1,0:T(8,128)S(1)} %add.32), channel_id=1, source_target_pairs={{0,6},{1,7},{2,4},{3,5},{4,2},{5,3},{6,0},{7,1},{8,14},{9,15},{10,... | collective-permute-start | bytes 86024 | tf_op jit(solution)/shard_map/ppermute | solution.py:407
  29.0 1.2 %collective-permute-start.6 = (f32[56,128]{1,0:T(8,128)S(1)}, f32[56,128]{1,0:T(8,128)S(1)}, u32[]{:S(2)}, u32[]{:S(2)}) collective-permute-start(f32[56,128]{1,0:T(8,128)S(1)} %add.33.mine), channel_id=1, source_target_pairs={{0,4},{1,5},{2,6},{3,7},{4,0},{5,1},{6,2},{7,3},{8,12},{9,13},{10,... | collective-permute-start | bytes 86024 | tf_op jit(solution)/shard_map/ppermute | solution.py:407

commit v4 on v3

--- a/solution.py
+++ b/solution.py
@@ -11,6 +11,7 @@
 BLOCKS = 3 * PAIR_ROWS * 3
 WINDOW = BLOCKS * 16
 LANES = 128
+STAGGER = 9
 MIB = 1024 * 1024
 
 
@@ -41,7 +42,7 @@
 
 
 def logistic(values):
-    return 1.0 / (1.0 + jnp.exp(-values))
+    return 1.0 / (1.0 + jnp.exp2(values * (-1.0 / math.log(2.0))))
 
 
 def matmul(left, right):
@@ -158,8 +159,8 @@
                 pre = part[plane * per_plane : (plane + 1) * per_plane]
                 sigma = logistic(pre)
                 hidden = pre * sigma
-                self.slope[plane * 64 : plane * 64 + per_plane, block_lanes(b)] = sigma * (
-                    1.0 + pre * (1.0 - sigma)
+                self.slope[plane * 64 : plane * 64 + per_plane, block_lanes(b)] = (
+                    sigma + hidden * (1.0 - sigma)
                 )
                 for par in range(per_plane // 32):
                     row = 2 * b + par
@@ -178,8 +179,9 @@
                 (32, LANES), jnp.bfloat16
             )
 
-    def backward(self, field_terms, density, sums_from, sums_to):
+    def middle(self, field_terms, density):
         logits = matmul(self.m_four[...], self.windows[...])
+        yield
         for res_x in range(4):
             for res_z in range(4):
                 at = (res_x * 4 + res_z) * 8
@@ -194,7 +196,10 @@
                 g = d * d * (1.0 - d) * (gain * d - loss)
                 for pair in range(self.pairs):
                     self.g_fine[at : at + 8, block_lanes(pair)] = g[8 * pair : 8 * pair + 8]
-            yield
+                if res_z % 2 == 1:
+                    yield
+
+    def backward(self, sums_from, sums_to):
         g_out = self.g_fine[...].astype(jnp.bfloat16)
         for plane in range(3):
             span = slice(plane * 240, plane * 240 + 240)
@@ -224,9 +229,24 @@
 def run(*streams):
     live = list(streams)
     while live:
-        for stream in list(live):
+        for entry in list(live):
+            stream, count = entry
+            for _ in range(count):
+                if next(stream, live) is live:
+                    live.remove(entry)
+                    break
+
+
+def staggered(pending, side, apart):
+    live = []
+    turn = 0
+    while pending or live or side:
+        if pending and turn % apart == 0:
+            live.append(pending.pop(0))
+        for stream in live + side[:1]:
             if next(stream, live) is live:
-                live.remove(stream)
+                (live if stream in live else side).remove(stream)
+        turn = turn + 1
 
 
 def chain(*streams):
@@ -234,14 +254,22 @@
         yield from stream
 
 
-def interior_kernel(scale, near_far, w_three, w_four, elec, temp, adj, adj_grad, *refs):
-    (density, sum_three, sum_four, m_three, m_four, m_back) = refs[:6]
+def interior_kernel(scale, inside, near, far, *refs):
+    (w_three_far, w_four_far, elec, temp, adj, adj_grad) = refs[:6]
+    refs = refs[6:]
+    (dense, sum_three, sum_four, m_three, m_four, m_back) = refs[:6]
     (onehot, last_gain, last_loss, last_cells) = refs[6:10]
-    (build, flat, cells, elec_v, temp_v, adj_v, adj_grad_v, dense) = refs[10:18]
-    sems = refs[18]
-    held = near_far.shape[2]
+    (build, flat, cells, elec_v, temp_v, adj_v, adj_grad_v) = refs[10:17]
+    (w_three, w_four, sems) = refs[17:20]
+    held = near.shape[1]
     groups = held // 4
-    scratch = refs[19:]
+    scratch = refs[20:]
+    weights = (
+        pltpu.make_async_copy(w_three_far, w_three, sems.at[0, 5]),
+        pltpu.make_async_copy(w_four_far, w_four, sems.at[1, 5]),
+    )
+    for copy in weights:
+        copy.start()
     sets = [scratch[4 * i : 4 * i + 4] for i in range(groups)]
     copies = []
     for q in range(groups):
@@ -257,7 +285,6 @@
         )
         for copy in copies[q]:
             copy.start()
-    outs = []
 
     def field_terms_at(first, count):
         rows = slice(first, first + count)
@@ -265,21 +292,25 @@
             elec_v, temp_v, adj_v, adj_grad_v, scale, res_x, rows, lanes
         )
 
-    def load_cells():
-        for plane in range(2):
-            flat[plane] = near_far[plane].astype(jnp.float32).reshape(flat.shape[1:])
-            yield
-        for b in range(held):
+    def flatten():
+        flat[0] = near[...].astype(jnp.float32).reshape(flat.shape[1:])
+        yield
+        known = inside[0].astype(jnp.float32)
+        flat[1] = known * far[...].astype(jnp.float32).reshape(flat.shape[1:])
+        yield
+
+    def load_cells(first, end):
+        for b in range(first, end):
             for plane in range(2):
                 tile = coarse_tile(flat[plane, pl.ds(b, 32, held), :])
                 cells[plane, b] = tile
                 if b >= held - 2:
                     last_cells[plane, b - held + 2] = tile
-            if b % 2 == 1:
-                yield
+            yield
 
     def zero_sums():
         sum_three[...] = jnp.zeros_like(sum_three)
+        yield
         sum_four[...] = jnp.zeros_like(sum_four)
         yield
 
@@ -290,21 +321,10 @@
         pairs = 2 if q < groups - 1 else 1
         parts.append(Group(pairs, 4 * q, matrices, (cells,) + tuple(sets[q]), False))
 
-    def second(q):
-        for copy in copies[q]:
-            copy.wait()
+    def middle(q):
         count = 8 * parts[q].pairs
         rows = slice(16 * q, 16 * q + count)
-        yield from parts[q].backward(
-            field_terms_at(16 * q, count), dense.at[:, rows, :], sums, sums
-        )
-        out = pltpu.make_async_copy(
-            dense.at[:, pl.ds(16 * q, count), :],
-            density.at[:, pl.ds(16 * q, count), :],
-            sems.at[q, 4],
-        )
-        out.start()
-        outs.append(out)
+        yield from parts[q].middle(field_terms_at(16 * q, count), dense.at[:, rows, :])
 
     def last_fields():
         terms = field_terms_at(16 * groups - 8, 8)
@@ -316,55 +336,59 @@
                 last_loss[res_x, :, lanes] = loss
             yield
 
+    def fill_late():
+        yield from fill_onehot(onehot)
+        weights[1].wait()
+        fill_four(w_four, onehot, m_four, m_back)
+        yield
+
+    run((flatten(), 1))
+    run((load_cells(0, 5), 1))
+    weights[0].wait()
     fill_three(w_three, m_three, build)
-    run(fill_onehot(onehot), load_cells(), zero_sums())
-    fill_four(w_four, onehot, m_four, m_back)
-    run(parts[0].forward())
-    for q in range(groups - 1):
-        run(second(q), parts[q + 1].forward())
-    run(second(groups - 1), last_fields())
-    for out in outs:
-        out.wait()
-
-
-def rim_kernel(place, rim, m_three, m_four, m_back, sum_three_in, sum_four_in, *refs):
-    (onehot, last_gain, last_loss, last_cells, _) = refs[:5]
-    (density, mine, other) = refs[5:8]
-    (packed, sum_three, sum_four, cells, dense, sem) = refs[8:14]
+    run((parts[0].forward(), 2), (fill_late(), 1), (load_cells(5, 9), 1), (zero_sums(), 1))
+    for group_copies in copies:
+        for copy in group_copies:
+            copy.wait()
+    later = [load_cells(9, held), last_fields()]
+    pending = [
+        chain(parts[q].forward() if q > 0 else (), middle(q), parts[q].backward(sums, sums))
+        for q in range(groups)
+    ]
+    staggered(pending, later, STAGGER)
+
+
+def rim_kernel(part, inside, rim, sum_three_in, sum_four_in, *refs):
+    (m_three, m_four, m_back, onehot, last_gain, last_loss, last_cells) = refs[:7]
+    (dense, mine, other) = refs[7:10]
+    (packed, sum_three, sum_four, cells) = refs[10:14]
     scratch = refs[14:]
-    fine_rows = density.shape[1]
+    known = (1.0, inside[0].astype(jnp.float32))
     for plane in range(2):
         for b in range(2):
             cells[plane, b] = last_cells[plane, b]
-        cells[plane, 2] = coarse_tile(rim[plane].astype(jnp.float32))
-    part = Group(1, 0, (m_three, m_four, m_back), (cells,) + tuple(scratch), True)
-    run(part.forward())
-    run(
-        part.backward(
-            lambda res_x, lanes: (last_gain[res_x, :, lanes], last_loss[res_x, :, lanes]),
-            dense,
-            (sum_three_in, sum_four_in),
-            (sum_three, sum_four),
-        )
-    )
-    out = pltpu.make_async_copy(dense, density.at[:, pl.ds(fine_rows - 8, 8), :], sem)
-    out.start()
+        cells[plane, 2] = coarse_tile(known[plane] * rim[plane].astype(jnp.float32))
+    group = Group(1, 0, (m_three, m_four, m_back), (cells,) + tuple(scratch), True)
+    run((group.forward(), 1))
+    terms = lambda res_x, lanes: (last_gain[res_x, :, lanes], last_loss[res_x, :, lanes])
+    run((group.middle(terms, dense), 1))
+    run((group.backward((sum_three_in, sum_four_in), (sum_three, sum_four)), 1))
     by_tap = (
         sum_three[64:128, 128:],
         sum_three[:64, :128] + sum_three[128:, 128:],
         sum_three[64:128, :128],
     )
     for tap_x in range(3):
-        part = by_tap[tap_x]
-        packed[32 * tap_x : 32 * tap_x + 16, :] = part[48:64]
+        along = by_tap[tap_x]
+        packed[32 * tap_x : 32 * tap_x + 16, :] = along[48:64]
         lanes = lane_index((16, LANES))
         mixed = jnp.where(
             lanes < 64,
-            part[16:32],
-            jnp.where(lanes < 96, part[32:48], pltpu.roll(part[32:48], 96, 1)),
+            along[16:32],
+            jnp.where(lanes < 96, along[32:48], pltpu.roll(along[32:48], 96, 1)),
         )
         packed[32 * tap_x + 16 : 32 * tap_x + 32, :] = mixed
-        packed[96:112, 32 * tap_x : 32 * tap_x + 32] = part[:16, :32]
+        packed[96:112, 32 * tap_x : 32 * tap_x + 32] = along[:16, :32]
     rest = jnp.concatenate(
         [sum_four[16 * block : 16 * block + 16, :] for block in range(BLOCKS)], 1
     )
@@ -375,11 +399,10 @@
         rest = rest - piece.astype(jnp.float32)
     folded = matmul_nt(jnp.concatenate(pieces, 0), onehot[...])
     packed[96:112, 96:128] = folded[:16] + folded[16:32] + folded[32:48]
-    which = place[0]
+    which = part[0]
     half = mine.shape[0]
     mine[...] = packed[pl.ds(pl.multiple_of(which * half, 8), half), :]
     other[...] = packed[pl.ds(pl.multiple_of((1 - which) * half, 8), half), :]
-    out.wait()
 
 
 def unpack_kernel(part, mine, other, grad_three, grad_four):
@@ -455,8 +478,9 @@
     inside = at_x + 1 < count_a
     near = lax.dynamic_index_in_dim(coarse, at_x, 1, keepdims=False)
     far = lax.dynamic_index_in_dim(coarse, jnp.minimum(at_x + 1, count_a - 1), 1, keepdims=False)
-    near_far = jnp.stack([near, jnp.where(inside, far, jnp.zeros_like(far))])
-    rim = lax.ppermute(near_far[:, :, 0, :], "gy", [(i + 1, i) for i in range(groups_y - 1)])
+    first_rows = jnp.stack([near[:, 0], far[:, 0]])
+    rim = lax.ppermute(first_rows, "gy", [(i + 1, i) for i in range(groups_y - 1)])
+    inside = inside.astype(jnp.int32).reshape(1)
     part = parity_of(lax.axis_index("gx")) ^ parity_of(lax.axis_index("gy"))
     part = part.astype(jnp.int32).reshape(1)
     groups = held // 4
@@ -476,11 +500,10 @@
         )
 
     in_vmem = pl.BlockSpec(memory_space=pltpu.VMEM)
-    anywhere = pl.BlockSpec(memory_space=pl.ANY)
     hbm = pl.BlockSpec(memory_space=pltpu.HBM)
     in_smem = pl.BlockSpec(memory_space=pltpu.SMEM)
-    dense = shape(adjoint.shape, jnp.float32)
     handed = (
+        shape((fine_x, fine_y - 8, fine_z), jnp.float32),
         shape((192, 256), jnp.float32),
         shape((WINDOW, LANES), jnp.float32),
         shape((192, 256), jnp.bfloat16),
@@ -495,11 +518,11 @@
     per_group = ()
     for q in range(groups):
         per_group = per_group + group_scratch(2 if q < groups - 1 else 1)
-    density, sum_three, sum_four, m_three, m_four, m_back, *rest = pl.pallas_call(
+    most, *held_back = pl.pallas_call(
         lambda *refs: interior_kernel(scale, *refs),
-        out_shape=(dense,) + handed,
-        in_specs=[in_vmem] * 3 + [hbm] * 4,
-        out_specs=(anywhere,) + (in_vmem,) * len(handed),
+        out_shape=handed,
+        in_specs=[in_smem] + [in_vmem] * 2 + [hbm] * 6,
+        out_specs=(in_vmem,) * len(handed),
         scratch_shapes=(
             pltpu.VMEM((192, 256), jnp.float32),
             pltpu.VMEM((2, chan_in * held, LANES), jnp.float32),
@@ -508,8 +531,9 @@
             pltpu.VMEM(temp_grad.shape, jnp.bfloat16),
             pltpu.VMEM(adjoint.shape, jnp.bfloat16),
             pltpu.VMEM(adjoint_grad.shape, jnp.bfloat16),
-            pltpu.VMEM(adjoint.shape, jnp.float32),
-            pltpu.SemaphoreType.DMA((groups, 5)),
+            pltpu.VMEM(w_three.shape, jnp.bfloat16),
+            pltpu.VMEM(w_four.shape[::-1], jnp.bfloat16),
+            pltpu.SemaphoreType.DMA((groups, 6)),
         )
         + per_group,
         compiler_params=pltpu.CompilerParams(vmem_limit_bytes=32 * MIB),
@@ -518,35 +542,35 @@
         ),
         name="interior",
     )(
-        near_far,
-        w_three,
-        w_four.T,
+        inside,
+        near,
+        far,
+        in_hbm(w_three),
+        in_hbm(w_four.T),
         in_hbm(elec_field),
         in_hbm(temp_grad),
         in_hbm(adjoint),
         in_hbm(adjoint_grad),
     )
-    density, mine, other = pl.pallas_call(
+    last_dense, mine, other = pl.pallas_call(
         rim_kernel,
-        out_shape=(dense, half, half),
-        in_specs=[in_smem] + [in_vmem] * (1 + len(handed)) + [anywhere],
-        out_specs=(anywhere, in_vmem, in_vmem),
+        out_shape=(shape((fine_x, 8, fine_z), jnp.float32), half, half),
+        in_specs=[in_smem] * 2 + [in_vmem] * len(handed),
+        out_specs=(in_vmem,) * 3,
         scratch_shapes=(
             pltpu.VMEM((112, LANES), jnp.float32),
             pltpu.VMEM((192, 256), jnp.float32),
             pltpu.VMEM((WINDOW, LANES), jnp.float32),
             pltpu.VMEM((2, 3, 64, LANES), jnp.bfloat16),
-            pltpu.VMEM((4, 8, fine_z), jnp.float32),
-            pltpu.SemaphoreType.DMA(()),
         )
         + group_scratch(1),
-        input_output_aliases={2 + len(handed): 0},
         compiler_params=pltpu.CompilerParams(vmem_limit_bytes=16 * MIB),
         cost_estimate=pl.CostEstimate(
             flops=400000000, bytes_accessed=2000000, transcendentals=400000
         ),
         name="rim",
-    )(part, rim, m_three, m_four, m_back, sum_three, sum_four, *rest, density)
+    )(part, inside, rim, *held_back)
+    density = jnp.concatenate([most, last_dense], 1)
     grad_three, grad_four = sum_everywhere(mine, other, part)
     return (density, grad_three, grad_four)
 

time: 31.3 us -> 30.1 us (0.962)
  local copies, waits for them, and re-layouts: 1.88 us -> 1.08 us
  other arithmetic: 0.12 us -> 0.87 us
  starting transfers between devices: 13 us -> 12.4 us
    concatenate x0 -> x1, other arithmetic: none -> 0.84 us  [shards(): density = jnp.concatenate([most, last_dense], 1)]
    unnamed x4 -> x0, local copies, waits for them, and re-layouts: 0.7 us -> none
    ppermute x6, waiting for transfers between devices: 7.95 us -> 7.3 us  [exchanged(): return lax.ppermute(value, ('gx', 'gy'), pairs)]
    ppermute x6, starting transfers between devices: 11.7 us -> 11.1 us  [exchanged(): return lax.ppermute(value, ('gx', 'gy'), pairs)]
    ppermute x1, waiting for transfers between devices: 0.01 us -> 0.35 us  [shards(): lax.ppermute(first_rows, 'gy', [(i + 1, i) for i in range(groups_y - 1)])]
  transfers between devices with their start and end apart: 7 -> 7, of which waited for: 6 -> 6; matrix products, arithmetic and copies ran while one was open for 1% -> 3% of each run, Pallas kernels for 16% -> 16%
where the time goes in v4:
time: 30.1 us; the launch traced here: 29.9 us
  starting transfers between devices  12.4 us (41%)
  waiting for transfers between devices  7.65 us (25%)
  Pallas kernels  7.14 us (24%)
  local copies, waits for them, and re-layouts  1.08 us (4%)
  other arithmetic  0.87 us (3%)
  between operations  0.73 us (2%)
    ppermute x6, starting transfers between devices, exchanged(): return lax.ppermute(value, ('gx', 'gy'), pairs)  11.1 us
    ppermute x6, waiting for transfers between devices, exchanged(): return lax.ppermute(value, ('gx', 'gy'), pairs)  7.3 us
    pallas_call x1, Pallas kernels, shards(): pl.pallas_call(lambda *refs: interior_kernel(scale, *refs), out_shape=han...  4.9 us
    pallas_call x1, Pallas kernels, shards(): pl.pallas_call(rim_kernel, out_shape=(shape((fine_x, 8, fine_z), jnp.floa...  1.44 us
    ppermute x1, starting transfers between devices, shards(): lax.ppermute(first_rows, 'gy', [(i + 1, i) for i in range(groups_y - 1)])  1.29 us
    dynamic_slice x1, local copies, waits for them, and re-layouts, shards(): near = lax.dynamic_index_in_dim(coarse, at_x, 1, keepdims=False)  1 us
    concatenate x1, other arithmetic, shards(): density = jnp.concatenate([most, last_dense], 1)  0.84 us
    pallas_call x1, Pallas kernels, sum_everywhere(): pl.pallas_call(unpack_kernel, out_shape=(jax.ShapeDtypeStruct((27, 16, 32...  0.8 us
  transfers between devices with their start and end apart: 7, of which 6 were waited for; matrix products, arithmetic and copies ran while one was open for 3% of the time, Pallas kernels for 16%

profile of v4, /device:TPU:0, one launch (start us, length us, event | category | flops | bytes accessed | tf_op | source)
XLA Modules:
  0.0 29.9 jit_solution(9131056136057161075)
XLA Ops:
  0.6 1.0 %constant_dynamic-slice_fusion.1 = (bf16[32,1,16,128]{3,2,1,0:T(8,128)(2,1)S(1)}, bf16[32,1,16,128]{3,2,1,0:T(8,128)(2,1)S(1)}) fusion(bf16[32,8,16,128]{3,2,1,0:T(8,128)(2,1)} %param.7, s32[]{:T(128)S(6)} %select_n.7, s32[]{:T(128)S(6)} %select_n.8), kind=kLoop, calls=%fused_computation.7 | loop fusion | bytes 524296 | tf_op jit(solution)/shard_map/jit(dynamic_index_in_dim)/dynamic_slice | solution.py:479
  1.6 0.1 copy_bitcast_fusion
  1.8 1.3 %collective-permute-start = (bf16[2,32,128]{2,1,0:T(8,128)(2,1)S(1)}, bf16[2,32,128]{2,1,0:T(8,128)(2,1)S(1)}, u32[]{:S(2)}, u32[]{:S(2)}) collective-permute-start(bf16[2,32,128]{2,1,0:T(8,128)(2,1)S(1)} %pad_maximum_fusion.1), channel_id=1, source_target_pairs={{1,0},{2,1},{3,2},{5,4},{6,5},{7,6},{9,8},{10,9},{11,10},{13,12},{... | collective-permute-start | bytes 49160 | tf_op jit(solution)/shard_map/ppermute | solution.py:482
  3.1 4.9 %interior.1 = (f32[4,56,512]{2,1,0:T(8,128)S(1)}, f32[192,256]{1,0:T(8,128)S(1)}, f32[720,128]{1,0:T(8,128)S(1)}, bf16[192,256]{1,0:T(8,128)(2,1)S(1)}, bf16[128...) custom-call(s32[1]{0:T(128)} %bitcast.refs_0_.inside, ...), custom_call_target="tpu_custom_call" | custom-call | flops 2000000000 | bytes 4000000 | tf_op jit(solution)/shard_map/interior/pallas_call | solution.py:521
  8.0 0.3 %collective-permute-done.rim = bf16[2,32,128]{2,1,0:T(8,128)(2,1)S(1)} collective-permute-done((bf16[2,32,128]{2,1,0:T(8,128)(2,1)S(1)}, bf16[2,32,128]{2,1,0:T(8,128)(2,1)S(1)}, u32[]{:S(2)}, u32[]{:S(2)}) %collective-permute-start) | collective-permute-done | bytes 16416 | tf_op jit(solution)/shard_map/ppermute | solution.py:482
  8.3 1.4 %rim.1 = (f32[4,8,512]{2,1,0:T(8,128)S(1)}, f32[56,128]{1,0:T(8,128)S(1)}, f32[56,128]{1,0:T(8,128)S(1)}) custom-call(s32[1]{0:T(128)} %bitcast.6.part, s32[1]{0:T(128)} %bitcast.refs_0_.inside, bf16[2,32,128]{2,1,0:T(8,128)(2,1)S(1)} %collective-permute-done.rim, f32[192,256]{1,0:T(8,128)S(1)} %get-tuple-element.19.sum_three_in, ...), custom_call_target="tpu_custom_call" | custom-call | flops 400000000 | bytes 2000000 | tf_op jit(solution)/shard_map/rim/pallas_call | solution.py:555
  9.8 0.2 collective-permute-start.1
  10.0 1.0 %collective-permute-done.1 = f32[56,128]{1,0:T(8,128)S(1)} collective-permute-done((f32[56,128]{1,0:T(8,128)S(1)}, f32[56,128]{1,0:T(8,128)S(1)}, u32[]{:S(2)}, u32[]{:S(2)}) %collective-permute-start.1) | collective-permute-done | bytes 28704 | tf_op jit(solution)/shard_map/ppermute | solution.py:430
  11.0 2.5 %collective-permute-start.2 = (f32[56,128]{1,0:T(8,128)S(1)}, f32[56,128]{1,0:T(8,128)S(1)}, u32[]{:S(2)}, u32[]{:S(2)}) collective-permute-start(f32[56,128]{1,0:T(8,128)S(1)} %add.29), channel_id=1, source_target_pairs={{0,12},{1,13},{2,14},{3,15},{4,8},{5,9},{6,10},{7,11},{8,4},{9,5},... | collective-permute-start | bytes 86024 | tf_op jit(solution)/shard_map/ppermute | solution.py:430
  13.5 1.6 %collective-permute-done.2 = f32[56,128]{1,0:T(8,128)S(1)} collective-permute-done((f32[56,128]{1,0:T(8,128)S(1)}, f32[56,128]{1,0:T(8,128)S(1)}, u32[]{:S(2)}, u32[]{:S(2)}) %collective-permute-start.2) | collective-permute-done | bytes 28704 | tf_op jit(solution)/shard_map/ppermute | solution.py:430
  15.1 2.7 %collective-permute-start.3 = (f32[56,128]{1,0:T(8,128)S(1)}, f32[56,128]{1,0:T(8,128)S(1)}, u32[]{:S(2)}, u32[]{:S(2)}) collective-permute-start(f32[56,128]{1,0:T(8,128)S(1)} %add.30), channel_id=1, source_target_pairs={{0,20},{1,21},{2,22},{3,23},{4,16},{5,17},{6,18},{7,19},{8,28},{9,... | collective-permute-start | bytes 86024 | tf_op jit(solution)/shard_map/ppermute | solution.py:430
  17.8 1.6 %collective-permute-done.3 = f32[56,128]{1,0:T(8,128)S(1)} collective-permute-done((f32[56,128]{1,0:T(8,128)S(1)}, f32[56,128]{1,0:T(8,128)S(1)}, u32[]{:S(2)}, u32[]{:S(2)}) %collective-permute-start.3) | collective-permute-done | bytes 28704 | tf_op jit(solution)/shard_map/ppermute | solution.py:430
  19.4 2.6 %collective-permute-start.4 = (f32[56,128]{1,0:T(8,128)S(1)}, f32[56,128]{1,0:T(8,128)S(1)}, u32[]{:S(2)}, u32[]{:S(2)}) collective-permute-start(f32[56,128]{1,0:T(8,128)S(1)} %add.31), channel_id=1, source_target_pairs={{0,5},{1,4},{2,7},{3,6},{4,1},{5,0},{6,3},{7,2},{8,13},{9,12},{10,... | collective-permute-start | bytes 86024 | tf_op jit(solution)/shard_map/ppermute | solution.py:430
  22.0 1.6 %collective-permute-done.4 = f32[56,128]{1,0:T(8,128)S(1)} collective-permute-done((f32[56,128]{1,0:T(8,128)S(1)}, f32[56,128]{1,0:T(8,128)S(1)}, u32[]{:S(2)}, u32[]{:S(2)}) %collective-permute-start.4) | collective-permute-done | bytes 28704 | tf_op jit(solution)/shard_map/ppermute | solution.py:430
  23.5 2.8 %collective-permute-start.5 = (f32[56,128]{1,0:T(8,128)S(1)}, f32[56,128]{1,0:T(8,128)S(1)}, u32[]{:S(2)}, u32[]{:S(2)}) collective-permute-start(f32[56,128]{1,0:T(8,128)S(1)} %add.32), channel_id=1, source_target_pairs={{0,6},{1,7},{2,4},{3,5},{4,2},{5,3},{6,0},{7,1},{8,14},{9,15},{10,... | collective-permute-start | bytes 86024 | tf_op jit(solution)/shard_map/ppermute | solution.py:430
  26.3 1.6 %collective-permute-done.5 = f32[56,128]{1,0:T(8,128)S(1)} collective-permute-done((f32[56,128]{1,0:T(8,128)S(1)}, f32[56,128]{1,0:T(8,128)S(1)}, u32[]{:S(2)}, u32[]{:S(2)}) %collective-permute-start.5) | collective-permute-done | bytes 28704 | tf_op jit(solution)/shard_map/ppermute | solution.py:430
  27.9 0.3 %collective-permute-start.6 = (f32[56,128]{1,0:T(8,128)S(1)}, f32[56,128]{1,0:T(8,128)S(1)}, u32[]{:S(2)}, u32[]{:S(2)}) collective-permute-start(f32[56,128]{1,0:T(8,128)S(1)} %add.33.mine), channel_id=1, source_target_pairs={{0,4},{1,5},{2,6},{3,7},{4,0},{5,1},{6,2},{7,3},{8,12},{9,13},{10,... | collective-permute-start | bytes 86024 | tf_op jit(solution)/shard_map/ppermute | solution.py:430
  28.2 0.8 %pad_maximum_fusion = f32[4,64,512]{2,1,0:T(8,128)} fusion(f32[4,8,512]{2,1,0:T(8,128)S(1)} %get-tuple-element.28, f32[4,56,512]{2,1,0:T(8,128)S(1)} %get-tuple-element.18), kind=kLoop, calls=%fused_computation | loop fusion | flops 131072 | bytes 1048576 | tf_op jit(solution)/shard_map/concatenate | solution.py:573
  29.0 0.0 collective-permute-done.6.other
  29.1 0.8 %unpack.1 = (f32[27,16,32]{2,1,0:T(8,128)}, f32[16,27]{1,0:T(8,128)}) custom-call(s32[1]{0:T(128)} %bitcast.6.part, f32[56,128]{1,0:T(8,128)S(1)} %add.33.mine, f32[56,128]{1,0:T(8,128)S(1)} %collective-permute-done.6.other), custom_call_target="tpu_custom_call" | custom-call | tf_op jit(solution)/shard_map/unpack/pallas_call | solution.py:455
  (8 shorter events, 0.0 us)
Async XLA Ops:
  1.8 6.6 %collective-permute-start = (bf16[2,32,128]{2,1,0:T(8,128)(2,1)S(1)}, bf16[2,32,128]{2,1,0:T(8,128)(2,1)S(1)}, u32[]{:S(2)}, u32[]{:S(2)}) collective-permute-start(bf16[2,32,128]{2,1,0:T(8,128)(2,1)S(1)} %pad_maximum_fusion.1), channel_id=1, source_target_pairs={{1,0},{2,1},{3,2},{5,4},{6,5},{7,6},{9,8},{10,9},{11,10},{13,12},{... | collective-permute-start | bytes 49160 | tf_op jit(solution)/shard_map/ppermute | solution.py:482
  9.8 1.2 %collective-permute-start.1 = (f32[56,128]{1,0:T(8,128)S(1)}, f32[56,128]{1,0:T(8,128)S(1)}, u32[]{:S(2)}, u32[]{:S(2)}) collective-permute-start(f32[56,128]{1,0:T(8,128)S(1)} %get-tuple-element.30), channel_id=1, source_target_pairs={{0,4},{1,5},{2,6},{3,7},{4,0},{5,1},{6,2},{7,3},{8,12},{9,13},{10,... | collective-permute-start | bytes 86024 | tf_op jit(solution)/shard_map/ppermute | solution.py:430
  11.0 4.1 %collective-permute-start.2 = (f32[56,128]{1,0:T(8,128)S(1)}, f32[56,128]{1,0:T(8,128)S(1)}, u32[]{:S(2)}, u32[]{:S(2)}) collective-permute-start(f32[56,128]{1,0:T(8,128)S(1)} %add.29), channel_id=1, source_target_pairs={{0,12},{1,13},{2,14},{3,15},{4,8},{5,9},{6,10},{7,11},{8,4},{9,5},... | collective-permute-start | bytes 86024 | tf_op jit(solution)/shard_map/ppermute | solution.py:430
  15.1 4.3 %collective-permute-start.3 = (f32[56,128]{1,0:T(8,128)S(1)}, f32[56,128]{1,0:T(8,128)S(1)}, u32[]{:S(2)}, u32[]{:S(2)}) collective-permute-start(f32[56,128]{1,0:T(8,128)S(1)} %add.30), channel_id=1, source_target_pairs={{0,20},{1,21},{2,22},{3,23},{4,16},{5,17},{6,18},{7,19},{8,28},{9,... | collective-permute-start | bytes 86024 | tf_op jit(solution)/shard_map/ppermute | solution.py:430
  19.4 4.1 %collective-permute-start.4 = (f32[56,128]{1,0:T(8,128)S(1)}, f32[56,128]{1,0:T(8,128)S(1)}, u32[]{:S(2)}, u32[]{:S(2)}) collective-permute-start(f32[56,128]{1,0:T(8,128)S(1)} %add.31), channel_id=1, source_target_pairs={{0,5},{1,4},{2,7},{3,6},{4,1},{5,0},{6,3},{7,2},{8,13},{9,12},{10,... | collective-permute-start | bytes 86024 | tf_op jit(solution)/shard_map/ppermute | solution.py:430
  23.5 4.3 %collective-permute-start.5 = (f32[56,128]{1,0:T(8,128)S(1)}, f32[56,128]{1,0:T(8,128)S(1)}, u32[]{:S(2)}, u32[]{:S(2)}) collective-permute-start(f32[56,128]{1,0:T(8,128)S(1)} %add.32), channel_id=1, source_target_pairs={{0,6},{1,7},{2,4},{3,5},{4,2},{5,3},{6,0},{7,1},{8,14},{9,15},{10,... | collective-permute-start | bytes 86024 | tf_op jit(solution)/shard_map/ppermute | solution.py:430
  27.9 1.2 %collective-permute-start.6 = (f32[56,128]{1,0:T(8,128)S(1)}, f32[56,128]{1,0:T(8,128)S(1)}, u32[]{:S(2)}, u32[]{:S(2)}) collective-permute-start(f32[56,128]{1,0:T(8,128)S(1)} %add.33.mine), channel_id=1, source_target_pairs={{0,4},{1,5},{2,6},{3,7},{4,0},{5,1},{6,2},{7,3},{8,12},{9,13},{10,... | collective-permute-start | bytes 86024 | tf_op jit(solution)/shard_map/ppermute | solution.py:430

commit v5 on v4

--- a/solution.py
+++ b/solution.py
@@ -11,7 +11,8 @@
 BLOCKS = 3 * PAIR_ROWS * 3
 WINDOW = BLOCKS * 16
 LANES = 128
-STAGGER = 9
+FRONT_APART = 5
+BACK_APART = 5
 MIB = 1024 * 1024
 
 
@@ -33,7 +34,7 @@
 
 def next_lane(tile):
     moved = pltpu.roll(tile, LANES - 1, 1)
-    return jnp.where(lane_index(tile.shape) == LANES - 1, 0.0, moved)
+    return jnp.where(lane_index(tile.shape) == LANES - 1, jnp.zeros_like(tile), moved)
 
 
 def previous_lane(tile):
@@ -69,12 +70,15 @@
     twice_x = (at >> 5) + 1 - tap_x
     twice_z = ((at >> 3) & 3) + 1 - tap_z
     twice_y = (at & 7) + 1 - tap_y
-    code = (twice_x + 2) * 256 + (twice_y + 2) * 16 + (twice_z + 2)
-    code = jnp.where(tap < 27, code, -1)
+    odd = (twice_x | twice_y | twice_z) & 1
+    inside = jnp.minimum(jnp.minimum(twice_x, twice_y), twice_z)
+    block_of = (twice_x >> 1) * 15 + (twice_y >> 1) * 3 + (twice_z >> 1)
+    known = jnp.where(odd == 0, block_of, -1)
+    known = jnp.where(inside >= 0, known, -1)
+    known = jnp.where(tap < 27, known, -1).astype(jnp.float32).astype(jnp.bfloat16)
+    one, zero = (jnp.ones((32, LANES), jnp.bfloat16), jnp.zeros((32, LANES), jnp.bfloat16))
     for block in range(BLOCKS):
-        src_x, src_y, src_z = (block // 15, block // 3 % 5, block % 3)
-        wanted = (2 * src_x + 2) * 256 + (2 * src_y + 2) * 16 + (2 * src_z + 2)
-        onehot[:, block_lanes(block)] = jnp.where(code == wanted, 1.0, 0.0).astype(jnp.bfloat16)
+        onehot[:, block_lanes(block)] = jnp.where(known == jnp.bfloat16(block), one, zero)
         if block % 5 == 4:
             yield
 
@@ -101,11 +105,11 @@
     spread = matmul(w_four[...], onehot[:27, :])
     columns = jnp.concatenate([spread[:, block_lanes(block)] for block in range(BLOCKS)], 0)
     m_back[...] = columns.astype(jnp.bfloat16)
-    m_four[...] = columns.T.astype(jnp.bfloat16)
+    m_four[...] = columns.astype(jnp.bfloat16).T
 
 
 def coarse_tile(rows):
-    return jnp.concatenate([rows, next_lane(rows)], 0).astype(jnp.bfloat16)
+    return jnp.concatenate([rows, next_lane(rows)], 0)
 
 
 def window_of(cells, b, last):
@@ -164,8 +168,8 @@
                 )
                 for par in range(per_plane // 32):
                     row = 2 * b + par
-                    two = hidden[par * 32 : par * 32 + 32]
-                    tall = jnp.concatenate([two, next_lane(two[:16])], 0).astype(jnp.bfloat16)
+                    two = hidden[par * 32 : par * 32 + 32].astype(jnp.bfloat16)
+                    tall = jnp.concatenate([two, next_lane(two[:16])], 0)
                     for pair in range(self.pairs):
                         within = row - 4 * pair
                         if 0 <= within < PAIR_ROWS:
@@ -179,28 +183,39 @@
                 (32, LANES), jnp.bfloat16
             )
 
-    def middle(self, field_terms, density):
+    def solid(self, density):
         logits = matmul(self.m_four[...], self.windows[...])
         yield
         for res_x in range(4):
             for res_z in range(4):
                 at = (res_x * 4 + res_z) * 8
-                lanes = block_lanes(res_z)
-                d = logistic(
+                density[res_x, :, block_lanes(res_z)] = logistic(
                     jnp.concatenate(
                         [logits[at : at + 8, block_lanes(pair)] for pair in range(self.pairs)], 0
                     )
                 )
-                density[res_x, :, lanes] = d
+            yield
+
+    def middle(self, field_terms, density):
+        for res_x in range(4):
+            for res_z in range(4):
+                at = (res_x * 4 + res_z) * 8
+                lanes = block_lanes(res_z)
+                d = density[res_x, :, lanes]
                 gain, loss = field_terms(res_x, lanes)
                 g = d * d * (1.0 - d) * (gain * d - loss)
+                if res_z % 2 == 0:
+                    before = g
+                    continue
                 for pair in range(self.pairs):
-                    self.g_fine[at : at + 8, block_lanes(pair)] = g[8 * pair : 8 * pair + 8]
-                if res_z % 2 == 1:
-                    yield
+                    rows = slice(8 * pair, 8 * pair + 8)
+                    self.g_fine[at - 8 : at + 8, block_lanes(pair)] = jnp.concatenate(
+                        [before[rows], g[rows]], 0
+                    ).astype(jnp.bfloat16)
+                yield
 
     def backward(self, sums_from, sums_to):
-        g_out = self.g_fine[...].astype(jnp.bfloat16)
+        g_out = self.g_fine[...]
         for plane in range(3):
             span = slice(plane * 240, plane * 240 + 240)
             spread = matmul(self.m_back[span, :], g_out)
@@ -254,37 +269,50 @@
         yield from stream
 
 
-def interior_kernel(scale, inside, near, far, *refs):
-    (w_three_far, w_four_far, elec, temp, adj, adj_grad) = refs[:6]
-    refs = refs[6:]
+def fetch_kernel(at_x, coarse, *refs):
+    sems = refs[-1]
+    count = (len(refs) - 4) // 2
+    last = coarse.shape[1] - 1
+    base = at_x[0] - lax.rem(at_x[0], 2)
+    copies = [
+        pltpu.make_async_copy(coarse.at[:, jnp.minimum(base + i, last), :, :], here, sems.at[i])
+        for i, here in enumerate(refs[count : count + 3])
+    ]
+    copies = copies + [
+        pltpu.make_async_copy(refs[i], refs[count + 3 + i], sems.at[3 + i]) for i in range(count)
+    ]
+    for copy in copies:
+        copy.start()
+    for copy in copies:
+        copy.wait()
+
+
+def interior_kernel(scale, core, inside, *refs):
+    (plane_a, plane_b, plane_c, w_three, w_four, elec, adj, temp, adj_grad) = refs[:9]
+    refs = refs[9:]
     (dense, sum_three, sum_four, m_three, m_four, m_back) = refs[:6]
     (onehot, last_gain, last_loss, last_cells) = refs[6:10]
-    (build, flat, cells, elec_v, temp_v, adj_v, adj_grad_v) = refs[10:17]
-    (w_three, w_four, sems) = refs[17:20]
-    held = near.shape[1]
+    (build, cells, elec_v, adj_v, temp_v, adj_grad_v, sems) = refs[10:17]
+    held = plane_a.shape[0]
     groups = held // 4
-    scratch = refs[20:]
-    weights = (
-        pltpu.make_async_copy(w_three_far, w_three, sems.at[0, 5]),
-        pltpu.make_async_copy(w_four_far, w_four, sems.at[1, 5]),
-    )
-    for copy in weights:
-        copy.start()
+    scratch = refs[17:]
     sets = [scratch[4 * i : 4 * i + 4] for i in range(groups)]
-    copies = []
-    for q in range(groups):
-        rows = pl.ds(16 * q, 16)
-        copies.append(
-            [
-                pltpu.make_async_copy(far.at[:, :, rows, :], here.at[:, :, rows, :], sems.at[q, i])
-                for i, (far, here) in enumerate(
-                    ((elec, elec_v), (temp, temp_v), (adj_grad, adj_grad_v))
-                )
-            ]
-            + [pltpu.make_async_copy(adj.at[:, rows, :], adj_v.at[:, rows, :], sems.at[q, 3])]
-        )
-        for copy in copies[q]:
+    def copies_of(comp):
+        return [
+            pltpu.make_async_copy(far.at[comp], here.at[comp], sems.at[comp, i])
+            for i, (far, here) in enumerate(
+                ((elec, elec_v), (temp, temp_v), (adj_grad, adj_grad_v))
+            )
+        ]
+
+    def start_copies(comp, carry):
+        for copy in copies_of(comp):
             copy.start()
+        return carry
+
+    adjoint_copy = pltpu.make_async_copy(adj, adj_v, sems.at[0, 3])
+    adjoint_copy.start()
+    lax.fori_loop(0, 3, start_copies, 0)
 
     def field_terms_at(first, count):
         rows = slice(first, first + count)
@@ -292,17 +320,15 @@
             elec_v, temp_v, adj_v, adj_grad_v, scale, res_x, rows, lanes
         )
 
-    def flatten():
-        flat[0] = near[...].astype(jnp.float32).reshape(flat.shape[1:])
-        yield
-        known = inside[0].astype(jnp.float32)
-        flat[1] = known * far[...].astype(jnp.float32).reshape(flat.shape[1:])
-        yield
-
-    def load_cells(first, end):
-        for b in range(first, end):
-            for plane in range(2):
-                tile = coarse_tile(flat[plane, pl.ds(b, 32, held), :])
+    known = inside[0].astype(jnp.float32).astype(jnp.bfloat16)
+
+    def load_cells():
+        low = core[0] == 0
+        for b in range(held):
+            near = jnp.where(low, plane_a[b], plane_b[b])
+            far = known * jnp.where(low, plane_b[b], plane_c[b])
+            for plane, rows in enumerate((near, far)):
+                tile = coarse_tile(rows)
                 cells[plane, b] = tile
                 if b >= held - 2:
                     last_cells[plane, b - held + 2] = tile
@@ -321,10 +347,18 @@
         pairs = 2 if q < groups - 1 else 1
         parts.append(Group(pairs, 4 * q, matrices, (cells,) + tuple(sets[q]), False))
 
-    def middle(q):
-        count = 8 * parts[q].pairs
-        rows = slice(16 * q, 16 * q + count)
-        yield from parts[q].middle(field_terms_at(16 * q, count), dense.at[:, rows, :])
+    def front(q):
+        yield from parts[q].forward()
+        yield from parts[q].solid(dense.at[:, rows_of(q), :])
+
+    def back(q):
+        yield from parts[q].middle(
+            field_terms_at(16 * q, 8 * parts[q].pairs), dense.at[:, rows_of(q), :]
+        )
+        yield from parts[q].backward(sums, sums)
+
+    def rows_of(q):
+        return slice(16 * q, 16 * q + 8 * parts[q].pairs)
 
     def last_fields():
         terms = field_terms_at(16 * groups - 8, 8)
@@ -336,26 +370,15 @@
                 last_loss[res_x, :, lanes] = loss
             yield
 
-    def fill_late():
-        yield from fill_onehot(onehot)
-        weights[1].wait()
-        fill_four(w_four, onehot, m_four, m_back)
-        yield
-
-    run((flatten(), 1))
-    run((load_cells(0, 5), 1))
-    weights[0].wait()
+    run((fill_onehot(onehot), 1), (load_cells(), 2), (zero_sums(), 1))
+    fill_four(w_four, onehot, m_four, m_back)
     fill_three(w_three, m_three, build)
-    run((parts[0].forward(), 2), (fill_late(), 1), (load_cells(5, 9), 1), (zero_sums(), 1))
-    for group_copies in copies:
-        for copy in group_copies:
+    staggered([front(q) for q in range(groups)], [], FRONT_APART)
+    adjoint_copy.wait()
+    for comp in range(3):
+        for copy in copies_of(comp):
             copy.wait()
-    later = [load_cells(9, held), last_fields()]
-    pending = [
-        chain(parts[q].forward() if q > 0 else (), middle(q), parts[q].backward(sums, sums))
-        for q in range(groups)
-    ]
-    staggered(pending, later, STAGGER)
+    staggered([back(q) for q in range(groups)], [last_fields()], BACK_APART)
 
 
 def rim_kernel(part, inside, rim, sum_three_in, sum_four_in, *refs):
@@ -363,14 +386,15 @@
     (dense, mine, other) = refs[7:10]
     (packed, sum_three, sum_four, cells) = refs[10:14]
     scratch = refs[14:]
-    known = (1.0, inside[0].astype(jnp.float32))
+    known = inside[0].astype(jnp.float32).astype(jnp.bfloat16)
     for plane in range(2):
         for b in range(2):
             cells[plane, b] = last_cells[plane, b]
-        cells[plane, 2] = coarse_tile(known[plane] * rim[plane].astype(jnp.float32))
+        cells[plane, 2] = coarse_tile(rim[plane] if plane == 0 else known * rim[plane])
     group = Group(1, 0, (m_three, m_four, m_back), (cells,) + tuple(scratch), True)
     run((group.forward(), 1))
     terms = lambda res_x, lanes: (last_gain[res_x, :, lanes], last_loss[res_x, :, lanes])
+    run((group.solid(dense), 1))
     run((group.middle(terms, dense), 1))
     run((group.backward((sum_three_in, sum_four_in), (sum_three, sum_four)), 1))
     by_tap = (
@@ -475,33 +499,55 @@
     cells = fine_x * groups_x * fine_y * groups_y * fine_z
     scale = 8.0 / math.sqrt(cells)
     at_x = lax.axis_index("gx").astype(jnp.int32)
-    inside = at_x + 1 < count_a
-    near = lax.dynamic_index_in_dim(coarse, at_x, 1, keepdims=False)
-    far = lax.dynamic_index_in_dim(coarse, jnp.minimum(at_x + 1, count_a - 1), 1, keepdims=False)
-    first_rows = jnp.stack([near[:, 0], far[:, 0]])
-    rim = lax.ppermute(first_rows, "gy", [(i + 1, i) for i in range(groups_y - 1)])
-    inside = inside.astype(jnp.int32).reshape(1)
+    inside = (at_x + 1 < count_a).astype(jnp.int32).reshape(1)
+    core = at_x % 2
+    in_vmem = pl.BlockSpec(memory_space=pltpu.VMEM)
+    hbm = pl.BlockSpec(memory_space=pltpu.HBM)
+    in_smem = pl.BlockSpec(memory_space=pltpu.SMEM)
+
+    def shape(dims, dtype):
+        return jax.ShapeDtypeStruct(dims, dtype)
+
+    def in_hbm(value):
+        return pltpu.with_memory_space_constraint(value, pltpu.HBM)
+
+    wanted = [w_three, w_four.T]
+    fetched = pl.pallas_call(
+        fetch_kernel,
+        out_shape=(shape((chan_in, held, depth), coarse.dtype),) * 3
+        + tuple(shape(value.shape, value.dtype) for value in wanted),
+        in_specs=[in_smem, hbm] + [hbm] * len(wanted),
+        out_specs=(in_vmem,) * (3 + len(wanted)),
+        scratch_shapes=(pltpu.SemaphoreType.DMA((3 + len(wanted),)),),
+        compiler_params=pltpu.CompilerParams(vmem_limit_bytes=4 * MIB),
+        name="fetch",
+    )(at_x.reshape(1), in_hbm(coarse), *(in_hbm(value) for value in wanted))
+    planes = fetched[:3]
+    planes = [plane.transpose(1, 0, 2) for plane in planes]
+    first_rows = jnp.stack(
+        [jnp.where(core == 0, planes[i + 1][0], planes[i][0]) for i in range(2)]
+    )
+    rim = lax.ppermute(
+        first_rows,
+        ("gx", "gy"),
+        [
+            ((i ^ 1) * groups_y + j + 1, i * groups_y + j)
+            for i in range(groups_x)
+            for j in range(groups_y - 1)
+        ],
+    )
     part = parity_of(lax.axis_index("gx")) ^ parity_of(lax.axis_index("gy"))
     part = part.astype(jnp.int32).reshape(1)
     groups = held // 4
-
-    def shape(dims, dtype):
-        return jax.ShapeDtypeStruct(dims, dtype)
-
-    def in_hbm(value):
-        return pltpu.with_memory_space_constraint(value, pltpu.HBM)
 
     def group_scratch(pairs):
         return (
             pltpu.VMEM((WINDOW, pairs * LANES), jnp.bfloat16),
             pltpu.VMEM((192, (2 * pairs + 1) * LANES), jnp.float32),
-            pltpu.VMEM((LANES, pairs * LANES), jnp.float32),
+            pltpu.VMEM((LANES, pairs * LANES), jnp.bfloat16),
             pltpu.VMEM((192, (2 * pairs + 1) * LANES), jnp.bfloat16),
         )
 
-    in_vmem = pl.BlockSpec(memory_space=pltpu.VMEM)
-    hbm = pl.BlockSpec(memory_space=pltpu.HBM)
-    in_smem = pl.BlockSpec(memory_space=pltpu.SMEM)
     handed = (
         shape((fine_x, fine_y - 8, fine_z), jnp.float32),
         shape((192, 256), jnp.float32),
@@ -521,19 +567,16 @@
     most, *held_back = pl.pallas_call(
         lambda *refs: interior_kernel(scale, *refs),
         out_shape=handed,
-        in_specs=[in_smem] + [in_vmem] * 2 + [hbm] * 6,
+        in_specs=[in_smem] * 2 + [in_vmem] * 5 + [hbm] * 4,
         out_specs=(in_vmem,) * len(handed),
         scratch_shapes=(
             pltpu.VMEM((192, 256), jnp.float32),
-            pltpu.VMEM((2, chan_in * held, LANES), jnp.float32),
             pltpu.VMEM((2, held, 64, LANES), jnp.bfloat16),
             pltpu.VMEM(elec_field.shape, jnp.bfloat16),
+            pltpu.VMEM(adjoint.shape, jnp.bfloat16),
             pltpu.VMEM(temp_grad.shape, jnp.bfloat16),
-            pltpu.VMEM(adjoint.shape, jnp.bfloat16),
             pltpu.VMEM(adjoint_grad.shape, jnp.bfloat16),
-            pltpu.VMEM(w_three.shape, jnp.bfloat16),
-            pltpu.VMEM(w_four.shape[::-1], jnp.bfloat16),
-            pltpu.SemaphoreType.DMA((groups, 6)),
+            pltpu.SemaphoreType.DMA((3, 4)),
         )
         + per_group,
         compiler_params=pltpu.CompilerParams(vmem_limit_bytes=32 * MIB),
@@ -542,14 +585,13 @@
         ),
         name="interior",
     )(
+        core.reshape(1),
         inside,
-        near,
-        far,
-        in_hbm(w_three),
-        in_hbm(w_four.T),
+        *planes,
+        *fetched[3:],
         in_hbm(elec_field),
+        in_hbm(adjoint),
         in_hbm(temp_grad),
-        in_hbm(adjoint),
         in_hbm(adjoint_grad),
     )
     last_dense, mine, other = pl.pallas_call(

time: 30.1 us -> 29.1 us (0.967)
  local copies, waits for them, and re-layouts: 1.08 us -> 0.11 us
    pallas_call x1, Pallas kernels: 4.9 us -> 3.75 us  [shards(): pl.pallas_call(lambda *refs: interior_kernel(scale, *refs), out_shape=han...]
    pallas_call x0 -> x1, Pallas kernels: none -> 1.15 us  [shards(): pl.pallas_call(fetch_kernel, out_shape=(shape((chan_in, held, depth), coa...]
    dynamic_slice x1 -> x0, local copies, waits for them, and re-layouts: 1 us -> none  [shards(): near = lax.dynamic_index_in_dim(coarse, at_x, 1, keepdims=False)]
    ppermute x6, starting transfers between devices: 11.1 us -> 10.8 us  [exchanged(): return lax.ppermute(value, ('gx', 'gy'), pairs)]
  transfers between devices with their start and end apart: 7 -> 7, of which waited for: 6 -> 7; matrix products, arithmetic and copies ran while one was open for 3% -> 3% of each run, Pallas kernels for 16% -> 13%
where the time goes in v5:
time: 29.1 us; the launch traced here: 28.9 us
  starting transfers between devices  12.1 us (42%)
  waiting for transfers between devices  7.94 us (27%)
  Pallas kernels  7.16 us (25%)
  other arithmetic  0.88 us (3%)
  between operations  0.74 us (3%)
    ppermute x6, starting transfers between devices, exchanged(): return lax.ppermute(value, ('gx', 'gy'), pairs)  10.8 us
    ppermute x6, waiting for transfers between devices, exchanged(): return lax.ppermute(value, ('gx', 'gy'), pairs)  7.3 us
    pallas_call x1, Pallas kernels, shards(): pl.pallas_call(lambda *refs: interior_kernel(scale, *refs), out_shape=han...  3.75 us
    pallas_call x1, Pallas kernels, shards(): pl.pallas_call(rim_kernel, out_shape=(shape((fine_x, 8, fine_z), jnp.floa...  1.46 us
    ppermute x1, starting transfers between devices, shards(): lax.ppermute(first_rows, ('gx', 'gy'), [((i ^ 1) * groups_y + j + 1, i *...  1.29 us
    pallas_call x1, Pallas kernels, shards(): pl.pallas_call(fetch_kernel, out_shape=(shape((chan_in, held, depth), coa...  1.15 us
    concatenate x1, other arithmetic, shards(): density = jnp.concatenate([most, last_dense], 1)  0.84 us
    pallas_call x1, Pallas kernels, sum_everywhere(): pl.pallas_call(unpack_kernel, out_shape=(jax.ShapeDtypeStruct((27, 16, 32...  0.8 us
  transfers between devices with their start and end apart: 7, of which 7 were waited for; matrix products, arithmetic and copies ran while one was open for 3% of the time, Pallas kernels for 13%

profile of v5, /device:TPU:0, one launch (start us, length us, event | category | flops | bytes accessed | tf_op | source)
XLA Modules:
  0.0 28.9 jit_solution(3140568430068974648)
XLA Ops:
  0.6 1.1 %fetch.1 = (bf16[32,16,128]{2,1,0:T(8,128)(2,1)S(1)}, bf16[32,16,128]{2,1,0:T(8,128)(2,1)S(1)}, bf16[32,16,128]{2,1,0:T(8,128)(2,1)S(1)}, bf16[27,16,32]{2,1,0:T(8,128)(2,1)S(1)}, bf16[16,27]{1,0:T(8,128)(2,1)S(1)}) custom-call(s32[1]{0:T(128)} %bitcast.2.at_x, bf16[32,8,16,128]{3,2,1,0:T(8,128)(2,1)} %coarse.1, bf16[27,16,32]{2,1,0:T(8,128)(2,1)} %refs_0_.1, ...), custom_call_target="tpu_custom_call" | custom-call | tf_op jit(solution)/shard_map/fetch/pallas_call | solution.py:515
  1.8 0.1 copy_bitcast_fusion
  2.0 1.3 %collective-permute-start = (bf16[2,32,128]{2,1,0:T(8,128)(2,1)S(1)}, bf16[2,32,128]{2,1,0:T(8,128)(2,1)S(1)}, u32[]{:S(2)}, u32[]{:S(2)}) collective-permute-start(bf16[2,32,128]{2,1,0:T(8,128)(2,1)S(1)} %pad_maximum_fusion.1), channel_id=1, source_target_pairs={{5,0},{6,1},{7,2},{1,4},{2,5},{3,6},{13,8},{14,9},{15,10},{9,12},{... | collective-permute-start | bytes 49160 | tf_op jit(solution)/shard_map/ppermute | solution.py:530
  3.3 3.8 %interior.1 = (f32[4,56,512]{2,1,0:T(8,128)S(1)}, f32[192,256]{1,0:T(8,128)S(1)}, f32[720,128]{1,0:T(8,128)S(1)}, bf16[192,256]{1,0:T(8,128)(2,1)S(1)}, bf16[128...) custom-call(s32[1]{0:T(128)} %bitcast.refs_0_, ...), custom_call_target="tpu_custom_call" | custom-call | flops 2000000000 | bytes 4000000 | tf_op jit(solution)/shard_map/interior/pallas_call | solution.py:567
  7.0 0.6 %collective-permute-done.rim = bf16[2,32,128]{2,1,0:T(8,128)(2,1)S(1)} collective-permute-done((bf16[2,32,128]{2,1,0:T(8,128)(2,1)S(1)}, bf16[2,32,128]{2,1,0:T(8,128)(2,1)S(1)}, u32[]{:S(2)}, u32[]{:S(2)}) %collective-permute-start) | collective-permute-done | bytes 16416 | tf_op jit(solution)/shard_map/ppermute | solution.py:530
  7.7 1.5 %rim.1 = (f32[4,8,512]{2,1,0:T(8,128)S(1)}, f32[56,128]{1,0:T(8,128)S(1)}, f32[56,128]{1,0:T(8,128)S(1)}) custom-call(s32[1]{0:T(128)} %bitcast.7.part, s32[1]{0:T(128)} %bitcast.1.refs_1_.inside, bf16[2,32,128]{2,1,0:T(8,128)(2,1)S(1)} %collective-permute-done.rim, f32[192,256]{1,0:T(8,128)S(1)} %get-tuple-element.29.sum_three_in, ...), custom_call_target="tpu_custom_call" | custom-call | flops 400000000 | bytes 2000000 | tf_op jit(solution)/shard_map/rim/pallas_call | solution.py:597
  9.1 0.7 %collective-permute-start.1 = (f32[56,128]{1,0:T(8,128)S(1)}, f32[56,128]{1,0:T(8,128)S(1)}, u32[]{:S(2)}, u32[]{:S(2)}) collective-permute-start(f32[56,128]{1,0:T(8,128)S(1)} %get-tuple-element.40), channel_id=1, source_target_pairs={{0,4},{1,5},{2,6},{3,7},{4,0},{5,1},{6,2},{7,3},{8,12},{9,13},{10,... | collective-permute-start | bytes 86024 | tf_op jit(solution)/shard_map/ppermute | solution.py:454
  9.8 0.9 %collective-permute-done.1 = f32[56,128]{1,0:T(8,128)S(1)} collective-permute-done((f32[56,128]{1,0:T(8,128)S(1)}, f32[56,128]{1,0:T(8,128)S(1)}, u32[]{:S(2)}, u32[]{:S(2)}) %collective-permute-start.1) | collective-permute-done | bytes 28704 | tf_op jit(solution)/shard_map/ppermute | solution.py:454
  10.7 1.9 %collective-permute-start.2 = (f32[56,128]{1,0:T(8,128)S(1)}, f32[56,128]{1,0:T(8,128)S(1)}, u32[]{:S(2)}, u32[]{:S(2)}) collective-permute-start(f32[56,128]{1,0:T(8,128)S(1)} %add.24), channel_id=1, source_target_pairs={{0,12},{1,13},{2,14},{3,15},{4,8},{5,9},{6,10},{7,11},{8,4},{9,5},... | collective-permute-start | bytes 86024 | tf_op jit(solution)/shard_map/ppermute | solution.py:454
  12.6 1.6 %collective-permute-done.2 = f32[56,128]{1,0:T(8,128)S(1)} collective-permute-done((f32[56,128]{1,0:T(8,128)S(1)}, f32[56,128]{1,0:T(8,128)S(1)}, u32[]{:S(2)}, u32[]{:S(2)}) %collective-permute-start.2) | collective-permute-done | bytes 28704 | tf_op jit(solution)/shard_map/ppermute | solution.py:454
  14.2 2.8 %collective-permute-start.3 = (f32[56,128]{1,0:T(8,128)S(1)}, f32[56,128]{1,0:T(8,128)S(1)}, u32[]{:S(2)}, u32[]{:S(2)}) collective-permute-start(f32[56,128]{1,0:T(8,128)S(1)} %add.25), channel_id=1, source_target_pairs={{0,20},{1,21},{2,22},{3,23},{4,16},{5,17},{6,18},{7,19},{8,28},{9,... | collective-permute-start | bytes 86024 | tf_op jit(solution)/shard_map/ppermute | solution.py:454
  17.0 1.6 %collective-permute-done.3 = f32[56,128]{1,0:T(8,128)S(1)} collective-permute-done((f32[56,128]{1,0:T(8,128)S(1)}, f32[56,128]{1,0:T(8,128)S(1)}, u32[]{:S(2)}, u32[]{:S(2)}) %collective-permute-start.3) | collective-permute-done | bytes 28704 | tf_op jit(solution)/shard_map/ppermute | solution.py:454
  18.5 2.5 %collective-permute-start.4 = (f32[56,128]{1,0:T(8,128)S(1)}, f32[56,128]{1,0:T(8,128)S(1)}, u32[]{:S(2)}, u32[]{:S(2)}) collective-permute-start(f32[56,128]{1,0:T(8,128)S(1)} %add.26), channel_id=1, source_target_pairs={{0,5},{1,4},{2,7},{3,6},{4,1},{5,0},{6,3},{7,2},{8,13},{9,12},{10,... | collective-permute-start | bytes 86024 | tf_op jit(solution)/shard_map/ppermute | solution.py:454
  21.0 1.6 %collective-permute-done.4 = f32[56,128]{1,0:T(8,128)S(1)} collective-permute-done((f32[56,128]{1,0:T(8,128)S(1)}, f32[56,128]{1,0:T(8,128)S(1)}, u32[]{:S(2)}, u32[]{:S(2)}) %collective-permute-start.4) | collective-permute-done | bytes 28704 | tf_op jit(solution)/shard_map/ppermute | solution.py:454
  22.6 2.8 %collective-permute-start.5 = (f32[56,128]{1,0:T(8,128)S(1)}, f32[56,128]{1,0:T(8,128)S(1)}, u32[]{:S(2)}, u32[]{:S(2)}) collective-permute-start(f32[56,128]{1,0:T(8,128)S(1)} %add.27), channel_id=1, source_target_pairs={{0,6},{1,7},{2,4},{3,5},{4,2},{5,3},{6,0},{7,1},{8,14},{9,15},{10,... | collective-permute-start | bytes 86024 | tf_op jit(solution)/shard_map/ppermute | solution.py:454
  25.3 1.6 %collective-permute-done.5 = f32[56,128]{1,0:T(8,128)S(1)} collective-permute-done((f32[56,128]{1,0:T(8,128)S(1)}, f32[56,128]{1,0:T(8,128)S(1)}, u32[]{:S(2)}, u32[]{:S(2)}) %collective-permute-start.5) | collective-permute-done | bytes 28704 | tf_op jit(solution)/shard_map/ppermute | solution.py:454
  26.9 0.2 collective-permute-start.6
  27.0 0.8 %pad_maximum_fusion = f32[4,64,512]{2,1,0:T(8,128)} fusion(f32[4,8,512]{2,1,0:T(8,128)S(1)} %get-tuple-element.38, f32[4,56,512]{2,1,0:T(8,128)S(1)} %get-tuple-element.28), kind=kLoop, calls=%fused_computation | loop fusion | flops 131072 | bytes 1048576 | tf_op jit(solution)/shard_map/concatenate | solution.py:615
  27.9 0.2 collective-permute-done.6.other
  28.1 0.8 %unpack.1 = (f32[27,16,32]{2,1,0:T(8,128)}, f32[16,27]{1,0:T(8,128)}) custom-call(s32[1]{0:T(128)} %bitcast.7.part, f32[56,128]{1,0:T(8,128)S(1)} %add.28.mine, f32[56,128]{1,0:T(8,128)S(1)} %collective-permute-done.6.other), custom_call_target="tpu_custom_call" | custom-call | tf_op jit(solution)/shard_map/unpack/pallas_call | solution.py:479
  (8 shorter events, 0.1 us)
Async XLA Ops:
  2.0 5.7 %collective-permute-start = (bf16[2,32,128]{2,1,0:T(8,128)(2,1)S(1)}, bf16[2,32,128]{2,1,0:T(8,128)(2,1)S(1)}, u32[]{:S(2)}, u32[]{:S(2)}) collective-permute-start(bf16[2,32,128]{2,1,0:T(8,128)(2,1)S(1)} %pad_maximum_fusion.1), channel_id=1, source_target_pairs={{5,0},{6,1},{7,2},{1,4},{2,5},{3,6},{13,8},{14,9},{15,10},{9,12},{... | collective-permute-start | bytes 49160 | tf_op jit(solution)/shard_map/ppermute | solution.py:530
  9.1 1.6 %collective-permute-start.1 = (f32[56,128]{1,0:T(8,128)S(1)}, f32[56,128]{1,0:T(8,128)S(1)}, u32[]{:S(2)}, u32[]{:S(2)}) collective-permute-start(f32[56,128]{1,0:T(8,128)S(1)} %get-tuple-element.40), channel_id=1, source_target_pairs={{0,4},{1,5},{2,6},{3,7},{4,0},{5,1},{6,2},{7,3},{8,12},{9,13},{10,... | collective-permute-start | bytes 86024 | tf_op jit(solution)/shard_map/ppermute | solution.py:454
  10.7 3.5 %collective-permute-start.2 = (f32[56,128]{1,0:T(8,128)S(1)}, f32[56,128]{1,0:T(8,128)S(1)}, u32[]{:S(2)}, u32[]{:S(2)}) collective-permute-start(f32[56,128]{1,0:T(8,128)S(1)} %add.24), channel_id=1, source_target_pairs={{0,12},{1,13},{2,14},{3,15},{4,8},{5,9},{6,10},{7,11},{8,4},{9,5},... | collective-permute-start | bytes 86024 | tf_op jit(solution)/shard_map/ppermute | solution.py:454
  14.2 4.3 %collective-permute-start.3 = (f32[56,128]{1,0:T(8,128)S(1)}, f32[56,128]{1,0:T(8,128)S(1)}, u32[]{:S(2)}, u32[]{:S(2)}) collective-permute-start(f32[56,128]{1,0:T(8,128)S(1)} %add.25), channel_id=1, source_target_pairs={{0,20},{1,21},{2,22},{3,23},{4,16},{5,17},{6,18},{7,19},{8,28},{9,... | collective-permute-start | bytes 86024 | tf_op jit(solution)/shard_map/ppermute | solution.py:454
  18.5 4.0 %collective-permute-start.4 = (f32[56,128]{1,0:T(8,128)S(1)}, f32[56,128]{1,0:T(8,128)S(1)}, u32[]{:S(2)}, u32[]{:S(2)}) collective-permute-start(f32[56,128]{1,0:T(8,128)S(1)} %add.26), channel_id=1, source_target_pairs={{0,5},{1,4},{2,7},{3,6},{4,1},{5,0},{6,3},{7,2},{8,13},{9,12},{10,... | collective-permute-start | bytes 86024 | tf_op jit(solution)/shard_map/ppermute | solution.py:454
  22.6 4.3 %collective-permute-start.5 = (f32[56,128]{1,0:T(8,128)S(1)}, f32[56,128]{1,0:T(8,128)S(1)}, u32[]{:S(2)}, u32[]{:S(2)}) collective-permute-start(f32[56,128]{1,0:T(8,128)S(1)} %add.27), channel_id=1, source_target_pairs={{0,6},{1,7},{2,4},{3,5},{4,2},{5,3},{6,0},{7,1},{8,14},{9,15},{10,... | collective-permute-start | bytes 86024 | tf_op jit(solution)/shard_map/ppermute | solution.py:454
  26.9 1.2 %collective-permute-start.6 = (f32[56,128]{1,0:T(8,128)S(1)}, f32[56,128]{1,0:T(8,128)S(1)}, u32[]{:S(2)}, u32[]{:S(2)}) collective-permute-start(f32[56,128]{1,0:T(8,128)S(1)} %add.28.mine), channel_id=1, source_target_pairs={{0,4},{1,5},{2,6},{3,7},{4,0},{5,1},{6,2},{7,3},{8,12},{9,13},{10,... | collective-permute-start | bytes 86024 | tf_op jit(solution)/shard_map/ppermute | solution.py:454

commit v6 on v5

--- a/solution.py
+++ b/solution.py
@@ -11,8 +11,8 @@
 BLOCKS = 3 * PAIR_ROWS * 3
 WINDOW = BLOCKS * 16
 LANES = 128
-FRONT_APART = 5
-BACK_APART = 5
+FRONT_APART = 7
+BACK_APART = 3
 MIB = 1024 * 1024
 
 

time: 29.1 us -> 28.8 us (0.990)
  starting transfers between devices: 12.1 us -> 11.8 us
  transfers between devices with their start and end apart: 7 -> 7, of which waited for: 7 -> 7; matrix products, arithmetic and copies ran while one was open for 3% -> 3% of each run, Pallas kernels for 13% -> 12%
where the time goes in v6:
time: 28.8 us; the launch traced here: 28.6 us
  starting transfers between devices  11.8 us (41%)
  waiting for transfers between devices  8.19 us (28%)
  Pallas kernels  6.9 us (24%)
  other arithmetic  0.88 us (3%)
  between operations  0.74 us (3%)
    ppermute x6, starting transfers between devices, exchanged(): return lax.ppermute(value, ('gx', 'gy'), pairs)  10.5 us
    ppermute x6, waiting for transfers between devices, exchanged(): return lax.ppermute(value, ('gx', 'gy'), pairs)  7.3 us
    pallas_call x1, Pallas kernels, shards(): pl.pallas_call(lambda *refs: interior_kernel(scale, *refs), out_shape=han...  3.5 us
    pallas_call x1, Pallas kernels, shards(): pl.pallas_call(rim_kernel, out_shape=(shape((fine_x, 8, fine_z), jnp.floa...  1.46 us
    ppermute x1, starting transfers between devices, shards(): lax.ppermute(first_rows, ('gx', 'gy'), [((i ^ 1) * groups_y + j + 1, i *...  1.29 us
    pallas_call x1, Pallas kernels, shards(): pl.pallas_call(fetch_kernel, out_shape=(shape((chan_in, held, depth), coa...  1.15 us
    ppermute x1, waiting for transfers between devices, shards(): lax.ppermute(first_rows, ('gx', 'gy'), [((i ^ 1) * groups_y + j + 1, i *...  0.89 us
    concatenate x1, other arithmetic, shards(): density = jnp.concatenate([most, last_dense], 1)  0.84 us
  transfers between devices with their start and end apart: 7, of which 7 were waited for; matrix products, arithmetic and copies ran while one was open for 3% of the time, Pallas kernels for 12%

profile of v6, /device:TPU:0, one launch (start us, length us, event | category | flops | bytes accessed | tf_op | source)
XLA Modules:
  0.0 28.6 jit_solution(15948292181772191638)
XLA Ops:
  0.6 1.1 %fetch.1 = (bf16[32,16,128]{2,1,0:T(8,128)(2,1)S(1)}, bf16[32,16,128]{2,1,0:T(8,128)(2,1)S(1)}, bf16[32,16,128]{2,1,0:T(8,128)(2,1)S(1)}, bf16[27,16,32]{2,1,0:T(8,128)(2,1)S(1)}, bf16[16,27]{1,0:T(8,128)(2,1)S(1)}) custom-call(s32[1]{0:T(128)} %bitcast.2.at_x, bf16[32,8,16,128]{3,2,1,0:T(8,128)(2,1)} %coarse.1, bf16[27,16,32]{2,1,0:T(8,128)(2,1)} %refs_0_.1, ...), custom_call_target="tpu_custom_call" | custom-call | tf_op jit(solution)/shard_map/fetch/pallas_call | solution.py:515
  1.8 0.1 copy_bitcast_fusion
  2.0 1.3 %collective-permute-start = (bf16[2,32,128]{2,1,0:T(8,128)(2,1)S(1)}, bf16[2,32,128]{2,1,0:T(8,128)(2,1)S(1)}, u32[]{:S(2)}, u32[]{:S(2)}) collective-permute-start(bf16[2,32,128]{2,1,0:T(8,128)(2,1)S(1)} %pad_maximum_fusion.1), channel_id=1, source_target_pairs={{5,0},{6,1},{7,2},{1,4},{2,5},{3,6},{13,8},{14,9},{15,10},{9,12},{... | collective-permute-start | bytes 49160 | tf_op jit(solution)/shard_map/ppermute | solution.py:530
  3.3 3.5 %interior.1 = (f32[4,56,512]{2,1,0:T(8,128)S(1)}, f32[192,256]{1,0:T(8,128)S(1)}, f32[720,128]{1,0:T(8,128)S(1)}, bf16[192,256]{1,0:T(8,128)(2,1)S(1)}, bf16[128...) custom-call(s32[1]{0:T(128)} %bitcast.refs_0_, ...), custom_call_target="tpu_custom_call" | custom-call | flops 2000000000 | bytes 4000000 | tf_op jit(solution)/shard_map/interior/pallas_call | solution.py:567
  6.8 0.9 %collective-permute-done.rim = bf16[2,32,128]{2,1,0:T(8,128)(2,1)S(1)} collective-permute-done((bf16[2,32,128]{2,1,0:T(8,128)(2,1)S(1)}, bf16[2,32,128]{2,1,0:T(8,128)(2,1)S(1)}, u32[]{:S(2)}, u32[]{:S(2)}) %collective-permute-start) | collective-permute-done | bytes 16416 | tf_op jit(solution)/shard_map/ppermute | solution.py:530
  7.7 1.5 %rim.1 = (f32[4,8,512]{2,1,0:T(8,128)S(1)}, f32[56,128]{1,0:T(8,128)S(1)}, f32[56,128]{1,0:T(8,128)S(1)}) custom-call(s32[1]{0:T(128)} %bitcast.7.part, s32[1]{0:T(128)} %bitcast.1.refs_1_.inside, bf16[2,32,128]{2,1,0:T(8,128)(2,1)S(1)} %collective-permute-done.rim, f32[192,256]{1,0:T(8,128)S(1)} %get-tuple-element.29.sum_three_in, ...), custom_call_target="tpu_custom_call" | custom-call | flops 400000000 | bytes 2000000 | tf_op jit(solution)/shard_map/rim/pallas_call | solution.py:597
  9.1 0.7 %collective-permute-start.1 = (f32[56,128]{1,0:T(8,128)S(1)}, f32[56,128]{1,0:T(8,128)S(1)}, u32[]{:S(2)}, u32[]{:S(2)}) collective-permute-start(f32[56,128]{1,0:T(8,128)S(1)} %get-tuple-element.40), channel_id=1, source_target_pairs={{0,4},{1,5},{2,6},{3,7},{4,0},{5,1},{6,2},{7,3},{8,12},{9,13},{10,... | collective-permute-start | bytes 86024 | tf_op jit(solution)/shard_map/ppermute | solution.py:454
  9.8 0.9 %collective-permute-done.1 = f32[56,128]{1,0:T(8,128)S(1)} collective-permute-done((f32[56,128]{1,0:T(8,128)S(1)}, f32[56,128]{1,0:T(8,128)S(1)}, u32[]{:S(2)}, u32[]{:S(2)}) %collective-permute-start.1) | collective-permute-done | bytes 28704 | tf_op jit(solution)/shard_map/ppermute | solution.py:454
  10.7 1.9 %collective-permute-start.2 = (f32[56,128]{1,0:T(8,128)S(1)}, f32[56,128]{1,0:T(8,128)S(1)}, u32[]{:S(2)}, u32[]{:S(2)}) collective-permute-start(f32[56,128]{1,0:T(8,128)S(1)} %add.24), channel_id=1, source_target_pairs={{0,12},{1,13},{2,14},{3,15},{4,8},{5,9},{6,10},{7,11},{8,4},{9,5},... | collective-permute-start | bytes 86024 | tf_op jit(solution)/shard_map/ppermute | solution.py:454
  12.6 1.6 %collective-permute-done.2 = f32[56,128]{1,0:T(8,128)S(1)} collective-permute-done((f32[56,128]{1,0:T(8,128)S(1)}, f32[56,128]{1,0:T(8,128)S(1)}, u32[]{:S(2)}, u32[]{:S(2)}) %collective-permute-start.2) | collective-permute-done | bytes 28704 | tf_op jit(solution)/shard_map/ppermute | solution.py:454
  14.2 2.8 %collective-permute-start.3 = (f32[56,128]{1,0:T(8,128)S(1)}, f32[56,128]{1,0:T(8,128)S(1)}, u32[]{:S(2)}, u32[]{:S(2)}) collective-permute-start(f32[56,128]{1,0:T(8,128)S(1)} %add.25), channel_id=1, source_target_pairs={{0,20},{1,21},{2,22},{3,23},{4,16},{5,17},{6,18},{7,19},{8,28},{9,... | collective-permute-start | bytes 86024 | tf_op jit(solution)/shard_map/ppermute | solution.py:454
  17.0 1.6 %collective-permute-done.3 = f32[56,128]{1,0:T(8,128)S(1)} collective-permute-done((f32[56,128]{1,0:T(8,128)S(1)}, f32[56,128]{1,0:T(8,128)S(1)}, u32[]{:S(2)}, u32[]{:S(2)}) %collective-permute-start.3) | collective-permute-done | bytes 28704 | tf_op jit(solution)/shard_map/ppermute | solution.py:454
  18.5 2.5 %collective-permute-start.4 = (f32[56,128]{1,0:T(8,128)S(1)}, f32[56,128]{1,0:T(8,128)S(1)}, u32[]{:S(2)}, u32[]{:S(2)}) collective-permute-start(f32[56,128]{1,0:T(8,128)S(1)} %add.26), channel_id=1, source_target_pairs={{0,5},{1,4},{2,7},{3,6},{4,1},{5,0},{6,3},{7,2},{8,13},{9,12},{10,... | collective-permute-start | bytes 86024 | tf_op jit(solution)/shard_map/ppermute | solution.py:454
  21.0 1.6 %collective-permute-done.4 = f32[56,128]{1,0:T(8,128)S(1)} collective-permute-done((f32[56,128]{1,0:T(8,128)S(1)}, f32[56,128]{1,0:T(8,128)S(1)}, u32[]{:S(2)}, u32[]{:S(2)}) %collective-permute-start.4) | collective-permute-done | bytes 28704 | tf_op jit(solution)/shard_map/ppermute | solution.py:454
  22.6 2.5 %collective-permute-start.5 = (f32[56,128]{1,0:T(8,128)S(1)}, f32[56,128]{1,0:T(8,128)S(1)}, u32[]{:S(2)}, u32[]{:S(2)}) collective-permute-start(f32[56,128]{1,0:T(8,128)S(1)} %add.27), channel_id=1, source_target_pairs={{0,6},{1,7},{2,4},{3,5},{4,2},{5,3},{6,0},{7,1},{8,14},{9,15},{10,... | collective-permute-start | bytes 86024 | tf_op jit(solution)/shard_map/ppermute | solution.py:454
  25.1 1.6 %collective-permute-done.5 = f32[56,128]{1,0:T(8,128)S(1)} collective-permute-done((f32[56,128]{1,0:T(8,128)S(1)}, f32[56,128]{1,0:T(8,128)S(1)}, u32[]{:S(2)}, u32[]{:S(2)}) %collective-permute-start.5) | collective-permute-done | bytes 28704 | tf_op jit(solution)/shard_map/ppermute | solution.py:454
  26.6 0.2 collective-permute-start.6
  26.8 0.8 %pad_maximum_fusion = f32[4,64,512]{2,1,0:T(8,128)} fusion(f32[4,8,512]{2,1,0:T(8,128)S(1)} %get-tuple-element.38, f32[4,56,512]{2,1,0:T(8,128)S(1)} %get-tuple-element.28), kind=kLoop, calls=%fused_computation | loop fusion | flops 131072 | bytes 1048576 | tf_op jit(solution)/shard_map/concatenate | solution.py:615
  27.6 0.2 collective-permute-done.6.other
  27.8 0.8 %unpack.1 = (f32[27,16,32]{2,1,0:T(8,128)}, f32[16,27]{1,0:T(8,128)}) custom-call(s32[1]{0:T(128)} %bitcast.7.part, f32[56,128]{1,0:T(8,128)S(1)} %add.28.mine, f32[56,128]{1,0:T(8,128)S(1)} %collective-permute-done.6.other), custom_call_target="tpu_custom_call" | custom-call | tf_op jit(solution)/shard_map/unpack/pallas_call | solution.py:479
  (8 shorter events, 0.1 us)
Async XLA Ops:
  2.0 5.7 %collective-permute-start = (bf16[2,32,128]{2,1,0:T(8,128)(2,1)S(1)}, bf16[2,32,128]{2,1,0:T(8,128)(2,1)S(1)}, u32[]{:S(2)}, u32[]{:S(2)}) collective-permute-start(bf16[2,32,128]{2,1,0:T(8,128)(2,1)S(1)} %pad_maximum_fusion.1), channel_id=1, source_target_pairs={{5,0},{6,1},{7,2},{1,4},{2,5},{3,6},{13,8},{14,9},{15,10},{9,12},{... | collective-permute-start | bytes 49160 | tf_op jit(solution)/shard_map/ppermute | solution.py:530
  9.1 1.6 %collective-permute-start.1 = (f32[56,128]{1,0:T(8,128)S(1)}, f32[56,128]{1,0:T(8,128)S(1)}, u32[]{:S(2)}, u32[]{:S(2)}) collective-permute-start(f32[56,128]{1,0:T(8,128)S(1)} %get-tuple-element.40), channel_id=1, source_target_pairs={{0,4},{1,5},{2,6},{3,7},{4,0},{5,1},{6,2},{7,3},{8,12},{9,13},{10,... | collective-permute-start | bytes 86024 | tf_op jit(solution)/shard_map/ppermute | solution.py:454
  10.7 3.5 %collective-permute-start.2 = (f32[56,128]{1,0:T(8,128)S(1)}, f32[56,128]{1,0:T(8,128)S(1)}, u32[]{:S(2)}, u32[]{:S(2)}) collective-permute-start(f32[56,128]{1,0:T(8,128)S(1)} %add.24), channel_id=1, source_target_pairs={{0,12},{1,13},{2,14},{3,15},{4,8},{5,9},{6,10},{7,11},{8,4},{9,5},... | collective-permute-start | bytes 86024 | tf_op jit(solution)/shard_map/ppermute | solution.py:454
  14.2 4.3 %collective-permute-start.3 = (f32[56,128]{1,0:T(8,128)S(1)}, f32[56,128]{1,0:T(8,128)S(1)}, u32[]{:S(2)}, u32[]{:S(2)}) collective-permute-start(f32[56,128]{1,0:T(8,128)S(1)} %add.25), channel_id=1, source_target_pairs={{0,20},{1,21},{2,22},{3,23},{4,16},{5,17},{6,18},{7,19},{8,28},{9,... | collective-permute-start | bytes 86024 | tf_op jit(solution)/shard_map/ppermute | solution.py:454
  18.5 4.0 %collective-permute-start.4 = (f32[56,128]{1,0:T(8,128)S(1)}, f32[56,128]{1,0:T(8,128)S(1)}, u32[]{:S(2)}, u32[]{:S(2)}) collective-permute-start(f32[56,128]{1,0:T(8,128)S(1)} %add.26), channel_id=1, source_target_pairs={{0,5},{1,4},{2,7},{3,6},{4,1},{5,0},{6,3},{7,2},{8,13},{9,12},{10,... | collective-permute-start | bytes 86024 | tf_op jit(solution)/shard_map/ppermute | solution.py:454
  22.6 4.1 %collective-permute-start.5 = (f32[56,128]{1,0:T(8,128)S(1)}, f32[56,128]{1,0:T(8,128)S(1)}, u32[]{:S(2)}, u32[]{:S(2)}) collective-permute-start(f32[56,128]{1,0:T(8,128)S(1)} %add.27), channel_id=1, source_target_pairs={{0,6},{1,7},{2,4},{3,5},{4,2},{5,3},{6,0},{7,1},{8,14},{9,15},{10,... | collective-permute-start | bytes 86024 | tf_op jit(solution)/shard_map/ppermute | solution.py:454
  26.6 1.2 %collective-permute-start.6 = (f32[56,128]{1,0:T(8,128)S(1)}, f32[56,128]{1,0:T(8,128)S(1)}, u32[]{:S(2)}, u32[]{:S(2)}) collective-permute-start(f32[56,128]{1,0:T(8,128)S(1)} %add.28.mine), channel_id=1, source_target_pairs={{0,4},{1,5},{2,6},{3,7},{4,0},{5,1},{6,2},{7,3},{8,12},{9,13},{10,... | collective-permute-start | bytes 86024 | tf_op jit(solution)/shard_map/ppermute | solution.py:454

commit v7 on v6

--- a/solution.py
+++ b/solution.py
@@ -234,10 +234,12 @@
                     both * self.slope[at : at + 32, lanes]
                 ).astype(jnp.bfloat16)
             yield
-            sums_to[1][span, :] = sums_from[1][span, :] + matmul_nt(self.windows[span, :], g_out)
+            part = matmul_nt(self.windows[span, :], g_out)
+            sums_to[1][span, :] = part if sums_from is None else sums_from[1][span, :] + part
             yield
         wide = jnp.concatenate([self.window(b) for b in range(2 * self.pairs + 1)], 1)
-        sums_to[0][...] = sums_from[0][...] + matmul_nt(self.g_pre[...], wide)
+        part = matmul_nt(self.g_pre[...], wide)
+        sums_to[0][...] = part if sums_from is None else sums_from[0][...] + part
         yield
 
 
@@ -334,12 +336,6 @@
                     last_cells[plane, b - held + 2] = tile
             yield
 
-    def zero_sums():
-        sum_three[...] = jnp.zeros_like(sum_three)
-        yield
-        sum_four[...] = jnp.zeros_like(sum_four)
-        yield
-
     matrices = (m_three, m_four, m_back)
     sums = (sum_three, sum_four)
     parts = []
@@ -355,7 +351,7 @@
         yield from parts[q].middle(
             field_terms_at(16 * q, 8 * parts[q].pairs), dense.at[:, rows_of(q), :]
         )
-        yield from parts[q].backward(sums, sums)
+        yield from parts[q].backward(sums if q > 0 else None, sums)
 
     def rows_of(q):
         return slice(16 * q, 16 * q + 8 * parts[q].pairs)
@@ -370,7 +366,7 @@
                 last_loss[res_x, :, lanes] = loss
             yield
 
-    run((fill_onehot(onehot), 1), (load_cells(), 2), (zero_sums(), 1))
+    run((fill_onehot(onehot), 1), (load_cells(), 2))
     fill_four(w_four, onehot, m_four, m_back)
     fill_three(w_three, m_three, build)
     staggered([front(q) for q in range(groups)], [], FRONT_APART)
@@ -466,13 +462,13 @@
     assert size_x & (size_x - 1) == 0 and size_y & (size_y - 1) == 0
     assert 2 <= size_x <= 256 and size_y <= 256
     mine = mine + exchanged(other, 1, 0)
+    bit = 1
+    while bit < size_y:
+        mine = mine + exchanged(mine, 1, bit)
+        bit = bit * 2
     bit = 2
     while bit < size_x:
         mine = mine + exchanged(mine, bit + 1, 0)
-        bit = bit * 2
-    bit = 1
-    while bit < size_y:
-        mine = mine + exchanged(mine, 1, bit)
         bit = bit * 2
     other = exchanged(mine, 1, 0)
     spec = pl.BlockSpec(memory_space=pltpu.VMEM)

time: 28.8 us -> 28.8 us (level)
  waiting for transfers between devices: 8.19 us -> 8.85 us
  starting transfers between devices: 11.8 us -> 11.2 us
    ppermute x6, waiting for transfers between devices: 7.3 us -> 7.97 us  [exchanged(): return lax.ppermute(value, ('gx', 'gy'), pairs)]
    ppermute x6, starting transfers between devices: 10.5 us -> 9.86 us  [exchanged(): return lax.ppermute(value, ('gx', 'gy'), pairs)]
where the time goes in v7:
time: 28.8 us; the launch traced here: 28.6 us
  starting transfers between devices  11.2 us (39%)
  waiting for transfers between devices  8.85 us (31%)
  Pallas kernels  6.92 us (24%)
  other arithmetic  0.88 us (3%)
  between operations  0.74 us (3%)
    ppermute x6, starting transfers between devices, exchanged(): return lax.ppermute(value, ('gx', 'gy'), pairs)  9.86 us
    ppermute x6, waiting for transfers between devices, exchanged(): return lax.ppermute(value, ('gx', 'gy'), pairs)  7.97 us
    pallas_call x1, Pallas kernels, shards(): pl.pallas_call(lambda *refs: interior_kernel(scale, *refs), out_shape=han...  3.52 us
    pallas_call x1, Pallas kernels, shards(): pl.pallas_call(rim_kernel, out_shape=(shape((fine_x, 8, fine_z), jnp.floa...  1.46 us
    ppermute x1, starting transfers between devices, shards(): lax.ppermute(first_rows, ('gx', 'gy'), [((i ^ 1) * groups_y + j + 1, i *...  1.29 us
    pallas_call x1, Pallas kernels, shards(): pl.pallas_call(fetch_kernel, out_shape=(shape((chan_in, held, depth), coa...  1.15 us
    ppermute x1, waiting for transfers between devices, shards(): lax.ppermute(first_rows, ('gx', 'gy'), [((i ^ 1) * groups_y + j + 1, i *...  0.88 us
    concatenate x1, other arithmetic, shards(): density = jnp.concatenate([most, last_dense], 1)  0.84 us
  transfers between devices with their start and end apart: 7, of which 7 were waited for; matrix products, arithmetic and copies ran while one was open for 3% of the time, Pallas kernels for 12%

profile of v7, /device:TPU:0, one launch (start us, length us, event | category | flops | bytes accessed | tf_op | source)
XLA Modules:
  0.0 28.6 jit_solution(711532230682544280)
XLA Ops:
  0.6 1.1 %fetch.1 = (bf16[32,16,128]{2,1,0:T(8,128)(2,1)S(1)}, bf16[32,16,128]{2,1,0:T(8,128)(2,1)S(1)}, bf16[32,16,128]{2,1,0:T(8,128)(2,1)S(1)}, bf16[27,16,32]{2,1,0:T(8,128)(2,1)S(1)}, bf16[16,27]{1,0:T(8,128)(2,1)S(1)}) custom-call(s32[1]{0:T(128)} %bitcast.2.at_x, bf16[32,8,16,128]{3,2,1,0:T(8,128)(2,1)} %coarse.1, bf16[27,16,32]{2,1,0:T(8,128)(2,1)} %refs_0_.1, ...), custom_call_target="tpu_custom_call" | custom-call | tf_op jit(solution)/shard_map/fetch/pallas_call | solution.py:511
  1.8 0.1 copy_bitcast_fusion
  2.0 1.3 %collective-permute-start = (bf16[2,32,128]{2,1,0:T(8,128)(2,1)S(1)}, bf16[2,32,128]{2,1,0:T(8,128)(2,1)S(1)}, u32[]{:S(2)}, u32[]{:S(2)}) collective-permute-start(bf16[2,32,128]{2,1,0:T(8,128)(2,1)S(1)} %pad_maximum_fusion.1), channel_id=1, source_target_pairs={{5,0},{6,1},{7,2},{1,4},{2,5},{3,6},{13,8},{14,9},{15,10},{9,12},{... | collective-permute-start | bytes 49160 | tf_op jit(solution)/shard_map/ppermute | solution.py:526
  3.3 3.5 %interior.1 = (f32[4,56,512]{2,1,0:T(8,128)S(1)}, f32[192,256]{1,0:T(8,128)S(1)}, f32[720,128]{1,0:T(8,128)S(1)}, bf16[192,256]{1,0:T(8,128)(2,1)S(1)}, bf16[128...) custom-call(s32[1]{0:T(128)} %bitcast.refs_0_, ...), custom_call_target="tpu_custom_call" | custom-call | flops 2000000000 | bytes 4000000 | tf_op jit(solution)/shard_map/interior/pallas_call | solution.py:563
  6.8 0.9 %collective-permute-done.rim = bf16[2,32,128]{2,1,0:T(8,128)(2,1)S(1)} collective-permute-done((bf16[2,32,128]{2,1,0:T(8,128)(2,1)S(1)}, bf16[2,32,128]{2,1,0:T(8,128)(2,1)S(1)}, u32[]{:S(2)}, u32[]{:S(2)}) %collective-permute-start) | collective-permute-done | bytes 16416 | tf_op jit(solution)/shard_map/ppermute | solution.py:526
  7.7 1.5 %rim.1 = (f32[4,8,512]{2,1,0:T(8,128)S(1)}, f32[56,128]{1,0:T(8,128)S(1)}, f32[56,128]{1,0:T(8,128)S(1)}) custom-call(s32[1]{0:T(128)} %bitcast.7.part, s32[1]{0:T(128)} %bitcast.1.refs_1_.inside, bf16[2,32,128]{2,1,0:T(8,128)(2,1)S(1)} %collective-permute-done.rim, f32[192,256]{1,0:T(8,128)S(1)} %get-tuple-element.29.sum_three_in, ...), custom_call_target="tpu_custom_call" | custom-call | flops 400000000 | bytes 2000000 | tf_op jit(solution)/shard_map/rim/pallas_call | solution.py:593
  9.1 0.7 %collective-permute-start.1 = (f32[56,128]{1,0:T(8,128)S(1)}, f32[56,128]{1,0:T(8,128)S(1)}, u32[]{:S(2)}, u32[]{:S(2)}) collective-permute-start(f32[56,128]{1,0:T(8,128)S(1)} %get-tuple-element.40), channel_id=1, source_target_pairs={{0,4},{1,5},{2,6},{3,7},{4,0},{5,1},{6,2},{7,3},{8,12},{9,13},{10,... | collective-permute-start | bytes 86024 | tf_op jit(solution)/shard_map/ppermute | solution.py:450
  9.8 0.9 %collective-permute-done.1 = f32[56,128]{1,0:T(8,128)S(1)} collective-permute-done((f32[56,128]{1,0:T(8,128)S(1)}, f32[56,128]{1,0:T(8,128)S(1)}, u32[]{:S(2)}, u32[]{:S(2)}) %collective-permute-start.1) | collective-permute-done | bytes 28704 | tf_op jit(solution)/shard_map/ppermute | solution.py:450
  10.7 2.8 %collective-permute-start.2 = (f32[56,128]{1,0:T(8,128)S(1)}, f32[56,128]{1,0:T(8,128)S(1)}, u32[]{:S(2)}, u32[]{:S(2)}) collective-permute-start(f32[56,128]{1,0:T(8,128)S(1)} %add.24), channel_id=1, source_target_pairs={{0,5},{1,4},{2,7},{3,6},{4,1},{5,0},{6,3},{7,2},{8,13},{9,12},{10,... | collective-permute-start | bytes 86024 | tf_op jit(solution)/shard_map/ppermute | solution.py:450
  13.5 1.6 %collective-permute-done.2 = f32[56,128]{1,0:T(8,128)S(1)} collective-permute-done((f32[56,128]{1,0:T(8,128)S(1)}, f32[56,128]{1,0:T(8,128)S(1)}, u32[]{:S(2)}, u32[]{:S(2)}) %collective-permute-start.2) | collective-permute-done | bytes 28704 | tf_op jit(solution)/shard_map/ppermute | solution.py:450
  15.1 2.5 %collective-permute-start.3 = (f32[56,128]{1,0:T(8,128)S(1)}, f32[56,128]{1,0:T(8,128)S(1)}, u32[]{:S(2)}, u32[]{:S(2)}) collective-permute-start(f32[56,128]{1,0:T(8,128)S(1)} %add.25), channel_id=1, source_target_pairs={{0,6},{1,7},{2,4},{3,5},{4,2},{5,3},{6,0},{7,1},{8,14},{9,15},{10,... | collective-permute-start | bytes 86024 | tf_op jit(solution)/shard_map/ppermute | solution.py:450
  17.6 1.6 %collective-permute-done.3 = f32[56,128]{1,0:T(8,128)S(1)} collective-permute-done((f32[56,128]{1,0:T(8,128)S(1)}, f32[56,128]{1,0:T(8,128)S(1)}, u32[]{:S(2)}, u32[]{:S(2)}) %collective-permute-start.3) | collective-permute-done | bytes 28704 | tf_op jit(solution)/shard_map/ppermute | solution.py:450
  19.1 1.3 %collective-permute-start.4 = (f32[56,128]{1,0:T(8,128)S(1)}, f32[56,128]{1,0:T(8,128)S(1)}, u32[]{:S(2)}, u32[]{:S(2)}) collective-permute-start(f32[56,128]{1,0:T(8,128)S(1)} %add.26), channel_id=1, source_target_pairs={{0,12},{1,13},{2,14},{3,15},{4,8},{5,9},{6,10},{7,11},{8,4},{9,5},... | collective-permute-start | bytes 86024 | tf_op jit(solution)/shard_map/ppermute | solution.py:450
  20.5 2.0 %collective-permute-done.4 = f32[56,128]{1,0:T(8,128)S(1)} collective-permute-done((f32[56,128]{1,0:T(8,128)S(1)}, f32[56,128]{1,0:T(8,128)S(1)}, u32[]{:S(2)}, u32[]{:S(2)}) %collective-permute-start.4) | collective-permute-done | bytes 28704 | tf_op jit(solution)/shard_map/ppermute | solution.py:450
  22.4 2.4 %collective-permute-start.5 = (f32[56,128]{1,0:T(8,128)S(1)}, f32[56,128]{1,0:T(8,128)S(1)}, u32[]{:S(2)}, u32[]{:S(2)}) collective-permute-start(f32[56,128]{1,0:T(8,128)S(1)} %add.27), channel_id=1, source_target_pairs={{0,20},{1,21},{2,22},{3,23},{4,16},{5,17},{6,18},{7,19},{8,28},{9,... | collective-permute-start | bytes 86024 | tf_op jit(solution)/shard_map/ppermute | solution.py:450
  24.8 1.8 %collective-permute-done.5 = f32[56,128]{1,0:T(8,128)S(1)} collective-permute-done((f32[56,128]{1,0:T(8,128)S(1)}, f32[56,128]{1,0:T(8,128)S(1)}, u32[]{:S(2)}, u32[]{:S(2)}) %collective-permute-start.5) | collective-permute-done | bytes 28704 | tf_op jit(solution)/shard_map/ppermute | solution.py:450
  26.6 0.2 collective-permute-start.6
  26.8 0.8 %pad_maximum_fusion = f32[4,64,512]{2,1,0:T(8,128)} fusion(f32[4,8,512]{2,1,0:T(8,128)S(1)} %get-tuple-element.38, f32[4,56,512]{2,1,0:T(8,128)S(1)} %get-tuple-element.28), kind=kLoop, calls=%fused_computation | loop fusion | flops 131072 | bytes 1048576 | tf_op jit(solution)/shard_map/concatenate | solution.py:611
  27.6 0.2 collective-permute-done.6.other
  27.8 0.8 %unpack.1 = (f32[27,16,32]{2,1,0:T(8,128)}, f32[16,27]{1,0:T(8,128)}) custom-call(s32[1]{0:T(128)} %bitcast.7.part, f32[56,128]{1,0:T(8,128)S(1)} %add.28.mine, f32[56,128]{1,0:T(8,128)S(1)} %collective-permute-done.6.other), custom_call_target="tpu_custom_call" | custom-call | tf_op jit(solution)/shard_map/unpack/pallas_call | solution.py:475
  (8 shorter events, 0.1 us)
Async XLA Ops:
  2.0 5.7 %collective-permute-start = (bf16[2,32,128]{2,1,0:T(8,128)(2,1)S(1)}, bf16[2,32,128]{2,1,0:T(8,128)(2,1)S(1)}, u32[]{:S(2)}, u32[]{:S(2)}) collective-permute-start(bf16[2,32,128]{2,1,0:T(8,128)(2,1)S(1)} %pad_maximum_fusion.1), channel_id=1, source_target_pairs={{5,0},{6,1},{7,2},{1,4},{2,5},{3,6},{13,8},{14,9},{15,10},{9,12},{... | collective-permute-start | bytes 49160 | tf_op jit(solution)/shard_map/ppermute | solution.py:526
  9.1 1.6 %collective-permute-start.1 = (f32[56,128]{1,0:T(8,128)S(1)}, f32[56,128]{1,0:T(8,128)S(1)}, u32[]{:S(2)}, u32[]{:S(2)}) collective-permute-start(f32[56,128]{1,0:T(8,128)S(1)} %get-tuple-element.40), channel_id=1, source_target_pairs={{0,4},{1,5},{2,6},{3,7},{4,0},{5,1},{6,2},{7,3},{8,12},{9,13},{10,... | collective-permute-start | bytes 86024 | tf_op jit(solution)/shard_map/ppermute | solution.py:450
  10.7 4.3 %collective-permute-start.2 = (f32[56,128]{1,0:T(8,128)S(1)}, f32[56,128]{1,0:T(8,128)S(1)}, u32[]{:S(2)}, u32[]{:S(2)}) collective-permute-start(f32[56,128]{1,0:T(8,128)S(1)} %add.24), channel_id=1, source_target_pairs={{0,5},{1,4},{2,7},{3,6},{4,1},{5,0},{6,3},{7,2},{8,13},{9,12},{10,... | collective-permute-start | bytes 86024 | tf_op jit(solution)/shard_map/ppermute | solution.py:450
  15.1 4.1 %collective-permute-start.3 = (f32[56,128]{1,0:T(8,128)S(1)}, f32[56,128]{1,0:T(8,128)S(1)}, u32[]{:S(2)}, u32[]{:S(2)}) collective-permute-start(f32[56,128]{1,0:T(8,128)S(1)} %add.25), channel_id=1, source_target_pairs={{0,6},{1,7},{2,4},{3,5},{4,2},{5,3},{6,0},{7,1},{8,14},{9,15},{10,... | collective-permute-start | bytes 86024 | tf_op jit(solution)/shard_map/ppermute | solution.py:450
  19.1 3.3 %collective-permute-start.4 = (f32[56,128]{1,0:T(8,128)S(1)}, f32[56,128]{1,0:T(8,128)S(1)}, u32[]{:S(2)}, u32[]{:S(2)}) collective-permute-start(f32[56,128]{1,0:T(8,128)S(1)} %add.26), channel_id=1, source_target_pairs={{0,12},{1,13},{2,14},{3,15},{4,8},{5,9},{6,10},{7,11},{8,4},{9,5},... | collective-permute-start | bytes 86024 | tf_op jit(solution)/shard_map/ppermute | solution.py:450
  22.4 4.2 %collective-permute-start.5 = (f32[56,128]{1,0:T(8,128)S(1)}, f32[56,128]{1,0:T(8,128)S(1)}, u32[]{:S(2)}, u32[]{:S(2)}) collective-permute-start(f32[56,128]{1,0:T(8,128)S(1)} %add.27), channel_id=1, source_target_pairs={{0,20},{1,21},{2,22},{3,23},{4,16},{5,17},{6,18},{7,19},{8,28},{9,... | collective-permute-start | bytes 86024 | tf_op jit(solution)/shard_map/ppermute | solution.py:450
  26.6 1.2 %collective-permute-start.6 = (f32[56,128]{1,0:T(8,128)S(1)}, f32[56,128]{1,0:T(8,128)S(1)}, u32[]{:S(2)}, u32[]{:S(2)}) collective-permute-start(f32[56,128]{1,0:T(8,128)S(1)} %add.28.mine), channel_id=1, source_target_pairs={{0,4},{1,5},{2,6},{3,7},{4,0},{5,1},{6,2},{7,3},{8,12},{9,13},{10,... | collective-permute-start | bytes 86024 | tf_op jit(solution)/shard_map/ppermute | solution.py:450
